TPU v7x, 32 devices: a whole 2x2x4 slice. The times are simulated.
32 devices in a mesh: seq: 4 (over y, x), fsdp: 8 (over z, core).
Axes of the slice: x: 2, y: 2, z: 4, core: 2. Of those that a mesh axis runs over, the one named last changes fastest.
Arguments:
- tokens: bfloat16 [8, 1024, 768], P('fsdp', 'seq'), may hold values from -6 to 6
- encoded: bfloat16 [8, 512, 768], P('fsdp', 'seq'), may hold values from -6 to 6
- lengths: int32 [8], P('fsdp'), may hold values from 512 to 1024, as said below
- cotangent: bfloat16 [8, 1024, 768], P('fsdp', 'seq'), may hold values from -6 to 6
- gain_self: bfloat16 [768], replicated, may hold values from 0.5 to 1.5
- gain_cross: bfloat16 [768], replicated, may hold values from 0.5 to 1.5
- gain_ff: bfloat16 [768], replicated, may hold values from 0.5 to 1.5
- bucket_table: bfloat16 [32, 12], replicated, may hold values from -4 to 4
- self_query: bfloat16 [768, 768], P('fsdp'), may hold values from -0.0390625 to 0.0390625
- self_key: bfloat16 [768, 768], P('fsdp'), may hold values from -0.21875 to 0.21875
- self_value: bfloat16 [768, 768], P('fsdp'), may hold values from -0.21875 to 0.21875
- self_out: bfloat16 [768, 768], P('fsdp'), may hold values from -3.5 to 3.5
- cross_query: bfloat16 [768, 768], P('fsdp'), may hold values from -0.0390625 to 0.0390625
- cross_key: bfloat16 [768, 768], P('fsdp'), may hold values from -0.21875 to 0.21875
- cross_value: bfloat16 [768, 768], P('fsdp'), may hold values from -0.21875 to 0.21875
- cross_out: bfloat16 [768, 768], P('fsdp'), may hold values from -1.5 to 1.5
- ff_gate: bfloat16 [768, 2048], P('fsdp'), may hold values from -0.21875 to 0.21875
- ff_up: bfloat16 [768, 2048], P('fsdp'), may hold values from -0.21875 to 0.21875
- ff_down: bfloat16 [2048, 768], P('fsdp'), may hold values from -0.125 to 0.125
Outputs:
- layer_out: bfloat16 [8, 1024, 768], P('fsdp', 'seq')
- grad_tokens: float32 [8, 1024, 768], P('fsdp', 'seq')
- grad_encoded: float32 [8, 512, 768], P('fsdp', 'seq')
- grad_gain_self: float32 [768], replicated
- grad_gain_cross: float32 [768], replicated
- grad_gain_ff: float32 [768], replicated
- grad_bucket_table: float32 [32, 12], replicated
- grad_self_query: float32 [768, 768], P('fsdp')
- grad_self_key: float32 [768, 768], P('fsdp')
- grad_self_value: float32 [768, 768], P('fsdp')
- grad_self_out: float32 [768, 768], P('fsdp')
- grad_cross_query: float32 [768, 768], P('fsdp')
- grad_cross_key: float32 [768, 768], P('fsdp')
- grad_cross_value: float32 [768, 768], P('fsdp')
- grad_cross_out: float32 [768, 768], P('fsdp')
- grad_ff_gate: float32 [768, 2048], P('fsdp')
- grad_ff_up: float32 [768, 2048], P('fsdp')
- grad_ff_down: float32 [2048, 768], P('fsdp')
Inputs may be any that keep to these rules, and one draw needn't show every extreme that they name: Slots from lengths[s] on are unused; some sequence uses all 1024 slots and some uses exactly half of them.
All inputs are finite; a program needn't handle non-finite values.
Results may differ from a plain program's by a relative error of at most 0.02.
The roundings to bfloat16 on the way count: a program that leaves them out, or rounds other values in their place, can miss the bound.
Values may be sent and summed in bfloat16 or wider, within the bound.
A program may use at most 192 MiB of HBM per device.

v0:
```python
import math

import jax
import jax.numpy as jnp
from jax import lax
from jax.sharding import PartitionSpec as P

HEADS = 12
BUCKETS = 32
MAX_DISTANCE = 128


EPSILON = 1e-06


def thresholds():
    exact_limit = BUCKETS // 2
    return [
        int(math.ceil(exact_limit * (MAX_DISTANCE / exact_limit) ** (number / exact_limit)))
        for number in range(1, exact_limit)
    ]


def bucket_ids(key_count):
    exact_limit = BUCKETS // 2
    offsets = jnp.arange(key_count, dtype=jnp.int32)
    passed = jnp.zeros((key_count,), jnp.int32)
    for border in thresholds():
        passed = passed + (offsets >= border).astype(jnp.int32)
    return jnp.where(offsets < exact_limit, offsets, exact_limit + passed)


def diagonal_fill(profile, first_row, block_rows):
    head_count, key_count = profile.shape
    flipped = profile[:, ::-1]
    padded = jnp.concatenate(
        [
            jnp.zeros((head_count, 1), profile.dtype),
            flipped,
            jnp.zeros((head_count, key_count + block_rows), profile.dtype),
        ],
        axis=1,
    )
    offset = key_count - block_rows - first_row
    span = key_count + block_rows + 1
    window = lax.dynamic_slice_in_dim(padded, offset, span, 1)
    repeated = jnp.broadcast_to(window[:, None, :], (head_count, block_rows, span))
    flattened = repeated.reshape(head_count, block_rows * span)[:, : block_rows * (span - 1)]
    return flattened.reshape(head_count, block_rows, span - 1)[
        :, :, block_rows : block_rows + key_count
    ]


def rms_scale(values, gain):
    return values * lax.rsqrt(jnp.mean(values * values, axis=-1, keepdims=True) + EPSILON) * gain


def matrix_product(left, right):
    return jnp.dot(left, right, preferred_element_type=jnp.float32)


def inner_rows(left, right):
    return lax.dot_general(
        left, right, (((0,), (0,)), ((), ())), preferred_element_type=jnp.float32
    )


def across_row_axis(left, right):
    return lax.dot_general(
        left, right, (((1,), (1,)), ((), ())), preferred_element_type=jnp.float32
    )


def norm_back(values, gain, grad_normed):
    _, pullback = jax.vjp(rms_scale, values, gain)
    return pullback(grad_normed)


def arrange_rows(matrix, owner_count, share_count):
    row_count, col_count = matrix.shape
    split = matrix.reshape(
        owner_count, share_count, row_count // (owner_count * share_count), col_count
    )
    return jnp.transpose(split, (1, 0, 2, 3)).reshape(row_count, col_count)


def block_scores(block_query, keys_three, first_row, setting):
    raw_scores = jnp.einsum(
        "qhd,khd->hqk", block_query, keys_three, preferred_element_type=jnp.float32
    )
    if setting is None:
        return raw_scores
    profile, length = setting
    block_rows = block_query.shape[0]
    key_count = keys_three.shape[0]
    row_ids = first_row + jnp.arange(block_rows, dtype=jnp.int32)
    col_ids = jnp.arange(key_count, dtype=jnp.int32)
    allowed = (col_ids[None, :] <= row_ids[:, None]) & (col_ids[None, :] < length)
    return jnp.where(
        allowed[None], raw_scores + diagonal_fill(profile, first_row, block_rows), -1e30
    )


def attend_forward(queries, keys_flat, values_flat, head_count, block_rows, setting):
    query_count, local_width = queries.shape
    head_size = local_width // head_count
    keys_three = keys_flat.reshape(keys_flat.shape[0], head_count, head_size)
    values_three = values_flat.reshape(values_flat.shape[0], head_count, head_size)

    def one_block(block_index):
        first_row = block_index * block_rows
        block_query = lax.dynamic_slice_in_dim(queries, first_row, block_rows, 0).reshape(
            block_rows, head_count, head_size
        )
        scores = block_scores(block_query, keys_three, first_row, setting)
        row_max = jnp.max(scores, axis=-1, keepdims=True)
        raised = jnp.exp(scores - row_max)
        row_total = jnp.sum(raised, axis=-1, keepdims=True)
        soft_low = (raised / row_total).astype(jnp.bfloat16)
        mixed_rows = jnp.einsum(
            "hqk,khd->qhd", soft_low, values_three, preferred_element_type=jnp.float32
        )
        return (
            mixed_rows.reshape(block_rows, local_width).astype(jnp.bfloat16),
            (row_max + jnp.log(row_total))[:, :, 0],
        )

    mixed_blocks, log_totals = lax.map(
        one_block, jnp.arange(query_count // block_rows, dtype=jnp.int32)
    )
    return (mixed_blocks.reshape(query_count, local_width), log_totals)


def attend_backward(
    queries, keys_flat, values_flat, grad_mixed, log_totals, head_count, block_rows, setting
):
    query_count, local_width = queries.shape
    head_size = local_width // head_count
    key_count = keys_flat.shape[0]
    keys_three = keys_flat.reshape(key_count, head_count, head_size)
    values_three = values_flat.reshape(key_count, head_count, head_size)

    def one_block(totals_carry, inputs):
        grad_keys, grad_values, grad_profile = totals_carry
        block_index, block_log = inputs
        first_row = block_index * block_rows
        block_query = lax.dynamic_slice_in_dim(queries, first_row, block_rows, 0).reshape(
            block_rows, head_count, head_size
        )
        block_grad = lax.dynamic_slice_in_dim(grad_mixed, first_row, block_rows, 0).reshape(
            block_rows, head_count, head_size
        )
        scores = block_scores(block_query, keys_three, first_row, setting)
        soft = jnp.exp(scores - block_log[:, :, None])
        soft_low = soft.astype(jnp.bfloat16)
        grad_values = grad_values + jnp.einsum(
            "hqk,qhd->khd", soft_low, block_grad, preferred_element_type=jnp.float32
        )
        grad_soft = jnp.einsum(
            "qhd,khd->hqk", block_grad, values_three, preferred_element_type=jnp.float32
        )
        delta_rows = jnp.sum(soft * grad_soft, axis=-1, keepdims=True)
        grad_scores = (soft * (grad_soft - delta_rows)).astype(jnp.bfloat16)
        grad_query = jnp.einsum(
            "hqk,khd->qhd", grad_scores, keys_three, preferred_element_type=jnp.float32
        )
        grad_keys = grad_keys + jnp.einsum(
            "hqk,qhd->khd", grad_scores, block_query, preferred_element_type=jnp.float32
        )
        if setting is not None:

            def fill_block(profile_rows):
                return diagonal_fill(profile_rows, first_row, block_rows)

            _, pull_fill = jax.vjp(fill_block, setting[0])
            grad_profile = grad_profile + pull_fill(grad_scores.astype(jnp.float32))[0]
        return (
            (grad_keys, grad_values, grad_profile),
            grad_query.reshape(block_rows, local_width).astype(jnp.bfloat16),
        )

    profile_shape = setting[0].shape if setting is not None else (1, 1)
    initial = (
        jnp.zeros((key_count, head_count, head_size), jnp.float32),
        jnp.zeros((key_count, head_count, head_size), jnp.float32),
        jnp.zeros(profile_shape, jnp.float32),
    )
    block_ids = jnp.arange(query_count // block_rows, dtype=jnp.int32)
    finished, grad_blocks = lax.scan(one_block, initial, (block_ids, log_totals))
    grad_queries = grad_blocks.reshape(query_count, local_width)
    grad_keys = finished[0].reshape(key_count, local_width).astype(jnp.bfloat16)
    grad_values = finished[1].reshape(key_count, local_width).astype(jnp.bfloat16)
    return (grad_queries, grad_keys, grad_values, finished[2])


def local(
    tokens,
    encoded,
    lengths,
    cotangent,
    gain_self,
    gain_cross,
    gain_ff,
    bucket_table,
    self_query,
    self_key,
    self_value,
    self_out,
    cross_query,
    cross_key,
    cross_value,
    cross_out,
    ff_gate,
    ff_up,
    ff_down,
):
    gathered = (
        lax.all_gather(self_query, "fsdp", axis=0, tiled=True),
        lax.all_gather(self_key, "fsdp", axis=0, tiled=True),
        lax.all_gather(self_value, "fsdp", axis=0, tiled=True),
        lax.all_gather(self_out, "fsdp", axis=0, tiled=True),
        lax.all_gather(cross_query, "fsdp", axis=0, tiled=True),
        lax.all_gather(cross_key, "fsdp", axis=0, tiled=True),
        lax.all_gather(cross_value, "fsdp", axis=0, tiled=True),
        lax.all_gather(cross_out, "fsdp", axis=0, tiled=True),
        lax.all_gather(ff_gate, "fsdp", axis=0, tiled=True),
        lax.all_gather(ff_up, "fsdp", axis=0, tiled=True),
        lax.all_gather(ff_down, "fsdp", axis=0, tiled=True),
    )
    (
        full_squery,
        gathered_self_key,
        full_svalue,
        full_sout,
        full_cquery,
        full_ckey,
        full_cvalue,
        full_cout,
        full_gate,
        full_up,
        full_down,
    ) = gathered
    rows_here = tokens.shape[1]
    seq_parts = lax.axis_size("seq")
    fsdp_parts = lax.axis_size("fsdp")
    slot_count = rows_here * seq_parts
    local_heads = HEADS // seq_parts
    block_rows = min(512, slot_count)
    length = lengths[0]
    seq_place = lax.axis_index("seq")
    gain_one = gain_self.astype(jnp.float32)
    gain_two = gain_cross.astype(jnp.float32)
    gain_three = gain_ff.astype(jnp.float32)
    table_cols = lax.dynamic_slice_in_dim(bucket_table, seq_place * local_heads, local_heads, 1)
    one_hot = (
        bucket_ids(slot_count)[:, None] == jnp.arange(BUCKETS, dtype=jnp.int32)[None, :]
    ).astype(jnp.bfloat16)
    profile = jnp.dot(one_hot, table_cols, preferred_element_type=jnp.float32).T
    source = tokens[0].astype(jnp.float32)
    enc_rows = encoded[0]
    first_normed_input = rms_scale(source, gain_one).astype(jnp.bfloat16)
    query_local = matrix_product(first_normed_input, full_squery).astype(jnp.bfloat16)
    local_key_rows = matrix_product(first_normed_input, gathered_self_key).astype(jnp.bfloat16)
    value_local = matrix_product(first_normed_input, full_svalue).astype(jnp.bfloat16)
    ckey_local = matrix_product(enc_rows, full_ckey).astype(jnp.bfloat16)
    cvalue_local = matrix_product(enc_rows, full_cvalue).astype(jnp.bfloat16)
    query_heads, key_heads, value_heads, ckey_heads, cvalue_heads = (
        lax.all_to_all(query_local, "seq", split_axis=1, concat_axis=0, tiled=True),
        lax.all_to_all(local_key_rows, "seq", split_axis=1, concat_axis=0, tiled=True),
        lax.all_to_all(value_local, "seq", split_axis=1, concat_axis=0, tiled=True),
        lax.all_to_all(ckey_local, "seq", split_axis=1, concat_axis=0, tiled=True),
        lax.all_to_all(cvalue_local, "seq", split_axis=1, concat_axis=0, tiled=True),
    )
    self_setting = (profile, length)
    mixed_self_heads, log_self = attend_forward(
        query_heads, key_heads, value_heads, local_heads, block_rows, self_setting
    )
    mixed_self = lax.all_to_all(mixed_self_heads, "seq", split_axis=0, concat_axis=1, tiled=True)
    hidden_one = source + matrix_product(mixed_self, full_sout)
    normed_two = rms_scale(hidden_one, gain_two).astype(jnp.bfloat16)
    cquery_local = matrix_product(normed_two, full_cquery).astype(jnp.bfloat16)
    cquery_heads = lax.all_to_all(cquery_local, "seq", split_axis=1, concat_axis=0, tiled=True)
    mixed_cross_heads, log_cross = attend_forward(
        cquery_heads, ckey_heads, cvalue_heads, local_heads, block_rows, None
    )
    mixed_cross = lax.all_to_all(mixed_cross_heads, "seq", split_axis=0, concat_axis=1, tiled=True)
    hidden_two = hidden_one + matrix_product(mixed_cross, full_cout)
    normed_three = rms_scale(hidden_two, gain_three).astype(jnp.bfloat16)
    gate_proj = matrix_product(normed_three, full_gate)
    up_part = matrix_product(normed_three, full_up)
    activated = (jax.nn.gelu(gate_proj, approximate=True) * up_part).astype(jnp.bfloat16)
    slot_ids = seq_place * rows_here + jnp.arange(rows_here, dtype=jnp.int32)
    valid = (slot_ids < length).astype(jnp.float32)[:, None]
    result = valid * (hidden_two + matrix_product(activated, full_down))
    backward_weights = (
        lax.all_gather(self_query, "fsdp", axis=0, tiled=True),
        lax.all_gather(self_key, "fsdp", axis=0, tiled=True),
        lax.all_gather(self_value, "fsdp", axis=0, tiled=True),
        lax.all_gather(self_out, "fsdp", axis=0, tiled=True),
        lax.all_gather(cross_query, "fsdp", axis=0, tiled=True),
        lax.all_gather(cross_key, "fsdp", axis=0, tiled=True),
        lax.all_gather(cross_value, "fsdp", axis=0, tiled=True),
        lax.all_gather(cross_out, "fsdp", axis=0, tiled=True),
        lax.all_gather(ff_gate, "fsdp", axis=0, tiled=True),
        lax.all_gather(ff_up, "fsdp", axis=0, tiled=True),
        lax.all_gather(ff_down, "fsdp", axis=0, tiled=True),
    )
    (
        back_squery,
        backward_self_key,
        back_svalue,
        back_sout,
        back_cquery,
        back_ckey,
        back_cvalue,
        back_cout,
        back_gate,
        back_up,
        back_down,
    ) = backward_weights
    grad_result = valid * cotangent[0].astype(jnp.float32)
    grad_branch_ff = grad_result.astype(jnp.bfloat16)
    grad_wdown = inner_rows(activated, grad_branch_ff)
    grad_activated = across_row_axis(grad_branch_ff, back_down)

    def gated(gate_rows, up_rows):
        return jax.nn.gelu(gate_rows, approximate=True) * up_rows

    _, pull_gate = jax.vjp(gated, gate_proj, up_part)
    grad_gate_f, grad_up_f = pull_gate(grad_activated)
    grad_gate = grad_gate_f.astype(jnp.bfloat16)
    grad_up = grad_up_f.astype(jnp.bfloat16)
    grad_wgate = inner_rows(normed_three, grad_gate)
    grad_wup = inner_rows(normed_three, grad_up)
    grad_normed_three = across_row_axis(grad_gate, back_gate) + across_row_axis(grad_up, back_up)
    grad_two_norm, grad_gain_three = norm_back(hidden_two, gain_three, grad_normed_three)
    grad_two = grad_result + grad_two_norm
    grad_branch_cross = grad_two.astype(jnp.bfloat16)
    grad_wcout = inner_rows(mixed_cross, grad_branch_cross)
    grad_mixed_cross = across_row_axis(grad_branch_cross, back_cout).astype(jnp.bfloat16)
    grad_mixed_cross_heads = lax.all_to_all(
        grad_mixed_cross, "seq", split_axis=1, concat_axis=0, tiled=True
    )
    grad_cq_heads, grad_ck_heads, grad_cv_heads, unused_profile = attend_backward(
        cquery_heads,
        ckey_heads,
        cvalue_heads,
        grad_mixed_cross_heads,
        log_cross,
        local_heads,
        block_rows,
        None,
    )
    grad_cq = lax.all_to_all(grad_cq_heads, "seq", split_axis=0, concat_axis=1, tiled=True)
    grad_wcquery = inner_rows(normed_two, grad_cq)
    grad_one_norm, grad_gain_two = norm_back(
        hidden_one, gain_two, across_row_axis(grad_cq, back_cquery)
    )
    grad_one = grad_two + grad_one_norm
    grad_branch_self = grad_one.astype(jnp.bfloat16)
    grad_wsout = inner_rows(mixed_self, grad_branch_self)
    grad_mixed_self = across_row_axis(grad_branch_self, back_sout).astype(jnp.bfloat16)
    grad_mixed_self_heads = lax.all_to_all(
        grad_mixed_self, "seq", split_axis=1, concat_axis=0, tiled=True
    )
    grad_q_heads, grad_k_heads, grad_v_heads, grad_profile = attend_backward(
        query_heads,
        key_heads,
        value_heads,
        grad_mixed_self_heads,
        log_self,
        local_heads,
        block_rows,
        self_setting,
    )
    grad_q, key_gradient, grad_v, grad_ck, grad_cv = (
        lax.all_to_all(grad_q_heads, "seq", split_axis=0, concat_axis=1, tiled=True),
        lax.all_to_all(grad_k_heads, "seq", split_axis=0, concat_axis=1, tiled=True),
        lax.all_to_all(grad_v_heads, "seq", split_axis=0, concat_axis=1, tiled=True),
        lax.all_to_all(grad_ck_heads, "seq", split_axis=0, concat_axis=1, tiled=True),
        lax.all_to_all(grad_cv_heads, "seq", split_axis=0, concat_axis=1, tiled=True),
    )
    grad_wsquery = inner_rows(first_normed_input, grad_q)
    grad_wskey = inner_rows(first_normed_input, key_gradient)
    grad_wsvalue = inner_rows(first_normed_input, grad_v)
    grad_normed_one = (
        across_row_axis(grad_q, back_squery)
        + across_row_axis(key_gradient, backward_self_key)
        + across_row_axis(grad_v, back_svalue)
    )
    grad_zero_norm, grad_gain_one = norm_back(source, gain_one, grad_normed_one)
    grad_source = grad_one + grad_zero_norm
    grad_enc_rows = across_row_axis(grad_ck, back_ckey) + across_row_axis(grad_cv, back_cvalue)
    grad_wckey = inner_rows(enc_rows, grad_ck)
    grad_wcvalue = inner_rows(enc_rows, grad_cv)
    table_part = lax.dot_general(
        one_hot.astype(jnp.float32),
        grad_profile,
        (((0,), (1,)), ((), ())),
        precision=lax.Precision.HIGHEST,
        preferred_element_type=jnp.float32,
    )
    table_full = lax.dynamic_update_slice(
        jnp.zeros((BUCKETS, HEADS), jnp.float32),
        table_part,
        (jnp.int32(0), seq_place * local_heads),
    )
    arranged = tuple(
        (
            arrange_rows(matrix, fsdp_parts, seq_parts)
            for matrix in (
                grad_wsquery,
                grad_wskey,
                grad_wsvalue,
                grad_wsout,
                grad_wcquery,
                grad_wckey,
                grad_wcvalue,
                grad_wcout,
                grad_wgate,
                grad_wup,
                grad_wdown,
            )
        )
    )
    spread = (
        lax.psum_scatter(arranged[0], ("seq", "fsdp"), scatter_dimension=0, tiled=True),
        lax.psum_scatter(arranged[1], ("seq", "fsdp"), scatter_dimension=0, tiled=True),
        lax.psum_scatter(arranged[2], ("seq", "fsdp"), scatter_dimension=0, tiled=True),
        lax.psum_scatter(arranged[3], ("seq", "fsdp"), scatter_dimension=0, tiled=True),
        lax.psum_scatter(arranged[4], ("seq", "fsdp"), scatter_dimension=0, tiled=True),
        lax.psum_scatter(arranged[5], ("seq", "fsdp"), scatter_dimension=0, tiled=True),
        lax.psum_scatter(arranged[6], ("seq", "fsdp"), scatter_dimension=0, tiled=True),
        lax.psum_scatter(arranged[7], ("seq", "fsdp"), scatter_dimension=0, tiled=True),
        lax.psum_scatter(arranged[8], ("seq", "fsdp"), scatter_dimension=0, tiled=True),
        lax.psum_scatter(arranged[9], ("seq", "fsdp"), scatter_dimension=0, tiled=True),
        lax.psum_scatter(arranged[10], ("seq", "fsdp"), scatter_dimension=0, tiled=True),
    )
    summed = (
        lax.all_gather(spread[0].astype(jnp.bfloat16), "seq", axis=0, tiled=True).astype(
            jnp.float32
        ),
        lax.all_gather(spread[1].astype(jnp.bfloat16), "seq", axis=0, tiled=True).astype(
            jnp.float32
        ),
        lax.all_gather(spread[2].astype(jnp.bfloat16), "seq", axis=0, tiled=True).astype(
            jnp.float32
        ),
        lax.all_gather(spread[3].astype(jnp.bfloat16), "seq", axis=0, tiled=True).astype(
            jnp.float32
        ),
        lax.all_gather(spread[4].astype(jnp.bfloat16), "seq", axis=0, tiled=True).astype(
            jnp.float32
        ),
        lax.all_gather(spread[5].astype(jnp.bfloat16), "seq", axis=0, tiled=True).astype(
            jnp.float32
        ),
        lax.all_gather(spread[6].astype(jnp.bfloat16), "seq", axis=0, tiled=True).astype(
            jnp.float32
        ),
        lax.all_gather(spread[7].astype(jnp.bfloat16), "seq", axis=0, tiled=True).astype(
            jnp.float32
        ),
        lax.all_gather(spread[8].astype(jnp.bfloat16), "seq", axis=0, tiled=True).astype(
            jnp.float32
        ),
        lax.all_gather(spread[9].astype(jnp.bfloat16), "seq", axis=0, tiled=True).astype(
            jnp.float32
        ),
        lax.all_gather(spread[10].astype(jnp.bfloat16), "seq", axis=0, tiled=True).astype(
            jnp.float32
        ),
    )
    small = lax.psum((grad_gain_one, grad_gain_two, grad_gain_three, table_full), ("seq", "fsdp"))
    return (
        result.astype(jnp.bfloat16)[None],
        grad_source[None],
        grad_enc_rows[None],
        small[0],
        small[1],
        small[2],
        small[3],
        summed[0],
        summed[1],
        summed[2],
        summed[3],
        summed[4],
        summed[5],
        summed[6],
        summed[7],
        summed[8],
        summed[9],
        summed[10],
    )


def solution(mesh):
    placed = (
        P("fsdp", "seq", None),
        P("fsdp", "seq", None),
        P("fsdp"),
        P("fsdp", "seq", None),
        P(),
        P(),
        P(),
        P(),
        P("fsdp", None),
        P("fsdp", None),
        P("fsdp", None),
        P("fsdp", None),
        P("fsdp", None),
        P("fsdp", None),
        P("fsdp", None),
        P("fsdp", None),
        P("fsdp", None),
        P("fsdp", None),
        P("fsdp", None),
    )
    return jax.shard_map(
        local,
        mesh=mesh,
        in_specs=placed,
        out_specs=(
            P("fsdp", "seq", None),
            P("fsdp", "seq", None),
            P("fsdp", "seq", None),
            P(),
            P(),
            P(),
            P(),
            P("fsdp", None),
            P("fsdp", None),
            P("fsdp", None),
            P("fsdp", None),
            P("fsdp", None),
            P("fsdp", None),
            P("fsdp", None),
            P("fsdp", None),
            P("fsdp", None),
            P("fsdp", None),
            P("fsdp", None),
        ),
        check_vma=False,
    )
```

profile of v0, /device:TPU:0, one launch (start us, length us, event | category | flops | bytes accessed | tf_op | source)
XLA Modules:
  0.0 1552.5 jit_solution(5246350604869401551)
XLA Ops:
  16.4 18.7 %all-gather.12.cloned.1.call-done = bf16[768,768]{1,0:T(8,128)(2,1)} async-done(((bf16[96,768]{1,0:T(8,128)(2,1)}), bf16[768,768]{1,0:T(8,128)(2,1)}) %all-gather.12.cloned.1.call-update) | async-done | bytes 1179664 | tf_op jit(solution)/shard_map/all_gather | solution.py:218
  41.6 17.6 %all-gather.14.cloned.1.call-done = bf16[768,768]{1,0:T(8,128)(2,1)} async-done(((bf16[96,768]{1,0:T(8,128)(2,1)}), bf16[768,768]{1,0:T(8,128)(2,1)}) %all-gather.14.cloned.1.call-update) | async-done | bytes 1179664 | tf_op jit(solution)/shard_map/all_gather | solution.py:219
  66.9 16.4 %all-gather.16.cloned.1.call-done = bf16[768,768]{1,0:T(8,128)(2,1)} async-done(((bf16[96,768]{1,0:T(8,128)(2,1)}), bf16[768,768]{1,0:T(8,128)(2,1)}) %all-gather.16.cloned.1.call-update) | async-done | bytes 1179664 | tf_op jit(solution)/shard_map/all_gather | solution.py:220
  99.4 130.2 %while.60 = (s32[]{:T(128)}, bf16[2,512,192]{1,2,0:T(8,128)(2,1)}, f32[2,3,512]{2,1,0:T(4,128)}, s32[2]{0:T(128)S(1)}, s32[]{:T(128)}, /*index=5*/bf16[1024,192]...) while((s32[]{:T(128)}, bf16[2,512,192]{1,2,0:T(8,128)(2,1)}, ...), condition=%wide.region_4.5_spmd, body=%wide.region_1.4_spmd.sunk | while | flops 416382976 | bytes 132237736 | solution.py:128
  118.7 15.9 %reshape.661 = f32[2360832]{0:T(1024)} reshape(f32[3,512,1537]{2,1,0:T(8,128)} %broadcast_in_dim.136) | data formatting | bytes 18886656 | tf_op jit(solution)/shard_map/while
  134.6 13.2 reshape.662
  152.5 6.6 copy.225
  177.3 16.0 %reshape.661 = f32[2360832]{0:T(1024)} reshape(f32[3,512,1537]{2,1,0:T(8,128)} %broadcast_in_dim.136) | data formatting | bytes 18886656 | tf_op jit(solution)/shard_map/while
  193.3 13.3 reshape.662
  211.1 6.6 copy.225
  298.0 22.6 %all-gather.32.cloned.1.call-done = bf16[2048,768]{1,0:T(8,128)(2,1)} async-done(((bf16[256,768]{1,0:T(8,128)(2,1)}), bf16[2048,768]{1,0:T(8,128)(2,1)}) %all-gather.32.cloned.1.call-update) | async-done | bytes 3145744 | tf_op jit(solution)/shard_map/all_gather | solution.py:228
  345.0 21.4 %while.62 = (s32[]{:T(128)}, f32[512,3,64]{0,2,1:T(8,128)}, f32[512,3,64]{0,2,1:T(8,128)}, bf16[2,512,192]{1,2,0:T(8,128)(2,1)}, s32[2]{0:T(128)S(1)}, /*index=5...) while((s32[]{:T(128)}, f32[512,3,64]{0,2,1:T(8,128)}, ...), condition=%wide.region_14.15_spmd.clone, body=%wide.region_12.14_spmd.clone.sunk | while | flops 510884352 | bytes 50031324 | solution.py:189
  367.5 8.1 all_to_all.280
  379.5 8.1 all_to_all.281
  392.0 9.4 all_to_all.282
  421.4 288.1 %while.63 = (s32[]{:T(128)}, f32[1024,3,64]{0,2,1:T(8,128)}, f32[1024,3,64]{0,2,1:T(8,128)}, f32[3,1024]{1,0:T(4,128)}, bf16[2,512,192]{1,2,0:T(8,128)(2,1)}, /*...) while((s32[]{:T(128)}, f32[1024,3,64]{0,2,1:T(8,128)}, ...), condition=%wide.region_19.20_spmd.clone, body=%wide.region_16.19_spmd.clone.sunk | while | flops 1027445248 | bytes 272312992 | solution.py:189
  435.5 15.8 %reshape.664 = f32[2360832]{0:T(1024)} reshape(f32[3,512,1537]{2,1,0:T(8,128)} %broadcast_in_dim.137) | data formatting | bytes 18886656 | tf_op jit(solution)/shard_map/while
  451.3 13.2 reshape.665
  464.5 22.7 %slice.43 = f32[3,786432]{1,0:T(4,128)} slice(f32[3,786944]{1,0:T(4,128)} %reshape.665), slice={[0:3], [0:786432]} | slice | bytes 18874368 | tf_op jit(solution)/shard_map/while/body/eval_jaxpr/slice | solution.py:48
  487.3 11.6 copy.226
  517.0 6.4 copy.227
  528.6 13.3 reshape.666
  541.9 16.7 %reshape.667 = f32[3,512,1537]{2,1,0:T(8,128)} reshape(f32[2360832]{0:T(1024)} %reshape.666) | data formatting | bytes 18886656 | tf_op jit(solution)/shard_map/while/body/eval_jaxpr/transpose(jvp())/reshape | solution.py:48
  581.2 15.9 %reshape.664 = f32[2360832]{0:T(1024)} reshape(f32[3,512,1537]{2,1,0:T(8,128)} %broadcast_in_dim.137) | data formatting | bytes 18886656 | tf_op jit(solution)/shard_map/while
  597.1 13.2 reshape.665
  610.3 11.5 slice.43
  621.8 11.6 copy.226
  652.8 6.4 copy.227
  664.4 13.4 reshape.666
  677.8 16.6 %reshape.667 = f32[3,512,1537]{2,1,0:T(8,128)} reshape(f32[2360832]{0:T(1024)} %reshape.666) | data formatting | bytes 18886656 | tf_op jit(solution)/shard_map/while/body/eval_jaxpr/transpose(jvp())/reshape | solution.py:48
  780.6 40.1 %all-reduce.2 = (f32[768]{0:T(1024)}, f32[768]{0:T(1024)}, f32[768]{0:T(1024)}, f32[32,12]{0,1:T(8,128)}) all-reduce(f32[768]{0:T(1024)S(1)} %get-tuple-element.478, f32[768]{0:T(1024)S(1)} %copy-done.73, f32[768]{0:T(1024)S(1)} %copy-done.72, f32[32,12]{0,1:T(8,128)S(1)} %dynamic_update_slice.38), channel_id=1, replica_groups=mesh['seq'=4,'fsdp'=8] {'seq','fsdp'}, use_global_device_ids=true, to_apply=%region_22.23 | all-reduce | flops 2688 | bytes 21504 | tf_op jit(solution)/shard_map/psum | solution.py:474
  821.5 9.9 all_gather.95
  833.0 8.7 all_gather.93
  843.3 7.6 all_gather.94
  852.5 8.8 all_gather.91
  864.9 8.5 all_gather.92
  874.1 93.9 %reduce-scatter.12.cloned.1.call-done = f32[24,768]{1,0:T(8,128)} async-done(((f32[768,768]{1,0:T(8,128)}), f32[24,768]{1,0:T(8,128)}) %reduce-scatter.12.cloned.1.call-update) | async-done | bytes 73744 | tf_op jit(solution)/shard_map/reduce_scatter | solution.py:427
  968.9 8.5 all_gather.88
  978.2 93.1 %reduce-scatter.14.cloned.1.call-done = f32[24,768]{1,0:T(8,128)} async-done(((f32[768,768]{1,0:T(8,128)}), f32[24,768]{1,0:T(8,128)}) %reduce-scatter.14.cloned.1.call-update) | async-done | bytes 73744 | tf_op jit(solution)/shard_map/reduce_scatter | solution.py:428
  1072.2 8.5 all_gather.89
  1081.4 94.1 %reduce-scatter.16.cloned.1.call-done = f32[24,768]{1,0:T(8,128)} async-done(((f32[768,768]{1,0:T(8,128)}), f32[24,768]{1,0:T(8,128)}) %reduce-scatter.16.cloned.1.call-update) | async-done | bytes 73744 | tf_op jit(solution)/shard_map/reduce_scatter | solution.py:429
  1176.4 8.5 all_gather.90
  1185.6 108.7 %reduce-scatter.28.cloned.1.call-done = f32[24,2048]{1,0:T(8,128)} async-done(((f32[768,2048]{1,0:T(8,128)}), f32[24,2048]{1,0:T(8,128)}) %reduce-scatter.28.cloned.1.call-update) | async-done | bytes 196624 | tf_op jit(solution)/shard_map/reduce_scatter | solution.py:435
  1295.3 10.1 all_gather.96
  1306.3 108.1 %reduce-scatter.30.cloned.1.call-done = f32[24,2048]{1,0:T(8,128)} async-done(((f32[768,2048]{1,0:T(8,128)}), f32[24,2048]{1,0:T(8,128)}) %reduce-scatter.30.cloned.1.call-update) | async-done | bytes 196624 | tf_op jit(solution)/shard_map/reduce_scatter | solution.py:436
  1415.4 10.0 all_gather.97
  1426.3 107.3 %reduce-scatter.32.cloned.1.call-done = f32[64,768]{1,0:T(8,128)} async-done(((f32[2048,768]{1,0:T(8,128)}), f32[64,768]{1,0:T(8,128)}) %reduce-scatter.32.cloned.1.call-update) | async-done | bytes 196624 | tf_op jit(solution)/shard_map/reduce_scatter | solution.py:437
  1534.5 10.0 all_gather.98
  (593 shorter events, 411.1 us)
Async XLA Ops:
  7.2 228.3 %copy-start = (bf16[1,128,768]{2,1,0:T(8,128)(2,1)S(1)}, bf16[1,128,768]{2,1,0:T(8,128)(2,1)}, u32[]{:S(2)}) copy-start(bf16[1,128,768]{2,1,0:T(8,128)(2,1)} %param.28) | copy-start | bytes 589828
  7.2 27.9 %copy-start.26 = (bf16[1,256,768]{2,1,0:T(8,128)(2,1)S(1)}, bf16[1,256,768]{2,1,0:T(8,128)(2,1)}, u32[]{:S(2)}) copy-start(bf16[1,256,768]{2,1,0:T(8,128)(2,1)} %param.27) | copy-start | bytes 1179652
  7.2 27.9 %all-gather.12.cloned.1.call-start = ((), (), s32[]{:S(2)}) async-start(), calls=%async_computation.27 | async-start | bytes 1327104 | tf_op jit(solution)/shard_map/all_gather | solution.py:218
  8.0 51.2 %all-gather.14.cloned.1.call-start = ((), (), s32[]{:S(2)}) async-start(), calls=%async_computation.28 | async-start | bytes 1327104 | tf_op jit(solution)/shard_map/all_gather | solution.py:219
  8.7 74.6 %all-gather.16.cloned.1.call-start = ((), (), s32[]{:S(2)}) async-start(), calls=%async_computation.29 | async-start | bytes 1327104 | tf_op jit(solution)/shard_map/all_gather | solution.py:220
  9.4 226.1 %all-gather.22.cloned.1.call-start = ((), (), s32[]{:S(2)}) async-start(), calls=%async_computation.32 | async-start | bytes 1327104 | tf_op jit(solution)/shard_map/all_gather | solution.py:223
  10.0 228.0 %all-gather.24.cloned.1.call-start = ((), (), s32[]{:S(2)}) async-start(), calls=%async_computation.33 | async-start | bytes 1327104 | tf_op jit(solution)/shard_map/all_gather | solution.py:224
  10.6 234.4 %all-gather.18.cloned.1.call-start = ((), (), s32[]{:S(2)}) async-start(), calls=%async_computation.30 | async-start | bytes 1327104 | tf_op jit(solution)/shard_map/all_gather | solution.py:221
  11.2 242.3 %all-gather.20.cloned.1.call-start = ((), (), s32[]{:S(2)}) async-start(), calls=%async_computation.31 | async-start | bytes 1327104 | tf_op jit(solution)/shard_map/all_gather | solution.py:222
  11.9 268.7 %all-gather.26.cloned.1.call-start = ((), (), s32[]{:S(2)}) async-start(), calls=%async_computation.34 | async-start | bytes 1327104 | tf_op jit(solution)/shard_map/all_gather | solution.py:225
  12.7 275.2 %all-gather.28.cloned.1.call-start = ((), (), s32[]{:S(2)}) async-start(), calls=%async_computation.35 | async-start | bytes 3538944 | tf_op jit(solution)/shard_map/all_gather | solution.py:226
  13.4 279.1 %all-gather.30.cloned.1.call-start = ((), (), s32[]{:S(2)}) async-start(), calls=%async_computation.36 | async-start | bytes 3538944 | tf_op jit(solution)/shard_map/all_gather | solution.py:227
  14.7 68.6 %copy-start.70 = (f32[768]{0:T(1024)}, f32[768]{0:T(1024)S(1)}, u32[]{:S(2)}) copy-start(f32[768]{0:T(1024)S(1)} %convert_element_type.428) | copy-start | bytes 9220
  16.4 66.9 %copy-start.76 = (f32[256]{0:T(256)}, f32[256]{0:T(256)S(1)}, u32[]{:S(2)}) copy-start(f32[256]{0:T(256)S(1)} %fusion.88) | copy-start | bytes 3076
  37.8 28.5 %copy-start.87 = (bf16[768]{0:T(1024)(128)(2,1)S(1)}, bf16[768]{0:T(1024)(128)(2,1)}, u32[]{:S(2)}) copy-start(bf16[768]{0:T(1024)(128)(2,1)} %param.32) | copy-start | bytes 4612
  37.8 24.1 %all-to-all-start = ((bf16[256,4,192]{0,2,1:T(8,128)(2,1)}), bf16[256,4,192]{0,2,1:T(8,128)(2,1)S(1)}, u32[]{:S(2)}, u32[]{:S(2)}) async-start(bf16[256,4,192]{0,2,1:T(8,128)(2,1)} %bitcast.13), calls=%async_computation | async-start | bytes 786432 | tf_op jit(solution)/shard_map/all_to_all | solution.py:268
  61.9 24.1 %all-to-all-start.1 = ((bf16[256,4,192]{0,2,1:T(8,128)(2,1)}), bf16[256,4,192]{0,2,1:T(8,128)(2,1)S(1)}, u32[]{:S(2)}, u32[]{:S(2)}) async-start(bf16[256,4,192]{0,2,1:T(8,128)(2,1)} %bitcast.15), calls=%async_computation.1 | async-start | bytes 786432 | tf_op jit(solution)/shard_map/all_to_all | solution.py:269
  65.5 255.0 %all-gather.32.cloned.1.call-start = ((), (), s32[]{:S(2)}) async-start(), calls=%async_computation.37 | async-start | bytes 3538944 | tf_op jit(solution)/shard_map/all_gather | solution.py:228
  86.0 10.7 all-to-all-start.2
  232.0 9.6 all-to-all-start.3
  241.6 8.5 all-to-all-start.5
  246.9 38.8 %copy-start.9 = (f32[256,768]{1,0:T(8,128)}, f32[256,768]{1,0:T(8,128)S(1)}, u32[]{:S(2)}) copy-start(f32[256,768]{1,0:T(8,128)S(1)} %get-tuple-element.581) | copy-start | bytes 2359300
  250.1 8.5 all-to-all-start.6
  258.7 9.3 all-to-all-start.4
  276.2 9.5 all-to-all-start.7
  280.5 40.0 %copy-start.78 = (f32[256]{0:T(256)}, f32[256]{0:T(256)S(1)}, u32[]{:S(2)}) copy-start(f32[256]{0:T(256)S(1)} %compare_convert_fusion) | copy-start | bytes 3076
  287.7 43.0 %copy-start.16 = (f32[256,768]{1,0:T(8,128)}, f32[256,768]{1,0:T(8,128)S(1)}, u32[]{:S(2)}) copy-start(f32[256,768]{1,0:T(8,128)S(1)} %get-tuple-element.583) | copy-start | bytes 2359300
  292.5 28.1 %copy-start.51 = (bf16[1,256,768]{2,1,0:T(8,128)(2,1)S(1)}, bf16[1,256,768]{2,1,0:T(8,128)(2,1)}, u32[]{:S(2)}) copy-start(bf16[1,256,768]{2,1,0:T(8,128)(2,1)} %param.30) | copy-start | bytes 1179652
  333.4 10.7 all-to-all-start.8
  337.1 483.5 %reduce-scatter.26.cloned.1.call-start = ((), (), s32[]{:S(2)}) async-start(), calls=%async_computation.45 | async-start | bytes 2433024 | tf_op jit(solution)/shard_map/reduce_scatter | solution.py:434
  339.3 492.9 %reduce-scatter.22.cloned.1.call-start = ((), (), s32[]{:S(2)}) async-start(), calls=%async_computation.43 | async-start | bytes 2433024 | tf_op jit(solution)/shard_map/reduce_scatter | solution.py:432
  378.4 464.1 %reduce-scatter.24.cloned.1.call-start = ((), (), s32[]{:S(2)}) async-start(), calls=%async_computation.44 | async-start | bytes 2433024 | tf_op jit(solution)/shard_map/reduce_scatter | solution.py:433
  390.4 461.3 %reduce-scatter.18.cloned.1.call-start = ((), (), s32[]{:S(2)}) async-start(), calls=%async_computation.41 | async-start | bytes 2433024 | tf_op jit(solution)/shard_map/reduce_scatter | solution.py:430
  408.5 10.7 all-to-all-start.10
  412.0 452.0 %reduce-scatter.20.cloned.1.call-start = ((), (), s32[]{:S(2)}) async-start(), calls=%async_computation.42 | async-start | bytes 2433024 | tf_op jit(solution)/shard_map/reduce_scatter | solution.py:431
  712.0 9.4 all-to-all-start.11
  721.4 12.9 all-to-all-start.12
  727.9 15.7 %copy-start.28 = (bf16[1,256,768]{2,1,0:T(8,128)(2,1)S(1)}, bf16[1,256,768]{2,1,0:T(8,128)(2,1)}, u32[]{:S(2)}) copy-start(bf16[1,256,768]{2,1,0:T(8,128)(2,1)} %param.27) | copy-start | bytes 1179652
  727.9 15.7 %copy-start.71 = (f32[768]{0:T(1024)S(1)}, f32[768]{0:T(1024)}, u32[]{:S(2)}) copy-start(f32[768]{0:T(1024)} %copy-done.70) | copy-start | bytes 9220
  727.9 15.7 %copy-start.77 = (f32[256]{0:T(256)S(1)}, f32[256]{0:T(256)}, u32[]{:S(2)}) copy-start(f32[256]{0:T(256)} %copy-done.76) | copy-start | bytes 3076
  734.3 9.3 all-to-all-start.13
  737.8 230.2 %reduce-scatter.12.cloned.1.call-start = ((), (), s32[]{:S(2)}) async-start(), calls=%async_computation.38 | async-start | bytes 2433024 | tf_op jit(solution)/shard_map/reduce_scatter | solution.py:427
  749.2 322.2 %reduce-scatter.14.cloned.1.call-start = ((), (), s32[]{:S(2)}) async-start(), calls=%async_computation.39 | async-start | bytes 2433024 | tf_op jit(solution)/shard_map/reduce_scatter | solution.py:428
  751.4 424.1 %reduce-scatter.16.cloned.1.call-start = ((), (), s32[]{:S(2)}) async-start(), calls=%async_computation.40 | async-start | bytes 2433024 | tf_op jit(solution)/shard_map/reduce_scatter | solution.py:429
  753.7 540.6 %reduce-scatter.28.cloned.1.call-start = ((), (), s32[]{:S(2)}) async-start(), calls=%async_computation.46 | async-start | bytes 6488064 | tf_op jit(solution)/shard_map/reduce_scatter | solution.py:435
  759.1 655.4 %reduce-scatter.30.cloned.1.call-start = ((), (), s32[]{:S(2)}) async-start(), calls=%async_computation.47 | async-start | bytes 6488064 | tf_op jit(solution)/shard_map/reduce_scatter | solution.py:436
  764.4 769.1 %reduce-scatter.32.cloned.1.call-start = ((), (), s32[]{:S(2)}) async-start(), calls=%async_computation.48 | async-start | bytes 6488064 | tf_op jit(solution)/shard_map/reduce_scatter | solution.py:437
  1295.2 250.2 %copy-start.1 = (bf16[1,128,768]{2,1,0:T(8,128)(2,1)S(1)}, bf16[1,128,768]{2,1,0:T(8,128)(2,1)}, u32[]{:S(2)}) copy-start(bf16[1,128,768]{2,1,0:T(8,128)(2,1)} %param.28) | copy-start | bytes 589828
  (107 other events, 403.4 us)
Sparse Core Ops, SparseCore 0:
  9.7 25.3 all-gather.11
  36.7 22.4 all-gather.13
  60.8 22.4 all-gather.15
  84.8 22.4 all-gather.21
  108.7 22.4 all-gather.23
  132.7 22.4 all-gather.17
  156.8 22.4 all-gather.19
  180.9 22.4 all-gather.25
  205.0 38.0 all-gather.27
  244.6 37.1 all-gather.29
  283.4 37.1 all-gather.31
  342.9 103.0 reduce-scatter.25
  452.2 97.9 reduce-scatter.21
  555.3 98.1 reduce-scatter.23
  659.5 100.9 reduce-scatter.17
  765.7 98.3 reduce-scatter.19
  870.0 97.9 reduce-scatter.11
  973.1 98.1 reduce-scatter.13
  1077.4 97.9 reduce-scatter.15
  1181.0 113.2 reduce-scatter.27
  1300.9 113.5 reduce-scatter.29
  1420.1 113.4 reduce-scatter.31
where the time goes:
time: 1560 us; the launch traced here: 1550 us
  waiting for transfers between devices  735 us (47%)
  local copies, waits for them, and re-layouts  381 us (24%)
  blocking collectives  165 us (11%)
  matrix products  118 us (8%)
  other arithmetic  64.8 us (4%)
  starting transfers between devices  46.8 us (3%)
  loops' own time  26.2 us (2%)
  between operations  16.4 us (1%)
    while x114, local copies, waits for them, and re-layouts  152 us
    reduce_scatter x1, waiting for transfers between devices, local(): lax.psum_scatter(arranged[8], ('seq', 'fsdp'), scatter_dimension=0, tiled...  109 us
    reduce_scatter x1, waiting for transfers between devices, local(): lax.psum_scatter(arranged[9], ('seq', 'fsdp'), scatter_dimension=0, tiled...  108 us
    reduce_scatter x1, waiting for transfers between devices, local(): lax.psum_scatter(arranged[10], ('seq', 'fsdp'), scatter_dimension=0, tile...  107 us
    reduce_scatter x1, waiting for transfers between devices, local(): lax.psum_scatter(arranged[2], ('seq', 'fsdp'), scatter_dimension=0, tiled...  94.1 us
    reduce_scatter x1, waiting for transfers between devices, local(): lax.psum_scatter(arranged[0], ('seq', 'fsdp'), scatter_dimension=0, tiled...  93.9 us
    reduce_scatter x1, waiting for transfers between devices, local(): lax.psum_scatter(arranged[1], ('seq', 'fsdp'), scatter_dimension=0, tiled...  93.1 us
    reshape x6, local copies, waits for them, and re-layouts, diagonal_fill(): repeated.reshape(head_count, block_rows * span)[:, :block_rows * (span - 1)]  86.3 us
  transfers between devices with their start and end apart: 35, of which 22 were waited for; matrix products, arithmetic and copies ran while one was open for 34% of the time, Pallas kernels for 0%

commit v1 on v0

v1 whole, which is shorter than its diff:
```python
import functools
import math

import jax
import jax.numpy as jnp
from jax import lax
from jax.experimental import pallas as pl
from jax.experimental.pallas import tpu as pltpu
from jax.sharding import PartitionSpec as P

HEADS = 12
HEAD = 64
BUCKETS = 32
MAX_DISTANCE = 128
EPSILON = 1e-06
NEGATIVE = -1e30
BLOCK = 256
PAIR = 2 * HEAD
MESH = pl.DeviceIdType.MESH


def thresholds():
    exact_limit = BUCKETS // 2
    return [
        int(math.ceil(exact_limit * (MAX_DISTANCE / exact_limit) ** (number / exact_limit)))
        for number in range(1, exact_limit)
    ]


def bucket_ids(key_count):
    exact_limit = BUCKETS // 2
    offsets = jnp.arange(key_count, dtype=jnp.int32)
    passed = jnp.zeros((key_count,), jnp.int32)
    for border in thresholds():
        passed = passed + (offsets >= border).astype(jnp.int32)
    return jnp.where(offsets < exact_limit, offsets, exact_limit + passed)


def rms_scale(values, gain):
    return values * lax.rsqrt(jnp.mean(values * values, axis=-1, keepdims=True) + EPSILON) * gain


def norm_back(values, gain, grad_normed):
    _, pullback = jax.vjp(rms_scale, values, gain)
    return pullback(grad_normed)


def product(left, right):
    return jnp.dot(left, right, preferred_element_type=jnp.float32)


def inner_rows(left, right):
    return lax.dot_general(
        left, right, (((0,), (0,)), ((), ())), preferred_element_type=jnp.float32
    )


def outer_rows(left, right):
    return lax.dot_general(
        left, right, (((1,), (1,)), ((), ())), preferred_element_type=jnp.float32
    )


def iota(shape, axis):
    return lax.broadcasted_iota(jnp.int32, shape, axis)


def head_rows(value, head):
    place = iota(value.shape, 0) // HEAD
    return jnp.where(place == head, value, jnp.zeros_like(value))


def head_cols(value, head):
    place = iota(value.shape, 1) // HEAD
    return jnp.where(place == head, value, jnp.zeros_like(value))


def skew(profile_row):
    wide = jnp.broadcast_to(profile_row, (BLOCK, BLOCK))
    return pltpu.roll(wide, 0, 1, stride=1, stride_axis=0)


def unskew(tile):
    rows = iota(tile.shape, 0)
    bit = 1
    while bit < BLOCK:
        tile = jnp.where((rows // bit) % 2 == 1, pltpu.roll(tile, BLOCK - bit, 1), tile)
        bit *= 2
    return tile


def self_forward_kernel(place_ref, profile_ref, q_ref, k_ref, v_ref, o_ref, ot_ref, log_ref, s_buf, vt_buf):
    place = place_ref[0]
    length = place_ref[1]
    qt = q_ref[...].T
    vt_buf[...] = v_ref[...].T
    later = iota((BLOCK, BLOCK), 1) >= iota((BLOCK, BLOCK), 0)
    key_rows = iota((BLOCK, BLOCK), 0)
    for head in range(2):
        qm = head_rows(qt, head)
        profile = profile_ref[0, head : head + 1, :]
        far = profile[:, BLOCK - 1 :]

        def tile_scores(block, bias):
            start = pl.multiple_of(block * BLOCK, BLOCK)
            scores = product(k_ref[pl.ds(start, BLOCK), :], qm) + bias
            scores = jnp.where(key_rows < length - start, scores, NEGATIVE)
            return start, scores

        def far_step(block, top):
            start, scores = tile_scores(block, far)
            s_buf[pl.ds(start, BLOCK), :] = scores
            return jnp.maximum(top, jnp.max(scores, axis=0, keepdims=True))

        top = lax.fori_loop(0, place - 1, far_step, jnp.full((1, BLOCK), NEGATIVE, jnp.float32))
        near = skew(profile)

        def near_step(block, top):
            start, scores = tile_scores(block, jnp.where(later, far, near))
            s_buf[pl.ds(start, BLOCK), :] = scores
            return jnp.maximum(top, jnp.max(scores, axis=0, keepdims=True))

        top = lax.fori_loop(jnp.maximum(place - 1, 0), place, near_step, top)
        start, scores = tile_scores(place, near)
        scores = jnp.where(later, scores, NEGATIVE)
        s_buf[pl.ds(start, BLOCK), :] = scores
        top = jnp.maximum(top, jnp.max(scores, axis=0, keepdims=True))

        def raise_step(block, total):
            start = pl.multiple_of(block * BLOCK, BLOCK)
            raised = jnp.exp(s_buf[pl.ds(start, BLOCK), :] - top)
            s_buf[pl.ds(start, BLOCK), :] = raised
            return total + jnp.sum(raised, axis=0, keepdims=True)

        total = lax.fori_loop(0, place + 1, raise_step, jnp.zeros((1, BLOCK), jnp.float32))
        share = 1.0 / total

        def mix_step(block, mixed):
            start = pl.multiple_of(block * BLOCK, BLOCK)
            soft = (s_buf[pl.ds(start, BLOCK), :] * share).astype(jnp.bfloat16)
            return mixed + product(
                vt_buf[head * HEAD : (head + 1) * HEAD, pl.ds(start, BLOCK)], soft
            )

        mixed = lax.fori_loop(0, place + 1, mix_step, jnp.zeros((HEAD, BLOCK), jnp.float32))
        ot_ref[head * HEAD : (head + 1) * HEAD, :] = mixed
        log_ref[0, head : head + 1, :] = top + jnp.log(total)
    o_ref[...] = ot_ref[...].T.astype(jnp.bfloat16)


def cross_forward_kernel(q_ref, k_ref, v_ref, o_ref, ot_ref, log_ref):
    qt = q_ref[...].T
    vt = v_ref[...].T
    for head in range(2):
        scores = product(k_ref[...], head_rows(qt, head))
        top = jnp.max(scores, axis=0, keepdims=True)
        raised = jnp.exp(scores - top)
        total = jnp.sum(raised, axis=0, keepdims=True)
        soft = (raised * (1.0 / total)).astype(jnp.bfloat16)
        ot_ref[head * HEAD : (head + 1) * HEAD, :] = product(
            vt[head * HEAD : (head + 1) * HEAD, :], soft
        )
        log_ref[0, head : head + 1, :] = top + jnp.log(total)
    o_ref[...] = ot_ref[...].T.astype(jnp.bfloat16)


def self_backward_kernel(
    place_ref, profile_ref, q_ref, k_ref, v_ref, g_ref, ot_ref, log_ref,
    dq_ref, dk_ref, dv_ref, near_ref, far_ref, tile_buf, kt_buf, dqt_buf, far_buf,
):
    place = place_ref[0]
    length = place_ref[1]
    q_value = q_ref[...]
    g_value = g_ref[...]
    qt = q_value.T
    gt = g_value.T
    kt_buf[...] = k_ref[...].T
    later = iota((BLOCK, BLOCK), 1) >= iota((BLOCK, BLOCK), 0)
    key_rows = iota((BLOCK, BLOCK), 0)
    both_q = jnp.concatenate([head_cols(q_value, 0), head_cols(q_value, 1)], axis=0)
    both_g = jnp.concatenate([head_cols(g_value, 0), head_cols(g_value, 1)], axis=0)
    weighted = gt.astype(jnp.float32) * ot_ref[...]
    sides = []
    for head in range(2):
        rows = slice(head * HEAD, (head + 1) * HEAD)
        profile = profile_ref[0, head : head + 1, :]
        delta = jnp.sum(weighted[rows, :], axis=0, keepdims=True)
        sides.append(
            (head_rows(qt, head), head_rows(gt, head), profile[:, BLOCK - 1 :], delta,
             log_ref[0, head : head + 1, :], rows)
        )
        tile_buf[head] = skew(profile)
    dqt_buf[...] = jnp.zeros_like(dqt_buf)
    far_buf[...] = jnp.zeros_like(far_buf)

    def one_block(block, kind):
        start = pl.multiple_of(block * BLOCK, BLOCK)
        k_block = k_ref[pl.ds(start, BLOCK), :]
        v_block = v_ref[pl.ds(start, BLOCK), :]
        softs, grads = [], []
        for head, (qm, gm, far, delta, log, rows) in enumerate(sides):
            if kind == 0:
                bias = tile_buf[head]
            elif kind == 1:
                bias = jnp.where(later, far, tile_buf[head])
            else:
                bias = far
            scores = product(k_block, qm) + bias
            allowed = key_rows < length - start
            if kind == 0:
                allowed = allowed & later
            soft = jnp.exp(jnp.where(allowed, scores, NEGATIVE) - log)
            grad_soft = product(v_block, gm)
            grad = (soft * (grad_soft - delta)).astype(jnp.bfloat16)
            softs.append(soft.astype(jnp.bfloat16))
            grads.append(grad)
            dqt_buf[rows, :] += product(kt_buf[rows, pl.ds(start, BLOCK)], grad)
            wide = grad.astype(jnp.float32)
            if kind == 2:
                far_buf[head : head + 1, :] += jnp.sum(wide, axis=0, keepdims=True)
            elif kind == 1:
                far_buf[head : head + 1, :] += jnp.sum(
                    jnp.where(later, wide, 0.0), axis=0, keepdims=True
                )
                near_ref[0, head : head + 1, :] += jnp.sum(
                    unskew(jnp.where(later, 0.0, wide)), axis=0, keepdims=True
                )
            else:
                near_ref[0, head : head + 1, :] = jnp.sum(unskew(wide), axis=0, keepdims=True)
        dv_ref[pl.ds(start, BLOCK), :] = product(jnp.concatenate(softs, axis=1), both_g).astype(
            jnp.bfloat16
        )
        dk_ref[pl.ds(start, BLOCK), :] = product(jnp.concatenate(grads, axis=1), both_q).astype(
            jnp.bfloat16
        )

    one_block(place, 0)

    @pl.when(place >= 1)
    def _():
        one_block(place - 1, 1)

    @pl.loop(0, place - 1)
    def _(block):
        one_block(block, 2)

    @pl.loop(place + 1, k_ref.shape[0] // BLOCK)
    def _(block):
        start = pl.multiple_of(block * BLOCK, BLOCK)
        dk_ref[pl.ds(start, BLOCK), :] = jnp.zeros((BLOCK, PAIR), jnp.bfloat16)
        dv_ref[pl.ds(start, BLOCK), :] = jnp.zeros((BLOCK, PAIR), jnp.bfloat16)

    dq_ref[...] = dqt_buf[...].T.astype(jnp.bfloat16)
    far_ref[0] = far_buf[...]


def cross_backward_kernel(q_ref, k_ref, v_ref, g_ref, ot_ref, log_ref, dq_ref, dk_ref, dv_ref, dqt_buf):
    q_value = q_ref[...]
    g_value = g_ref[...]
    qt = q_value.T
    gt = g_value.T
    kt = k_ref[...].T
    both_q = jnp.concatenate([head_cols(q_value, 0), head_cols(q_value, 1)], axis=0)
    both_g = jnp.concatenate([head_cols(g_value, 0), head_cols(g_value, 1)], axis=0)
    weighted = gt.astype(jnp.float32) * ot_ref[...]
    keys = k_ref.shape[0]
    sides = []
    for head in range(2):
        rows = slice(head * HEAD, (head + 1) * HEAD)
        delta = jnp.sum(weighted[rows, :], axis=0, keepdims=True)
        sides.append(
            (head_rows(qt, head), head_rows(gt, head), delta, log_ref[0, head : head + 1, :], rows)
        )
    dqt_buf[...] = jnp.zeros_like(dqt_buf)
    step = min(BLOCK, keys)
    for start in range(0, keys, step):
        k_block = k_ref[start : start + step, :]
        v_block = v_ref[start : start + step, :]
        softs, grads = [], []
        for qm, gm, delta, log, rows in sides:
            soft = jnp.exp(product(k_block, qm) - log)
            grad = (soft * (product(v_block, gm) - delta)).astype(jnp.bfloat16)
            softs.append(soft.astype(jnp.bfloat16))
            grads.append(grad)
            dqt_buf[rows, :] += product(kt[rows, start : start + step], grad)
        dv_ref[start : start + step, :] = product(jnp.concatenate(softs, axis=1), both_g).astype(
            jnp.bfloat16
        )
        dk_ref[start : start + step, :] = product(jnp.concatenate(grads, axis=1), both_q).astype(
            jnp.bfloat16
        )
    dq_ref[...] = dqt_buf[...].T.astype(jnp.bfloat16)


def pair_block(rows):
    return pl.BlockSpec((rows, PAIR), lambda pair: (0, pair))


def turned_block(rows):
    return pl.BlockSpec((PAIR, rows), lambda pair: (pair, 0))


def head_block(width):
    return pl.BlockSpec((1, 2, width), lambda pair: (pair, 0, 0))


SCALARS = pl.BlockSpec(memory_space=pltpu.SMEM)
PAIRS = HEADS // 2


def shaped(shape, dtype):
    return jax.ShapeDtypeStruct(shape, dtype)


def self_forward(place, profile, queries, keys, values):
    rows, width = queries.shape
    count = keys.shape[0]
    return pl.pallas_call(
        self_forward_kernel,
        grid=(PAIRS,),
        in_specs=[SCALARS, head_block(BLOCK), pair_block(rows), pair_block(count), pair_block(count)],
        out_specs=[pair_block(rows), turned_block(rows), head_block(rows)],
        out_shape=[
            shaped((rows, width), jnp.bfloat16),
            shaped((width, rows), jnp.float32),
            shaped((PAIRS, 2, rows), jnp.float32),
        ],
        scratch_shapes=[pltpu.VMEM((count, rows), jnp.float32), pltpu.VMEM((PAIR, count), jnp.bfloat16)],
        name="self_forward",
    )(place, profile, queries, keys, values)


def cross_forward(queries, keys, values):
    rows, width = queries.shape
    count = keys.shape[0]
    return pl.pallas_call(
        cross_forward_kernel,
        grid=(PAIRS,),
        in_specs=[pair_block(rows), pair_block(count), pair_block(count)],
        out_specs=[pair_block(rows), turned_block(rows), head_block(rows)],
        out_shape=[
            shaped((rows, width), jnp.bfloat16),
            shaped((width, rows), jnp.float32),
            shaped((PAIRS, 2, rows), jnp.float32),
        ],
        name="cross_forward",
    )(queries, keys, values)


def self_backward(place, profile, queries, keys, values, grad_mixed, mixed_turned, log_totals):
    rows, width = queries.shape
    count = keys.shape[0]
    return pl.pallas_call(
        self_backward_kernel,
        grid=(PAIRS,),
        in_specs=[
            SCALARS, head_block(BLOCK), pair_block(rows), pair_block(count), pair_block(count),
            pair_block(rows), turned_block(rows), head_block(rows),
        ],
        out_specs=[
            pair_block(rows), pair_block(count), pair_block(count), head_block(BLOCK), head_block(rows),
        ],
        out_shape=[
            shaped((rows, width), jnp.bfloat16),
            shaped((count, width), jnp.bfloat16),
            shaped((count, width), jnp.bfloat16),
            shaped((PAIRS, 2, BLOCK), jnp.float32),
            shaped((PAIRS, 2, rows), jnp.float32),
        ],
        scratch_shapes=[
            pltpu.VMEM((2, BLOCK, BLOCK), jnp.float32),
            pltpu.VMEM((PAIR, count), jnp.bfloat16),
            pltpu.VMEM((PAIR, rows), jnp.float32),
            pltpu.VMEM((2, rows), jnp.float32),
        ],
        name="self_backward",
    )(place, profile, queries, keys, values, grad_mixed, mixed_turned, log_totals)


def cross_backward(queries, keys, values, grad_mixed, mixed_turned, log_totals):
    rows, width = queries.shape
    count = keys.shape[0]
    return pl.pallas_call(
        cross_backward_kernel,
        grid=(PAIRS,),
        in_specs=[
            pair_block(rows), pair_block(count), pair_block(count),
            pair_block(rows), turned_block(rows), head_block(rows),
        ],
        out_specs=[pair_block(rows), pair_block(count), pair_block(count)],
        out_shape=[
            shaped((rows, width), jnp.bfloat16),
            shaped((count, width), jnp.bfloat16),
            shaped((count, width), jnp.bfloat16),
        ],
        scratch_shapes=[pltpu.VMEM((PAIR, rows), jnp.float32)],
        name="cross_backward",
    )(queries, keys, values, grad_mixed, mixed_turned, log_totals)


class Peers:
    def __init__(self, planes):
        self.seq = lax.axis_index("seq")
        fsdp = lax.axis_index("fsdp")
        self.planes = planes
        self.plane = fsdp // 2
        self.core = fsdp % 2
        self.fsdp = fsdp
        self.along_x = self.seq + 1 - 2 * (self.seq % 2)
        self.along_y = (self.seq + 2) % 4
        self.corner = (self.along_x + 2) % 4
        self.partner = (self.seq, fsdp + 1 - 2 * self.core)
        self.to_x = (self.along_x, fsdp)
        self.to_y = (self.along_y, fsdp)
        self.to_corner = (self.corner, fsdp)

    def ahead(self, steps):
        return (self.plane + steps) % self.planes

    def at_plane(self, plane):
        return (self.seq, 2 * plane + self.core)

    def everyone(self):
        return [self.partner, self.to_x, self.to_y, self.to_corner] + [
            self.at_plane(self.ahead(k)) for k in range(1, self.planes)
        ]

    def meet(self):
        barrier = pltpu.get_barrier_semaphore()
        others = self.everyone()
        for other in others:
            pl.semaphore_signal(barrier, inc=1, device_id=other, device_id_type=MESH)
        pl.semaphore_wait(barrier, len(others))


def remote(source, target, send_sem, recv_sem, device):
    return pltpu.make_async_remote_copy(
        src_ref=source, dst_ref=target, send_sem=send_sem, recv_sem=recv_sem,
        device_id=device, device_id_type=MESH,
    )


class Stack:
    def __init__(self, rows, cols):
        self.rows, self.cols = rows, cols

    def own(self, ref, quarter, first=0, count=None):
        return ref.at[quarter, pl.ds(first, count or self.rows), :]

    def part(self, ref, quarter, plane, core, first=0, count=None):
        return ref.at[quarter, plane, core, pl.ds(first, count or self.rows), :]

    def planes(self, ref, quarter, core):
        return ref.at[quarter, :, core]

    def whole(self, ref, plane, core):
        return ref.at[:, plane, core]


class Wide:
    def __init__(self, rows, cols):
        self.rows, self.cols = rows, cols

    def own(self, ref, quarter, first=0, count=None):
        return ref.at[pl.ds(first, count or self.rows), pl.ds(quarter * self.cols, self.cols)]

    def part(self, ref, quarter, plane, core, first=0, count=None):
        return ref.at[
            plane, core, pl.ds(first, count or self.rows), pl.ds(quarter * self.cols, self.cols)
        ]

    def planes(self, ref, quarter, core):
        return ref.at[:, core, :, pl.ds(quarter * self.cols, self.cols)]

    def whole(self, ref, plane, core):
        return ref.at[plane, core]


class Tall:
    def __init__(self, rows, cols):
        self.rows, self.cols = rows, cols

    def own(self, ref, quarter, first=0, count=None):
        return ref.at[pl.ds(quarter * self.rows + first, count or self.rows), :]

    def part(self, ref, quarter, plane, core, first=0, count=None):
        return ref.at[plane, core, pl.ds(quarter * self.rows + first, count or self.rows), :]

    def planes(self, ref, quarter, core):
        return ref.at[:, core, pl.ds(quarter * self.rows, self.rows), :]

    def whole(self, ref, plane, core):
        return ref.at[plane, core]


def gather_kernel(kinds, planes, *refs):
    groups = len(kinds)
    ins, refs = refs[:groups], refs[groups:]
    rows_in, refs = refs[:2], refs[2:]
    outs, refs = refs[:groups], refs[groups:]
    rows_out, refs = refs[:2], refs[2:]
    own_sem, z_send, z_recv, x_send, x_recv, y_send, y_recv, dx_send, dx_recv, dy_send, dy_recv = refs[:11]
    c_send, c_recv, r_own, r_send, r_recv = refs[11:]
    here = Peers(planes)
    me, plane, core = here.seq, here.plane, here.core
    here.meet()
    started, local = [], []

    def send(source, target, send_sem, recv_sem, device):
        copy = remote(source, target, send_sem, recv_sem, device)
        copy.start()
        started.append(copy)
        return copy

    for item in range(2):
        to = rows_out[item].at[me]
        send(rows_in[item], to, r_send.at[item, 0], r_recv.at[item, 0], here.to_x)
        send(rows_in[item], to, r_send.at[item, 1], r_recv.at[item, 1], here.to_y)
    for g, kind in enumerate(kinds):
        for k in range(1, planes):
            send(
                kind.own(ins[g], me), kind.part(outs[g], me, plane, core),
                z_send.at[g, k - 1], z_recv.at[g, k - 1], here.at_plane(here.ahead(k)),
            )
    for g, kind in enumerate(kinds):
        send(ins[g], kind.whole(outs[g], plane, core), c_send.at[g, 0], c_recv.at[g, 0], here.partner)
    for item in range(2):
        copy = pltpu.make_async_copy(rows_in[item], rows_out[item].at[me], r_own.at[item])
        copy.start()
        local.append(copy)
    for g, kind in enumerate(kinds):
        copy = pltpu.make_async_copy(ins[g], kind.whole(outs[g], plane, core), own_sem.at[g])
        copy.start()
        local.append(copy)

    def arrived(target, recv_sem):
        pltpu.make_async_copy(target, target, recv_sem).wait()

    half_rows = [ref.shape[0] // 2 for ref in rows_in]
    for item in range(2):
        half = half_rows[item]
        first = rows_out[item].at[here.along_x, pl.ds(0, half), :]
        second = rows_out[item].at[here.along_y, pl.ds(half, half), :]
        arrived(rows_out[item].at[here.along_x], r_recv.at[item, 0])
        send(first, first, r_send.at[item, 2], r_recv.at[item, 2], here.to_y)
        arrived(rows_out[item].at[here.along_y], r_recv.at[item, 1])
        send(second, second, r_send.at[item, 3], r_recv.at[item, 3], here.to_x)

    def from_plane(g, k):
        kind = kinds[g]
        behind = here.ahead(planes - k)
        chunk = kind.part(outs[g], me, behind, core)
        arrived(chunk, z_recv.at[g, k - 1])
        send(chunk, chunk, x_send.at[g, k - 1], x_recv.at[g, k - 1], here.to_x)
        send(chunk, chunk, y_send.at[g, k - 1], y_recv.at[g, k - 1], here.to_y)

    def from_sides(g, k):
        kind = kinds[g]
        behind = here.ahead(planes - k)
        half = kind.rows // 2
        arrived(kind.part(outs[g], here.along_x, behind, core), x_recv.at[g, k - 1])
        first = kind.part(outs[g], here.along_x, behind, core, 0, half)
        send(first, first, dy_send.at[g, k - 1], dy_recv.at[g, k - 1], here.to_y)
        arrived(kind.part(outs[g], here.along_y, behind, core), y_recv.at[g, k - 1])
        second = kind.part(outs[g], here.along_y, behind, core, half, half)
        send(second, second, dx_send.at[g, k - 1], dx_recv.at[g, k - 1], here.to_x)

    def from_corner(g, k):
        kind = kinds[g]
        behind = here.ahead(planes - k)
        half = kind.rows // 2
        arrived(kind.part(outs[g], here.corner, behind, core, 0, half), dy_recv.at[g, k - 1])
        arrived(kind.part(outs[g], here.corner, behind, core, half, half), dx_recv.at[g, k - 1])
        whole = kind.whole(outs[g], behind, core)
        send(whole, whole, c_send.at[g, k], c_recv.at[g, k], here.partner)

    for step in range(groups + 2):
        for k in range(1, planes):
            if step < groups:
                from_plane(step, k)
            if 0 <= step - 1 < groups:
                from_sides(step - 1, k)
            if 0 <= step - 2 < groups:
                from_corner(step - 2, k)
    for item in range(2):
        half = half_rows[item]
        arrived(rows_out[item].at[here.corner, pl.ds(0, half), :], r_recv.at[item, 2])
        arrived(rows_out[item].at[here.corner, pl.ds(half, half), :], r_recv.at[item, 3])
    for g, kind in enumerate(kinds):
        arrived(kind.whole(outs[g], plane, 1 - core), c_recv.at[g, 0])
        for k in range(1, planes):
            arrived(kind.whole(outs[g], here.ahead(planes - k), 1 - core), c_recv.at[g, k])
    for copy in started:
        copy.wait_send()
    for copy in local:
        copy.wait()


def full_shapes(kinds, planes, cores=2):
    shapes = []
    for kind in kinds:
        if isinstance(kind, Stack):
            shapes.append((4, planes, cores, kind.rows, kind.cols))
        elif isinstance(kind, Wide):
            shapes.append((planes, cores, kind.rows, 4 * kind.cols))
        else:
            shapes.append((planes, cores, 4 * kind.rows, kind.cols))
    return shapes


ANYWHERE = pl.BlockSpec(memory_space=pl.ANY)
DMA = pltpu.SemaphoreType.DMA


def make_kinds(shards):
    square, wide, down = shards[0], shards[8], shards[10]
    stack = Stack(*square.shape)
    band = Wide(wide.shape[0], wide.shape[1] // 4)
    tall = Tall(down.shape[0] // 4, down.shape[1])
    return [stack, stack, band, band, tall]


def kernels_fit(shards):
    kinds = make_kinds(shards)
    return (
        lax.axis_size("seq") == 4
        and lax.axis_size("fsdp") == 8
        and all(kind.rows % 32 == 0 and kind.cols % 128 == 0 for kind in kinds)
    )


def gather_plain(shards, tokens, encoded):
    full = [lax.all_gather(shard, "fsdp", axis=0, tiled=True) for shard in shards]
    return (
        full,
        lax.all_gather(tokens, "seq", axis=0, tiled=True),
        lax.all_gather(encoded, "seq", axis=0, tiled=True),
    )


def gather_all(shards, tokens, encoded):
    if not kernels_fit(shards):
        return gather_plain(shards, tokens, encoded)
    kinds = make_kinds(shards)
    planes = lax.axis_size("fsdp") // 2
    groups = len(kinds)
    ins = [jnp.stack(shards[:4]), jnp.stack(shards[4:8]), *shards[8:], tokens, encoded]
    shapes = full_shapes(kinds, planes) + [(4,) + tokens.shape, (4,) + encoded.shape]
    steps = planes - 1
    outs = pl.pallas_call(
        functools.partial(gather_kernel, kinds, planes),
        in_specs=[ANYWHERE] * len(ins),
        out_specs=[ANYWHERE] * len(shapes),
        out_shape=[shaped(shape, jnp.bfloat16) for shape in shapes],
        scratch_shapes=[DMA((groups,))]
        + [DMA((groups, steps))] * 10
        + [DMA((groups, steps + 1))] * 2
        + [DMA((2,)), DMA((2, 4)), DMA((2, 4))],
        compiler_params=pltpu.CompilerParams(collective_id=0, has_side_effects=True),
        name="gather_all",
    )(*ins)
    one, two, gate, up, down, tokens_all, encoded_all = outs
    width = shards[0].shape[1]
    one = one.reshape(4, -1, width)
    two = two.reshape(4, -1, width)
    full = [one[m] for m in range(4)] + [two[m] for m in range(4)]
    full += [gate.reshape(-1, gate.shape[-1]), up.reshape(-1, up.shape[-1]), down.reshape(-1, width)]
    return full, tokens_all.reshape(-1, width), encoded_all.reshape(-1, width)


def add_low(target, *terms):
    total = target[...].astype(jnp.float32)
    for term in terms:
        total = total + term[...].astype(jnp.float32)
    target[...] = total.astype(jnp.bfloat16)


def reduce_kernel(kinds, planes, *refs):
    groups = len(kinds)
    parts, refs = refs[:groups], refs[groups:]
    row_parts, refs = refs[:2], refs[2:]
    small_ref, refs = refs[0], refs[1:]
    outs, refs = refs[:groups], refs[groups:]
    row_outs, refs = refs[:2], refs[2:]
    small_out, refs = refs[0], refs[1:]
    mine, refs = refs[:groups], refs[groups:]
    other, refs = refs[:groups], refs[groups:]
    side_x, refs = refs[:groups], refs[groups:]
    side_y, refs = refs[:groups], refs[groups:]
    last, refs = refs[:groups], refs[groups:]
    from_z, refs = refs[:groups], refs[groups:]
    final, refs = refs[:groups], refs[groups:]
    row_got, refs = refs[:2], refs[2:]
    small_core, small_seq, small_plane = refs[:3]
    (l_sem, c_send, c_recv, a_send, a_recv, b_send, b_recv, z_send, z_recv, g_send, g_recv,
     rl_sem, r_send, r_recv, s_send, s_recv) = refs[3:]
    here = Peers(planes)
    me, plane, core = here.seq, here.plane, here.core
    lower = planes // 2
    here.meet()
    started = []

    def send(source, target, send_sem, recv_sem, device):
        copy = remote(source, target, send_sem, recv_sem, device)
        copy.start()
        started.append(copy)

    def arrived(target, recv_sem):
        pltpu.make_async_copy(target, target, recv_sem).wait()

    for g, kind in enumerate(kinds):
        for q in range(4):
            send(
                kind.planes(parts[g], q, 1 - core), other[g].at[q],
                c_send.at[g, q], c_recv.at[g, q], here.partner,
            )
            pltpu.make_async_copy(
                kind.planes(parts[g], q, core), mine[g].at[q], l_sem.at[g, q]
            ).start()
    send(small_ref, small_core.at[1], s_send.at[0], s_recv.at[0], here.partner)
    for item in range(2):
        for k, (quarter, device) in enumerate(
            ((here.along_x, here.to_x), (here.along_y, here.to_y), (here.corner, here.to_corner))
        ):
            send(
                row_parts[item].at[quarter], row_got[item].at[k],
                r_send.at[item, k], r_recv.at[item, k], device,
            )
        pltpu.make_async_copy(row_parts[item].at[me], row_got[item].at[3], rl_sem.at[item]).start()

    def pair_sum(g):
        for q in range(4):
            arrived(other[g].at[q], c_recv.at[g, q])
            pltpu.make_async_copy(
                kinds[g].planes(parts[g], q, core), mine[g].at[q], l_sem.at[g, q]
            ).wait()

        @pl.loop(0, 4)
        def _(q):
            @pl.loop(0, planes)
            def _(z):
                add_low(mine[g].at[q, z], other[g].at[q, z])

        low, high = pl.ds(0, lower), pl.ds(lower, planes - lower)
        for n, quarter in enumerate((here.along_x, here.corner)):
            send(mine[g].at[quarter, low], side_x[g].at[n], a_send.at[g, n], a_recv.at[g, n], here.to_x)
        for n, quarter in enumerate((here.along_y, here.corner)):
            send(
                mine[g].at[quarter, high], side_y[g].at[n],
                a_send.at[g, 2 + n], a_recv.at[g, 2 + n], here.to_y,
            )

    def first_side(g):
        for n in range(2):
            arrived(side_x[g].at[n], a_recv.at[g, n])
            arrived(side_y[g].at[n], a_recv.at[g, 2 + n])

        @pl.loop(0, lower)
        def _(z):
            add_low(mine[g].at[here.along_y, z], side_x[g].at[1, z])
            add_low(mine[g].at[here.along_x, lower + z], side_y[g].at[1, z])

        send(
            mine[g].at[here.along_y, pl.ds(0, lower)], last[g].at[0],
            b_send.at[g, 0], b_recv.at[g, 0], here.to_y,
        )
        send(
            mine[g].at[here.along_x, pl.ds(lower, lower)], last[g].at[1],
            b_send.at[g, 1], b_recv.at[g, 1], here.to_x,
        )

    def second_side(g):
        arrived(last[g].at[0], b_recv.at[g, 0])
        arrived(last[g].at[1], b_recv.at[g, 1])

        @pl.loop(0, lower)
        def _(z):
            add_low(mine[g].at[me, z], side_x[g].at[0, z], last[g].at[0, z])
            add_low(mine[g].at[me, lower + z], side_y[g].at[0, z], last[g].at[1, z])

        for k in range(1, planes):
            to = here.ahead(k)
            send(
                mine[g].at[me, to], from_z[g].at[k - 1],
                z_send.at[g, k - 1], z_recv.at[g, k - 1], here.at_plane(to),
            )

    def along_planes(g):
        for k in range(1, planes):
            arrived(from_z[g].at[k - 1], z_recv.at[g, k - 1])
        total = mine[g][me, plane].astype(jnp.float32)
        for k in range(1, planes):
            total = total + from_z[g][k - 1].astype(jnp.float32)
        final[g][me] = total.astype(jnp.bfloat16)
        chunk = final[g].at[me]
        send(chunk, chunk, g_send.at[g, 0], g_recv.at[g, 0], here.to_x)
        send(chunk, chunk, g_send.at[g, 1], g_recv.at[g, 1], here.to_y)

    def spread(g):
        half = kinds[g].rows // 2
        arrived(final[g].at[here.along_x], g_recv.at[g, 0])
        first = final[g].at[here.along_x, pl.ds(0, half), :]
        send(first, first, g_send.at[g, 2], g_recv.at[g, 2], here.to_y)
        arrived(final[g].at[here.along_y], g_recv.at[g, 1])
        second = final[g].at[here.along_y, pl.ds(half, half), :]
        send(second, second, g_send.at[g, 3], g_recv.at[g, 3], here.to_x)

    def finish(g):
        kind = kinds[g]
        half = kind.rows // 2
        arrived(final[g].at[here.corner, pl.ds(0, half), :], g_recv.at[g, 2])
        arrived(final[g].at[here.corner, pl.ds(half, half), :], g_recv.at[g, 3])
        for q in range(4):
            if isinstance(kind, Stack):
                outs[g][q] = final[g][q]
            elif isinstance(kind, Wide):
                outs[g][:, q * kind.cols : (q + 1) * kind.cols] = final[g][q]
            else:
                outs[g][q * kind.rows : (q + 1) * kind.rows, :] = final[g][q]

    def rows_sum(item):
        for k in range(3):
            arrived(row_got[item].at[k], r_recv.at[item, k])
        pltpu.make_async_copy(row_parts[item].at[me], row_got[item].at[3], rl_sem.at[item]).wait()
        step = 64

        @pl.loop(0, row_got[item].shape[1] // step)
        def _(n):
            rows = pl.ds(pl.multiple_of(n * step, step), step)
            total = row_got[item][3, rows, :].astype(jnp.float32)
            for k in range(3):
                total = total + row_got[item][k, rows, :].astype(jnp.float32)
            row_outs[item][rows, :] = total

    def small_pair():
        arrived(small_core.at[1], s_recv.at[0])
        small_seq[me] = small_ref[...] + small_core[1]
        for k, device in enumerate((here.to_x, here.to_y, here.to_corner)):
            send(small_seq.at[me], small_seq.at[me], s_send.at[1 + k], s_recv.at[1 + k], device)

    def small_square():
        for k, quarter in enumerate((here.along_x, here.along_y, here.corner)):
            arrived(small_seq.at[quarter], s_recv.at[1 + k])
        small_plane[plane] = (small_seq[0] + small_seq[1]) + (small_seq[2] + small_seq[3])
        for k in range(1, planes):
            send(
                small_plane.at[plane], small_plane.at[plane],
                s_send.at[3 + k], s_recv.at[3 + k], here.at_plane(here.ahead(k)),
            )

    def small_end():
        for k in range(1, planes):
            arrived(small_plane.at[here.ahead(planes - k)], s_recv.at[3 + k])
        total = small_plane[0]
        for k in range(1, planes):
            total = total + small_plane[k]
        small_out[...] = total

    small_stages = [small_pair, small_square, small_end]
    stages = [pair_sum, first_side, second_side, along_planes, spread, finish]
    for step in range(groups + len(stages) - 1):
        for depth, stage in enumerate(stages):
            if 0 <= step - depth < groups:
                stage(step - depth)
        if step < 3:
            small_stages[step]()
        if 1 <= step < 3:
            rows_sum(step - 1)
    for copy in started:
        copy.wait_send()


def reduce_plain(grads, token_part, enc_part, small):
    def sums(value):
        return lax.psum_scatter(value.astype(jnp.float32), "seq", scatter_dimension=0, tiled=True)

    reduced = [
        lax.psum(
            lax.psum_scatter(grad.astype(jnp.float32), "fsdp", scatter_dimension=0, tiled=True), "seq"
        )
        for grad in grads
    ]
    return reduced, sums(token_part), sums(enc_part), lax.psum(small, ("seq", "fsdp"))


def reduce_all(shards, grads, token_part, enc_part, small):
    if not kernels_fit(shards):
        return reduce_plain(grads, token_part, enc_part, small)
    kinds = make_kinds(shards)
    planes = lax.axis_size("fsdp") // 2
    lower = planes // 2
    groups = len(kinds)
    width = token_part.shape[1]
    order = [2, 3, 4, 1, 0]
    kinds = [kinds[n] for n in order]
    shapes = full_shapes(kinds, planes)
    whole = [jnp.stack(grads[:4]), jnp.stack(grads[4:8]), *grads[8:]]
    parts = [whole[n].reshape(shape) for n, shape in zip(order, shapes)]
    rows = [token_part.reshape(4, -1, width), enc_part.reshape(4, -1, width)]
    own = [stack if stack.ndim == 2 else stack for stack in (jnp.stack(shards[:4]), jnp.stack(shards[4:8]), *shards[8:])]
    low = jnp.bfloat16
    in_vmem = pl.BlockSpec(memory_space=pltpu.VMEM)

    def chunks(*lead):
        return [pltpu.VMEM(lead + (kind.rows, kind.cols), low) for kind in kinds]

    outs = pl.pallas_call(
        functools.partial(reduce_kernel, kinds, planes),
        in_specs=[ANYWHERE] * (groups + 2) + [in_vmem],
        out_specs=[in_vmem] * (groups + 3),
        out_shape=[shaped(own[n].shape, low) for n in order]
        + [shaped(row.shape[1:], jnp.float32) for row in rows]
        + [shaped(small.shape, jnp.float32)],
        scratch_shapes=chunks(4, planes)
        + chunks(4, planes)
        + chunks(2, lower)
        + chunks(2, lower)
        + chunks(2, lower)
        + chunks(planes - 1)
        + chunks(4)
        + [pltpu.VMEM((4,) + row.shape[1:], low) for row in rows]
        + [
            pltpu.VMEM((2,) + small.shape, jnp.float32),
            pltpu.VMEM((4,) + small.shape, jnp.float32),
            pltpu.VMEM((planes,) + small.shape, jnp.float32),
        ]
        + [DMA((groups, 4))] * 5
        + [DMA((groups, 2))] * 2
        + [DMA((groups, planes - 1))] * 2
        + [DMA((groups, 4))] * 2
        + [DMA((2,))]
        + [DMA((2, 3))] * 2
        + [DMA((3 + planes,))] * 2,
        compiler_params=pltpu.CompilerParams(
            collective_id=1, has_side_effects=True, vmem_limit_bytes=62 * 1024 * 1024
        ),
        name="reduce_all",
    )(*parts, *rows, small)
    got = dict(zip(order, outs[:groups]))
    reduced = [got[0][m] for m in range(4)] + [got[1][m] for m in range(4)] + [got[2], got[3], got[4]]
    return [value.astype(jnp.float32) for value in reduced], outs[groups], outs[groups + 1], outs[groups + 2]


def local(
    tokens, encoded, lengths, cotangent, gain_self, gain_cross, gain_ff, bucket_table,
    self_query, self_key, self_value, self_out, cross_query, cross_key, cross_value, cross_out,
    ff_gate, ff_up, ff_down,
):
    rows_here = tokens.shape[1]
    seq_place = lax.axis_index("seq")
    length = lengths[0]
    bf16, f32 = jnp.bfloat16, jnp.float32
    gain_one = gain_self.astype(f32)
    gain_two = gain_cross.astype(f32)
    gain_three = gain_ff.astype(f32)
    shards = (
        self_query, self_key, self_value, self_out, cross_query, cross_key, cross_value, cross_out,
        ff_gate, ff_up, ff_down,
    )
    weights, tokens_all, enc_all = gather_all(shards, tokens[0], encoded[0])
    (w_query, w_key, w_value, w_sout, w_cquery, w_ckey, w_cvalue, w_cout, w_gate, w_up, w_down) = weights
    one_hot = (
        bucket_ids(BLOCK)[:, None] == jnp.arange(BUCKETS, dtype=jnp.int32)[None, :]
    ).astype(bf16)
    profile = inner_rows(bucket_table, one_hot.T).reshape(PAIRS, 2, BLOCK)
    place = jnp.stack([seq_place.astype(jnp.int32), length])

    source = tokens[0].astype(f32)
    normed_all = rms_scale(tokens_all.astype(f32), gain_one).astype(bf16)
    normed_one = rms_scale(source, gain_one).astype(bf16)
    queries = product(normed_one, w_query).astype(bf16)
    keys = product(normed_all, w_key).astype(bf16)
    values = product(normed_all, w_value).astype(bf16)
    mixed_self, mixed_self_turned, log_self = self_forward(place, profile, queries, keys, values)
    hidden_one = source + product(mixed_self, w_sout)
    normed_two = rms_scale(hidden_one, gain_two).astype(bf16)
    cqueries = product(normed_two, w_cquery).astype(bf16)
    ckeys = product(enc_all, w_ckey).astype(bf16)
    cvalues = product(enc_all, w_cvalue).astype(bf16)
    mixed_cross, mixed_cross_turned, log_cross = cross_forward(cqueries, ckeys, cvalues)
    hidden_two = hidden_one + product(mixed_cross, w_cout)
    normed_three = rms_scale(hidden_two, gain_three).astype(bf16)
    gate = product(normed_three, w_gate)
    up = product(normed_three, w_up)

    def gated(gate_rows, up_rows):
        return jax.nn.gelu(gate_rows, approximate=True) * up_rows

    activated_f, pull_gate = jax.vjp(gated, gate, up)
    activated = activated_f.astype(bf16)
    slot_ids = seq_place * rows_here + jnp.arange(rows_here, dtype=jnp.int32)
    valid = (slot_ids < length).astype(f32)[:, None]
    result = (valid * (hidden_two + product(activated, w_down))).astype(bf16)

    grad_result = valid * cotangent[0].astype(f32)
    branch_ff = grad_result.astype(bf16)
    grad_gate_f, grad_up_f = pull_gate(outer_rows(branch_ff, w_down))
    grad_gate = grad_gate_f.astype(bf16)
    grad_up = grad_up_f.astype(bf16)
    g_down = inner_rows(activated, branch_ff).astype(bf16)
    g_gate = inner_rows(normed_three, grad_gate).astype(bf16)
    g_up = inner_rows(normed_three, grad_up).astype(bf16)
    grad_three, grad_gain_three = norm_back(
        hidden_two, gain_three, outer_rows(grad_gate, w_gate) + outer_rows(grad_up, w_up)
    )
    grad_two = grad_result + grad_three
    branch_cross = grad_two.astype(bf16)
    g_cout = inner_rows(mixed_cross, branch_cross).astype(bf16)
    grad_mixed_cross = outer_rows(branch_cross, w_cout).astype(bf16)
    grad_cq, grad_ck, grad_cv = cross_backward(
        cqueries, ckeys, cvalues, grad_mixed_cross, mixed_cross_turned, log_cross
    )
    g_cquery = inner_rows(normed_two, grad_cq).astype(bf16)
    g_ckey = inner_rows(enc_all, grad_ck).astype(bf16)
    g_cvalue = inner_rows(enc_all, grad_cv).astype(bf16)
    enc_part = (outer_rows(grad_ck, w_ckey) + outer_rows(grad_cv, w_cvalue)).astype(bf16)
    grad_two_back, grad_gain_two = norm_back(hidden_one, gain_two, outer_rows(grad_cq, w_cquery))
    grad_one = grad_two + grad_two_back
    branch_self = grad_one.astype(bf16)
    g_sout = inner_rows(mixed_self, branch_self).astype(bf16)
    grad_mixed_self = outer_rows(branch_self, w_sout).astype(bf16)
    grad_q, grad_k, grad_v, near_part, far_part = self_backward(
        place, profile, queries, keys, values, grad_mixed_self, mixed_self_turned, log_self
    )
    g_query = inner_rows(normed_one, grad_q).astype(bf16)
    g_key = inner_rows(normed_all, grad_k).astype(bf16)
    g_value = inner_rows(normed_all, grad_v).astype(bf16)
    token_part = (outer_rows(grad_k, w_key) + outer_rows(grad_v, w_value)).astype(bf16)
    query_part = outer_rows(grad_q, w_query)

    near_rows = near_part.reshape(HEADS, BLOCK)
    far_rows = jnp.sum(far_part, axis=-1).reshape(HEADS)
    table_part = lax.dot_general(
        one_hot.astype(f32), near_rows, (((0,), (1,)), ((), ())),
        precision=lax.Precision.HIGHEST, preferred_element_type=f32,
    )
    table_part = table_part.at[BUCKETS - 1].add(far_rows)

    hat_all = rms_scale(tokens_all.astype(f32), jnp.ones_like(gain_one))
    hat_one = rms_scale(source, jnp.ones_like(gain_one))
    grad_gain_one = jnp.sum(token_part.astype(f32) * hat_all, axis=0) + jnp.sum(
        query_part * hat_one, axis=0
    )
    table_row = jnp.zeros((gain_one.shape[0],), f32).at[: BUCKETS * HEADS].set(table_part.reshape(-1))
    small = jnp.stack([grad_gain_one, grad_gain_two, grad_gain_three, table_row] + [jnp.zeros_like(gain_one)] * 4)
    reduced, token_sum, enc_sum, small = reduce_all(
        shards,
        (g_query, g_key, g_value, g_sout, g_cquery, g_ckey, g_cvalue, g_cout, g_gate, g_up, g_down),
        token_part, enc_part, small,
    )
    grad_zero, _ = norm_back(source, gain_one, query_part + token_sum)
    grad_tokens = grad_one + grad_zero
    table_sum = small[3, : BUCKETS * HEADS].reshape(BUCKETS, HEADS)
    small = (small[0], small[1], small[2], table_sum)
    return (result[None], grad_tokens[None], enc_sum[None], *small, *reduced)


def solution(mesh):
    rows3 = P("fsdp", "seq", None)
    rows2 = P("fsdp", None)
    return jax.shard_map(
        local,
        mesh=mesh,
        in_specs=(rows3, rows3, P("fsdp"), rows3, P(), P(), P(), P(), *([rows2] * 11)),
        out_specs=(rows3, rows3, rows3, P(), P(), P(), P(), *([rows2] * 11)),
        check_vma=False,
    )
```

time: 1560 us -> 420 us (0.27)
  waiting for transfers between devices: 735 us -> 0 us
  local copies, waits for them, and re-layouts: 381 us -> 19.2 us
  Pallas kernels: 0 us -> 308 us
  blocking collectives: 165 us -> 0 us
  matrix products: 118 us -> 64.3 us
  starting transfers between devices: 46.8 us -> 0 us
  other arithmetic: 64.8 us -> 21.4 us
  loops' own time: 26.2 us -> 0 us
    reduce_scatter x11 -> x0, waiting for transfers between devices: 607 us -> none  [the longest x1 109 us: local(): lax.psum_scatter(arranged[8], ('seq', 'fsdp'), scatter_dimension=0, tiled...]
    pallas_call x0 -> x6, Pallas kernels: none -> 308 us  [the longest x1 169 us: reduce_all(): pl.pallas_call(functools.partial(reduce_kernel, kinds, planes), in_specs=...]
    while x118 -> x0, local copies, waits for them, and re-layouts: 155 us -> none
    all_gather x11 -> x0, blocking collectives: 98.9 us -> none  [the longest x1 10.1 us: local(): lax.all_gather(spread[8].astype(jnp.bfloat16), 'seq', axis=0, tiled=True)]
    reshape x10 -> x4, local copies, waits for them, and re-layouts: 88.5 us -> 1.35 us  [the longest x1 0.72 us: local(): near_rows = near_part.reshape(HEADS, BLOCK)]
    all_gather x11 -> x0, waiting for transfers between devices: 75.4 us -> none  [the longest x1 22.6 us: local(): lax.all_gather(ff_down, 'fsdp', axis=0, tiled=True)]
    dot_general x52 -> x23, matrix products: 111 us -> 49.1 us  [the longest x11 25.6 us: outer_rows(): lax.dot_general(left, right, (((1,), (1,)), ((), ())), preferred_element_...]
    all_to_all x13 -> x0, starting transfers between devices: 46 us -> none  [the longest x1 3.78 us: local(): lax.all_to_all(query_local, 'seq', split_axis=1, concat_axis=0, tiled=True)]
  transfers between devices with their start and end apart: 35 -> 0, of which waited for: 22 -> 0; matrix products, arithmetic and copies ran while one was open for 34% -> 0% of each run, Pallas kernels for 0% -> 0%
where the time goes in v1:
time: 420 us; the launch traced here: 415 us
  Pallas kernels  308 us (73%)
  matrix products  64.3 us (15%)
  other arithmetic  21.4 us (5%)
  local copies, waits for them, and re-layouts  19.2 us (5%)
    pallas_call x1, Pallas kernels, reduce_all(): pl.pallas_call(functools.partial(reduce_kernel, kinds, planes), in_specs=...  169 us
    pallas_call x1, Pallas kernels, gather_all(): pl.pallas_call(functools.partial(gather_kernel, kinds, planes), in_specs=...  97.5 us
    dot_general x11, matrix products, outer_rows(): lax.dot_general(left, right, (((1,), (1,)), ((), ())), preferred_element_...  25.6 us
    dot_general x11, matrix products, product(): return jnp.dot(left, right, preferred_element_type=jnp.float32)  23.3 us
    dot_general x12, matrix products, inner_rows(): lax.dot_general(left, right, (((0,), (0,)), ((), ())), preferred_element_...  15.3 us
    pallas_call x1, Pallas kernels, self_backward(): pl.pallas_call(self_backward_kernel, grid=(PAIRS,), in_specs=[SCALARS, he...  12.8 us
    pallas_call x1, Pallas kernels, cross_backward(): pl.pallas_call(cross_backward_kernel, grid=(PAIRS,), in_specs=[pair_block...  9.89 us
    pallas_call x1, Pallas kernels, self_forward(): pl.pallas_call(self_forward_kernel, grid=(PAIRS,), in_specs=[SCALARS, hea...  9.54 us

profile of v1, /device:TPU:0, one launch (start us, length us, event | category | flops | bytes accessed | tf_op | source)
XLA Modules:
  0.0 415.2 jit_solution(210999333240373778)
XLA Ops:
  0.7 2.0 pad_maximum_fusion.2.refs_0_
  2.7 2.0 pad_maximum_fusion.3.refs_1_
  4.7 97.5 %gather_all.1 = (bf16[4,4,2,96,768]{4,3,2,1,0:T(8,128)(2,1)}, bf16[4,4,2,96,768]{4,3,2,1,0:T(8,128)(2,1)}, bf16[4,2,96,2048]{3,2,1,0:T(8,128)(2,1)}, bf16[4,2,96...) custom-call(bf16[4,96,768]{2,1,0:T(8,128)(2,1)} %pad_maximum_fusion., ...), custom_call_target="tpu_custom_call" | custom-call | tf_op jit(solution)/shard_map/gather_all/pallas_call | solution.py:650
  102.2 1.9 multiply_reduce_fusion.1
  104.6 6.7 %fusion.78 = (bf16[1,4,2,96,768]{4,3,2,1,0:T(8,128)(2,1)}, bf16[1,4,2,96,768]{4,3,2,1,0:T(8,128)(2,1)}, bf16[1,4,2,96,768]{4,3,2,1,0:T(8,128)(2,1)}, bf16[1,4,2,...) fusion(bf16[4,4,2,96,768]{4,3,2,1,0:T(8,128)(2,1)} %get-tuple-e, ...), kind=kLoop, calls=%fused_computation.173 | loop fusion | bytes 18874368 | tf_op jit(solution)/shard_map/slice | solution.py:666
  111.3 2.6 convolution_convert_fusion.3.v_ref
  113.9 2.6 convolution_convert_fusion.4.k_ref
  116.6 1.3 convolution_convert_fusion.18.q_ref
  120.0 9.5 %self_forward.1 = (bf16[256,768]{1,0:T(8,128)(2,1)}, f32[768,256]{1,0:T(8,128)}, f32[6,2,256]{2,1,0:T(2,128)}) custom-call(s32[2]{0:T(128)} %pad_add_fusion.place_ref, f32[6,2,256]{2,1,0:T(2,128)} %reshape.381.profile_ref, bf16[256,768]{1,0:T(8,128)(2,1)} %convolution_convert_fusion.18.q_ref, bf16[1024,768]{1,0:T(8,128)(2,1)} %convolution_convert_fusion.4.k_ref, ...), custom_call_target="tpu_custom_call" | custom-call | tf_op jit(solution)/shard_map/self_forward/pallas_call | solution.py:318
  129.6 1.7 multiply_reduce_fusion.7
  131.3 1.3 convolution_convert_fusion.17.q_ref
  132.7 1.7 convolution_convert_fusion.13.v_ref
  134.4 1.7 convolution_convert_fusion.14.k_ref
  136.1 8.8 %cross_forward.1 = (bf16[256,768]{1,0:T(8,128)(2,1)}, f32[768,256]{1,0:T(8,128)}, f32[6,2,256]{2,1,0:T(2,128)}) custom-call(bf16[256,768]{1,0:T(8,128)(2,1)} %convolution_convert_fusion.17.q_ref, bf16[512,768]{1,0:T(8,128)(2,1)} %convolution_convert_fusion.14.k_ref, bf16[512,768]{1,0:T(8,128)(2,1)} %convolution_convert_fusion.13.v_ref), custom_call_target="tpu_custom_call" | custom-call | tf_op jit(solution)/shard_map/cross_forward/pallas_call | solution.py:336
  144.9 2.1 multiply_reduce_fusion.6
  147.3 2.4 fusion.81
  149.7 2.3 fusion.80
  152.1 6.7 %multiply_convert_fusion.2 = (bf16[256,2048]{1,0:T(8,128)(2,1)S(1)}, bf16[256,2048]{1,0:T(8,128)(2,1)S(1)}, bf16[256,2048]{1,0:T(8,128)(2,1)}) fusion(f32[256,2048]{1,0:T(8,128)} %fusion.80, f32[256,2048]{1,0:T(8,128)} %fusion.81, bf16[2048,768]{1,0:T(8,128)(2,1)} %bitcast.210, bf16[1,256,768]{2,1,0:T(8,128)(2,1)S(1)} %copy-done.24, ...), kind=kOutput, calls=%fused_computation.20 | convolution fusion | flops 819527680 | bytes 10880000 | tf_op jit(solution)/shard_map/dot_general | solution.py:59
  158.8 1.0 fusion.82
  160.1 1.3 copy-done.4
  161.4 1.2 multiply_reduce_fusion.2
  163.0 1.0 copy-done.10
  163.9 1.3 convolution_convert_fusion.16.g_ref
  165.2 9.9 %cross_backward.1 = (bf16[256,768]{1,0:T(8,128)(2,1)}, bf16[512,768]{1,0:T(8,128)(2,1)}, bf16[512,768]{1,0:T(8,128)(2,1)}) custom-call(bf16[256,768]{1,0:T(8,128)(2,1)} %convolution_convert_fusion.17.q_ref, bf16[512,768]{1,0:T(8,128)(2,1)} %convolution_convert_fusion.14.k_ref, bf16[512,768]{1,0:T(8,128)(2,1)} %convolution_convert_fusion.13.v_ref, ...), custom_call_target="tpu_custom_call" | custom-call | tf_op jit(solution)/shard_map/cross_backward/pallas_call | solution.py:383
  175.1 2.0 multiply_reduce_fusion.3
  178.6 1.3 convolution_convert_fusion.15.g_ref
  179.9 12.8 %self_backward.1 = (bf16[256,768]{1,0:T(8,128)(2,1)}, bf16[1024,768]{1,0:T(8,128)(2,1)}, bf16[1024,768]{1,0:T(8,128)(2,1)}, f32[6,2,256]{2,1,0:T(2,128)}, f32[6,2,256]{2,1,0:T(2,128)}) custom-call(s32[2]{0:T(128)} %pad_add_fusion.place_ref, f32[6,2,256]{2,1,0:T(2,128)} %reshape.381.profile_ref, bf16[256,768]{1,0:T(8,128)(2,1)} %convolution_convert_fusion.18.q_ref, ...), custom_call_target="tpu_custom_call" | custom-call | tf_op jit(solution)/shard_map/self_backward/pallas_call | solution.py:353
  195.1 3.3 fusion.83
  198.5 3.3 multiply_reduce_fusion
  201.7 1.4 fusion.13
  203.8 2.5 fusion.84
  206.3 1.7 add_convert_fusion.1
  208.4 1.5 convolution_convert_fusion.7
  209.9 1.5 convolution_convert_fusion.6
  213.0 2.7 pad_maximum_fusion.1.refs_4_
  219.4 2.4 pad_maximum_fusion.refs_3_
  221.8 2.7 convolution_convert_fusion.1
  224.5 2.7 convolution_convert_fusion.2
  227.2 2.9 convolution_convert_fusion
  230.1 169.5 %reduce_all.1 = (bf16[96,2048]{1,0:T(8,128)(2,1)}, bf16[96,2048]{1,0:T(8,128)(2,1)}, bf16[256,768]{1,0:T(8,128)(2,1)}, bf16[4,96,768]{2,1,0:T(8,128)(2,1)}, bf16...) custom-call(bf16[4,2,96,2048]{3,2,1,0:T(8,128)(2,1)} %bitcast.165, ...), custom_call_target="tpu_custom_call" | custom-call | tf_op jit(solution)/shard_map/reduce_all/pallas_call | solution.py:907
  399.6 2.3 bitcast_convert_fusion.4
  401.9 1.0 bitcast_convert_fusion
  403.5 1.2 fusion.20
  404.7 1.0 convert_element_type.434
  405.6 1.0 convert_element_type.435
  406.6 0.9 convert_element_type.436
  409.0 1.5 slice_reduce_fusion
  410.5 3.7 fusion.9
  (157 shorter events, 16.1 us)
Async XLA Ops:
  0.7 118.5 %copy-start = (bf16[32,12]{0,1:T(8,128)(2,1)S(1)}, bf16[32,12]{0,1:T(8,128)(2,1)}, u32[]{:S(2)}) copy-start(bf16[32,12]{0,1:T(8,128)(2,1)} %param.30) | copy-start | bytes 2308
  4.7 99.4 %copy-start.45 = (bf16[768]{0:T(1024)(128)(2,1)S(1)}, bf16[768]{0:T(1024)(128)(2,1)}, u32[]{:S(2)}) copy-start(bf16[768]{0:T(1024)(128)(2,1)} %param.27) | copy-start | bytes 4612
  102.2 2.0 copy-start.13
  111.2 2.7 copy-start.35
  111.2 2.7 copy-start.37
  111.2 5.4 %copy-start.15 = (bf16[1,4,2,96,768]{4,3,2,1,0:T(8,128)(2,1)}, bf16[1,4,2,96,768]{4,3,2,1,0:T(8,128)(2,1)S(1)}, u32[]{:S(2)}) copy-start(bf16[1,4,2,96,768]{4,3,2,1,0:T(8,128)(2,1)S(1)} %get-tuple-element.175) | copy-start | bytes 3538948
  111.2 18.3 %copy-start.8 = (bf16[1,4,2,96,768]{4,3,2,1,0:T(8,128)(2,1)}, bf16[1,4,2,96,768]{4,3,2,1,0:T(8,128)(2,1)S(1)}, u32[]{:S(2)}) copy-start(bf16[1,4,2,96,768]{4,3,2,1,0:T(8,128)(2,1)S(1)} %get-tuple-element.178) | copy-start | bytes 3538948
  113.9 2.6 copy-start.2
  129.6 1.7 copy-start.46
  129.6 1.7 copy-start.11
  131.2 1.3 copy-start.32
  131.3 1.5 copy-start.51
  132.7 1.7 copy-start.34
  144.9 2.1 copy-start.47
  144.9 2.4 copy-start.3
  147.3 2.4 copy-start.21
  149.7 2.3 copy-start.24
  152.1 6.7 %copy-start.22 = (bf16[4,2,96,2048]{3,2,1,0:T(8,128)(2,1)S(1)}, bf16[4,2,96,2048]{3,2,1,0:T(8,128)(2,1)}, u32[]{:S(2)}) copy-start(bf16[4,2,96,2048]{3,2,1,0:T(8,128)(2,1)} %get-tuple-element.77) | copy-start | bytes 9437188
  158.8 1.3 copy-start.17
  158.8 2.6 copy-start.4
  177.1 1.5 copy-start.9
  195.0 3.4 copy-start.14
  195.1 3.4 copy-start.36
  195.1 3.4 copy-start.48
  198.4 3.3 copy-start.16
  198.4 3.3 copy-start.28
  203.8 2.5 copy-start.33
  203.8 2.5 copy-start.53
  206.3 1.7 copy-start.50
  206.3 2.1 copy-start.55
  208.4 1.5 copy-start.49
  209.9 1.5 copy-start.6
  209.9 1.5 copy-start.27
  213.0 2.7 copy-start.31
  215.7 1.4 copy-start.54
  219.4 2.4 copy-start.18
  221.8 2.7 copy-start.39
  224.5 2.7 copy-start.19
  224.5 2.7 copy-start.26
  399.6 2.3 copy-start.40
  399.6 3.4 copy-start.12
  399.6 3.3 copy-start.23
  401.9 1.6 copy-start.7
  403.5 2.1 copy-start.43
  404.6 1.9 copy-start.42
  404.7 5.8 %copy-start.20 = (bf16[256,2048]{1,0:T(8,128)(2,1)S(1)}, bf16[256,2048]{1,0:T(8,128)(2,1)}, u32[]{:S(2)}) copy-start(bf16[256,2048]{1,0:T(8,128)(2,1)} %get-tuple-element.153) | copy-start | bytes 3145732
  410.5 3.7 copy-start.41
  410.5 4.4 %copy-start.1 = (bf16[32,12]{0,1:T(8,128)(2,1)S(1)}, bf16[32,12]{0,1:T(8,128)(2,1)}, u32[]{:S(2)}) copy-start(bf16[32,12]{0,1:T(8,128)(2,1)} %param.30) | copy-start | bytes 2308
  (8 other events, 8.8 us)

commit v2 on v1

v2 whole, which is shorter than its diff:
```python
import functools
import math

import jax
import jax.numpy as jnp
from jax import lax
from jax.experimental import pallas as pl
from jax.experimental.pallas import tpu as pltpu
from jax.sharding import PartitionSpec as P

HEADS = 12
HEAD = 64
BUCKETS = 32
MAX_DISTANCE = 128
EPSILON = 1e-06
NEGATIVE = -1e30
BLOCK = 256
PAIR = 2 * HEAD
MESH = pl.DeviceIdType.MESH


def thresholds():
    exact_limit = BUCKETS // 2
    return [
        int(math.ceil(exact_limit * (MAX_DISTANCE / exact_limit) ** (number / exact_limit)))
        for number in range(1, exact_limit)
    ]


def bucket_ids(key_count):
    exact_limit = BUCKETS // 2
    offsets = jnp.arange(key_count, dtype=jnp.int32)
    passed = jnp.zeros((key_count,), jnp.int32)
    for border in thresholds():
        passed = passed + (offsets >= border).astype(jnp.int32)
    return jnp.where(offsets < exact_limit, offsets, exact_limit + passed)


def rms_scale(values, gain):
    return values * lax.rsqrt(jnp.mean(values * values, axis=-1, keepdims=True) + EPSILON) * gain


def norm_back(values, gain, grad_normed):
    _, pullback = jax.vjp(rms_scale, values, gain)
    return pullback(grad_normed)


def product(left, right):
    return jnp.dot(left, right, preferred_element_type=jnp.float32)


def inner_rows(left, right):
    return lax.dot_general(
        left, right, (((0,), (0,)), ((), ())), preferred_element_type=jnp.float32
    )


def outer_rows(left, right):
    return lax.dot_general(
        left, right, (((1,), (1,)), ((), ())), preferred_element_type=jnp.float32
    )


def iota(shape, axis):
    return lax.broadcasted_iota(jnp.int32, shape, axis)


def head_rows(value, head):
    place = iota(value.shape, 0) // HEAD
    return jnp.where(place == head, value, jnp.zeros_like(value))


def head_cols(value, head):
    place = iota(value.shape, 1) // HEAD
    return jnp.where(place == head, value, jnp.zeros_like(value))


def skew(profile_row):
    wide = jnp.broadcast_to(profile_row, (BLOCK, BLOCK))
    return pltpu.roll(wide, 0, 1, stride=1, stride_axis=0)


def unskew(tile):
    rows = iota(tile.shape, 0)
    bit = 1
    while bit < BLOCK:
        tile = jnp.where((rows // bit) % 2 == 1, pltpu.roll(tile, BLOCK - bit, 1), tile)
        bit *= 2
    return tile


def fill_pads(pads, length):
    rows = pads.shape[1]
    lanes = iota((BLOCK, PAIR), 1)

    @pl.loop(0, rows // BLOCK)
    def _(n):
        start = pl.multiple_of(n * BLOCK, BLOCK)
        beyond = iota((BLOCK, PAIR), 0) >= length - start
        for head in range(2):
            first = (1 - head) * HEAD
            ones = jnp.where((lanes > first) & (lanes <= first + 3), 1.0, 0.0)
            pads[head, pl.ds(start, BLOCK), :] = jnp.where(
                (lanes == first) & beyond, NEGATIVE, ones
            ).astype(jnp.bfloat16)


def padded(value, pads, head, start):
    own = iota(value.shape, 1) // HEAD == head
    return jnp.where(own, value, pads[head, start : start + value.shape[0], :])


def split_low(value):
    first = value.astype(jnp.bfloat16).astype(jnp.float32)
    rest = value - first
    second = rest.astype(jnp.bfloat16).astype(jnp.float32)
    return first, second, rest - second


def with_terms(turned, head, mask_term, terms):
    place = iota(turned.shape, 0)
    first = (1 - head) * HEAD
    value = jnp.where(place // HEAD == head, turned.astype(jnp.float32), 0.0)
    value = jnp.where(place == first, mask_term, value)
    for n, term in enumerate(terms):
        value = jnp.where(place == first + 1 + n, term, value)
    return value.astype(jnp.bfloat16)


HIDDEN, DIAGONAL, NEAR, FAR = range(4)


def fill_fixed_bias(bias):
    for head in range(2):
        bias[head, HIDDEN] = jnp.full((BLOCK, BLOCK), NEGATIVE, jnp.float32)
        bias[head, FAR] = jnp.zeros((BLOCK, BLOCK), jnp.float32)


def fill_near_bias(bias, profile_ref):
    later = iota((BLOCK, BLOCK), 1) >= iota((BLOCK, BLOCK), 0)
    for head in range(2):
        profile = profile_ref[head : head + 1, :]
        near = skew(profile - profile[:, BLOCK - 1 :])
        bias[head, DIAGONAL] = jnp.where(later, near, NEGATIVE)
        bias[head, NEAR] = jnp.where(later, 0.0, near)


def bias_kind(place, block):
    return jnp.clip(place - block, -1, 2) + 1


def self_forward_pair(place, profile_ref, q_ref, k_ref, v_ref, o_ref, ot_ref, log_ref, pads, bias, s_buf, vt_buf):
    qt = q_ref[...].T
    vt_buf[...] = v_ref[...].T
    fill_near_bias(bias, profile_ref)
    blocks = k_ref.shape[0] // BLOCK
    tops = []
    for head in range(2):
        far = profile_ref[head : head + 1, BLOCK - 1 :]
        queries = with_terms(qt, head, 1.0, (far,))
        top = None
        for block in range(blocks):
            start = block * BLOCK
            keys = padded(k_ref[start : start + BLOCK, :], pads, head, start)
            scores = product(keys, queries) + bias[head, bias_kind(place, block)]
            s_buf[head, start : start + BLOCK, :] = scores
            most = jnp.max(scores, axis=0, keepdims=True)
            top = most if top is None else jnp.maximum(top, most)
        tops.append(top)
    totals = []
    for head in range(2):
        total = None
        for block in range(blocks):
            part = slice(block * BLOCK, (block + 1) * BLOCK)
            raised = jnp.exp(s_buf[head, part, :] - tops[head])
            s_buf[head, part, :] = raised
            amount = jnp.sum(raised, axis=0, keepdims=True)
            total = amount if total is None else total + amount
        totals.append(total)
    for head in range(2):
        rows = slice(head * HEAD, (head + 1) * HEAD)
        scale, mixed = 1.0 / totals[head], None
        for block in range(blocks):
            part = slice(block * BLOCK, (block + 1) * BLOCK)
            soft = (s_buf[head, part, :] * scale).astype(jnp.bfloat16)
            share = product(vt_buf[rows, part], soft)
            mixed = share if mixed is None else mixed + share
        ot_ref[rows, :] = mixed
        log_ref[head : head + 1, :] = tops[head] + jnp.log(totals[head])
    o_ref[...] = ot_ref[...].T.astype(jnp.bfloat16)


def self_forward_kernel(place_ref, profile_ref, q_ref, k_ref, v_ref, o_ref, ot_ref, log_ref, pads, bias, s_buf, vt_buf):
    @pl.when(pl.program_id(0) == 0)
    def _():
        fill_pads(pads, place_ref[1])
        fill_fixed_bias(bias)

    self_forward_pair(
        place_ref[0], profile_ref.at[0], q_ref, k_ref, v_ref, o_ref, ot_ref, log_ref.at[0],
        pads, bias, s_buf, vt_buf,
    )


def cross_forward_pair(q_ref, k_ref, v_ref, o_ref, ot_ref, log_ref):
    qt = q_ref[...].T
    vt = v_ref[...].T
    all_scores = [product(k_ref[...], head_rows(qt, head)) for head in range(2)]
    for head, scores in enumerate(all_scores):
        top = jnp.max(scores, axis=0, keepdims=True)
        raised = jnp.exp(scores - top)
        total = jnp.sum(raised, axis=0, keepdims=True)
        soft = (raised * (1.0 / total)).astype(jnp.bfloat16)
        ot_ref[head * HEAD : (head + 1) * HEAD, :] = product(vt[head * HEAD : (head + 1) * HEAD, :], soft)
        log_ref[head : head + 1, :] = top + jnp.log(total)
    o_ref[...] = ot_ref[...].T.astype(jnp.bfloat16)


def cross_forward_kernel(q_ref, k_ref, v_ref, o_ref, ot_ref, log_ref):
    cross_forward_pair(q_ref, k_ref, v_ref, o_ref, ot_ref, log_ref.at[0])


EXTRA = 16


def backward_pair(
    place, profile_ref, q_ref, k_ref, v_ref, g_ref, ot_ref, log_ref, dq_ref, dk_ref, dv_ref,
    near_ref, far_ref, pads, bias, kt_buf, grad_buf,
):
    q_value = q_ref[...]
    g_value = g_ref[...]
    qt = q_value.T
    gt = g_value.T
    kt = k_ref[...].T
    keys_count = k_ref.shape[0]
    ones = jnp.ones((EXTRA, keys_count), jnp.bfloat16)
    for head in range(2):
        kt_buf[head, 0:HEAD, 0:keys_count] = kt[head * HEAD : (head + 1) * HEAD, :]
        kt_buf[head, HEAD : HEAD + EXTRA, 0:keys_count] = ones
    both_q = jnp.concatenate([head_cols(q_value, 0), head_cols(q_value, 1)], axis=0)
    both_g = jnp.concatenate([head_cols(g_value, 0), head_cols(g_value, 1)], axis=0)
    weighted = gt.astype(jnp.float32) * ot_ref[...]
    if profile_ref is not None:
        fill_near_bias(bias, profile_ref)
    queries, grads_out = [], []
    for head in range(2):
        rows = slice(head * HEAD, (head + 1) * HEAD)
        delta = jnp.sum(weighted[rows, :], axis=0, keepdims=True)
        constant = -log_ref[head : head + 1, :]
        if profile_ref is not None:
            constant = constant + profile_ref[head : head + 1, BLOCK - 1 :]
        queries.append(with_terms(qt, head, 1.0, split_low(constant)))
        grads_out.append(with_terms(gt, head, 0.0, split_low(-delta)))
    sums = [None, None]
    for start in range(0, keys_count, BLOCK):
        k_block = k_ref[start : start + BLOCK, :]
        v_block = v_ref[start : start + BLOCK, :]
        softs, grads = [], []
        for head in range(2):
            scores = product(padded(k_block, pads, head, start), queries[head])
            if profile_ref is not None:
                scores = scores + bias[head, bias_kind(place, start // BLOCK)]
            soft = jnp.exp(scores)
            change = product(padded(v_block, pads, head, start), grads_out[head])
            grad = (soft * change).astype(jnp.bfloat16)
            softs.append(soft.astype(jnp.bfloat16))
            grads.append(grad)
            if profile_ref is not None:
                grad_buf[head, start // BLOCK] = grad
            share = product(kt_buf[head, :, start : start + BLOCK], grad)
            sums[head] = share if sums[head] is None else sums[head] + share
        dv_ref[start : start + BLOCK, :] = product(jnp.concatenate(softs, axis=1), both_g).astype(
            jnp.bfloat16
        )
        dk_ref[start : start + BLOCK, :] = product(jnp.concatenate(grads, axis=1), both_q).astype(
            jnp.bfloat16
        )
    turned = jnp.concatenate([sums[0][0:HEAD, :], sums[1][0:HEAD, :]], axis=0)
    dq_ref[...] = turned.T.astype(jnp.bfloat16)
    if profile_ref is not None:
        later = iota((BLOCK, BLOCK), 1) >= iota((BLOCK, BLOCK), 0)
        for head in range(2):
            diagonal = grad_buf[head, place].astype(jnp.float32)
            before = grad_buf[head, jnp.maximum(place - 1, 0)].astype(jnp.float32)
            before = jnp.where(place >= 1, before, 0.0)
            near = jnp.sum(unskew(jnp.where(later, diagonal, before)), axis=0, keepdims=True)
            near_ref[head : head + 1, :] = near
            far_ref[head : head + 1, :] = sums[head][HEAD : HEAD + 1, :] - near


def self_backward_kernel(
    place_ref, profile_ref, q_ref, k_ref, v_ref, g_ref, ot_ref, log_ref,
    dq_ref, dk_ref, dv_ref, near_ref, far_ref, pads, bias, kt_buf, grad_buf,
):
    @pl.when(pl.program_id(0) == 0)
    def _():
        fill_pads(pads, place_ref[1])
        fill_fixed_bias(bias)

    backward_pair(
        place_ref[0], profile_ref.at[0], q_ref, k_ref, v_ref, g_ref, ot_ref, log_ref.at[0],
        dq_ref, dk_ref, dv_ref, near_ref.at[0], far_ref.at[0], pads, bias, kt_buf, grad_buf,
    )


def cross_backward_kernel(q_ref, k_ref, v_ref, g_ref, ot_ref, log_ref, dq_ref, dk_ref, dv_ref, pads, kt_buf):
    @pl.when(pl.program_id(0) == 0)
    def _():
        fill_pads(pads, pads.shape[1])

    backward_pair(
        None, None, q_ref, k_ref, v_ref, g_ref, ot_ref, log_ref.at[0], dq_ref, dk_ref, dv_ref,
        None, None, pads, None, kt_buf, None,
    )


def forward_scratch(count, rows):
    return [
        pltpu.VMEM((2, count, PAIR), jnp.bfloat16),
        pltpu.VMEM((2, 4, BLOCK, BLOCK), jnp.float32),
        pltpu.VMEM((2, count, rows), jnp.float32),
        pltpu.VMEM((PAIR, count), jnp.bfloat16),
    ]


def backward_scratch(count):
    return [
        pltpu.VMEM((2, count, PAIR), jnp.bfloat16),
        pltpu.VMEM((2, 4, BLOCK, BLOCK), jnp.float32),
        pltpu.VMEM((2, HEAD + EXTRA, count), jnp.bfloat16),
        pltpu.VMEM((2, count // BLOCK, BLOCK, BLOCK), jnp.bfloat16),
    ]


def pair_block(rows):
    return pl.BlockSpec((rows, PAIR), lambda pair: (0, pair))


def turned_block(rows):
    return pl.BlockSpec((PAIR, rows), lambda pair: (pair, 0))


def head_block(width):
    return pl.BlockSpec((1, 2, width), lambda pair: (pair, 0, 0))


SCALARS = pl.BlockSpec(memory_space=pltpu.SMEM)
PAIRS = HEADS // 2


def shaped(shape, dtype):
    return jax.ShapeDtypeStruct(shape, dtype)


def self_forward(place, profile, queries, keys, values):
    rows, width = queries.shape
    count = keys.shape[0]
    return pl.pallas_call(
        self_forward_kernel,
        grid=(PAIRS,),
        in_specs=[SCALARS, head_block(BLOCK), pair_block(rows), pair_block(count), pair_block(count)],
        out_specs=[pair_block(rows), turned_block(rows), head_block(rows)],
        out_shape=[
            shaped((rows, width), jnp.bfloat16),
            shaped((width, rows), jnp.float32),
            shaped((PAIRS, 2, rows), jnp.float32),
        ],
        scratch_shapes=forward_scratch(count, rows),
        name="self_forward",
    )(place, profile, queries, keys, values)


def cross_forward(queries, keys, values):
    rows, width = queries.shape
    count = keys.shape[0]
    return pl.pallas_call(
        cross_forward_kernel,
        grid=(PAIRS,),
        in_specs=[pair_block(rows), pair_block(count), pair_block(count)],
        out_specs=[pair_block(rows), turned_block(rows), head_block(rows)],
        out_shape=[
            shaped((rows, width), jnp.bfloat16),
            shaped((width, rows), jnp.float32),
            shaped((PAIRS, 2, rows), jnp.float32),
        ],
        name="cross_forward",
    )(queries, keys, values)


def self_backward(place, profile, queries, keys, values, grad_mixed, mixed_turned, log_totals):
    rows, width = queries.shape
    count = keys.shape[0]
    return pl.pallas_call(
        self_backward_kernel,
        grid=(PAIRS,),
        in_specs=[
            SCALARS, head_block(BLOCK), pair_block(rows), pair_block(count), pair_block(count),
            pair_block(rows), turned_block(rows), head_block(rows),
        ],
        out_specs=[
            pair_block(rows), pair_block(count), pair_block(count), head_block(BLOCK), head_block(rows),
        ],
        out_shape=[
            shaped((rows, width), jnp.bfloat16),
            shaped((count, width), jnp.bfloat16),
            shaped((count, width), jnp.bfloat16),
            shaped((PAIRS, 2, BLOCK), jnp.float32),
            shaped((PAIRS, 2, rows), jnp.float32),
        ],
        scratch_shapes=backward_scratch(count),
        name="self_backward",
    )(place, profile, queries, keys, values, grad_mixed, mixed_turned, log_totals)


def cross_backward(queries, keys, values, grad_mixed, mixed_turned, log_totals):
    rows, width = queries.shape
    count = keys.shape[0]
    return pl.pallas_call(
        cross_backward_kernel,
        grid=(PAIRS,),
        in_specs=[
            pair_block(rows), pair_block(count), pair_block(count),
            pair_block(rows), turned_block(rows), head_block(rows),
        ],
        out_specs=[pair_block(rows), pair_block(count), pair_block(count)],
        out_shape=[
            shaped((rows, width), jnp.bfloat16),
            shaped((count, width), jnp.bfloat16),
            shaped((count, width), jnp.bfloat16),
        ],
        scratch_shapes=[
            pltpu.VMEM((2, count, PAIR), jnp.bfloat16),
            pltpu.VMEM((2, HEAD + EXTRA, count), jnp.bfloat16),
        ],
        name="cross_backward",
    )(queries, keys, values, grad_mixed, mixed_turned, log_totals)


class Peers:
    def __init__(self, planes):
        self.seq = lax.axis_index("seq")
        fsdp = lax.axis_index("fsdp")
        self.planes = planes
        self.plane = fsdp // 2
        self.core = fsdp % 2
        self.fsdp = fsdp
        self.along_x = self.seq + 1 - 2 * (self.seq % 2)
        self.along_y = (self.seq + 2) % 4
        self.corner = (self.along_x + 2) % 4
        self.partner = (self.seq, fsdp + 1 - 2 * self.core)
        self.to_x = (self.along_x, fsdp)
        self.to_y = (self.along_y, fsdp)
        self.to_corner = (self.corner, fsdp)

    def ahead(self, steps):
        return (self.plane + steps) % self.planes

    def at_plane(self, plane):
        return (self.seq, 2 * plane + self.core)

    def everyone(self):
        return [self.partner, self.to_x, self.to_y, self.to_corner] + [
            self.at_plane(self.ahead(k)) for k in range(1, self.planes)
        ]

    def meet(self):
        barrier = pltpu.get_barrier_semaphore()
        others = self.everyone()
        for other in others:
            pl.semaphore_signal(barrier, inc=1, device_id=other, device_id_type=MESH)
        pl.semaphore_wait(barrier, len(others))


def remote(source, target, send_sem, recv_sem, device):
    return pltpu.make_async_remote_copy(
        src_ref=source, dst_ref=target, send_sem=send_sem, recv_sem=recv_sem,
        device_id=device, device_id_type=MESH,
    )


class Stack:
    def __init__(self, rows, cols):
        self.rows, self.cols = rows, cols

    def own(self, ref, quarter, first=0, count=None):
        return ref.at[quarter, pl.ds(first, count or self.rows), :]

    def part(self, ref, quarter, plane, core, first=0, count=None):
        return ref.at[quarter, plane, core, pl.ds(first, count or self.rows), :]

    def planes(self, ref, quarter, core):
        return ref.at[quarter, :, core]

    def whole(self, ref, plane, core):
        return ref.at[:, plane, core]


class Wide:
    def __init__(self, rows, cols):
        self.rows, self.cols = rows, cols

    def own(self, ref, quarter, first=0, count=None):
        return ref.at[pl.ds(first, count or self.rows), pl.ds(quarter * self.cols, self.cols)]

    def part(self, ref, quarter, plane, core, first=0, count=None):
        return ref.at[
            plane, core, pl.ds(first, count or self.rows), pl.ds(quarter * self.cols, self.cols)
        ]

    def planes(self, ref, quarter, core):
        return ref.at[:, core, :, pl.ds(quarter * self.cols, self.cols)]

    def whole(self, ref, plane, core):
        return ref.at[plane, core]


class Tall:
    def __init__(self, rows, cols):
        self.rows, self.cols = rows, cols

    def own(self, ref, quarter, first=0, count=None):
        return ref.at[pl.ds(quarter * self.rows + first, count or self.rows), :]

    def part(self, ref, quarter, plane, core, first=0, count=None):
        return ref.at[plane, core, pl.ds(quarter * self.rows + first, count or self.rows), :]

    def planes(self, ref, quarter, core):
        return ref.at[:, core, pl.ds(quarter * self.rows, self.rows), :]

    def whole(self, ref, plane, core):
        return ref.at[plane, core]


def full_shapes(kinds, planes, cores=2):
    shapes = []
    for kind in kinds:
        if isinstance(kind, Stack):
            shapes.append((4, planes, cores, kind.rows, kind.cols))
        elif isinstance(kind, Wide):
            shapes.append((planes, cores, kind.rows, 4 * kind.cols))
        else:
            shapes.append((planes, cores, 4 * kind.rows, kind.cols))
    return shapes


ANYWHERE = pl.BlockSpec(memory_space=pl.ANY)
DMA = pltpu.SemaphoreType.DMA


def make_kinds(shards):
    square, wide, down = shards[0], shards[8], shards[10]
    stack = Stack(*square.shape)
    band = Wide(wide.shape[0], wide.shape[1] // 4)
    tall = Tall(down.shape[0] // 4, down.shape[1])
    return [stack, stack, band, band, tall]


def kernels_fit(shards):
    kinds = make_kinds(shards)
    return (
        lax.axis_size("seq") == 4
        and lax.axis_size("fsdp") == 8
        and all(kind.rows % 32 == 0 and kind.cols % 128 == 0 for kind in kinds)
    )


def gather_plain(shards, tokens, encoded):
    full = [lax.all_gather(shard, "fsdp", axis=0, tiled=True) for shard in shards]
    return (
        full,
        lax.all_gather(tokens, "seq", axis=0, tiled=True),
        lax.all_gather(encoded, "seq", axis=0, tiled=True),
    )


def add_low(target, *terms):
    total = target[...].astype(jnp.float32)
    for term in terms:
        total = total + term[...].astype(jnp.float32)
    target[...] = total.astype(jnp.bfloat16)


def reduce_plain(grads, token_part, enc_part, small):
    def sums(value):
        return lax.psum_scatter(value.astype(jnp.float32), "seq", scatter_dimension=0, tiled=True)

    reduced = [
        lax.psum(
            lax.psum_scatter(grad.astype(jnp.float32), "fsdp", scatter_dimension=0, tiled=True), "seq"
        )
        for grad in grads
    ]
    return reduced, sums(token_part), sums(enc_part), lax.psum(small, ("seq", "fsdp"))


def columns(pair):
    return pl.ds(pl.multiple_of(pair * PAIR, PAIR), PAIR)


def tiles(count):
    def run(body):
        @pl.loop(0, count // BLOCK)
        def _(n):
            body(pl.ds(pl.multiple_of(n * BLOCK, BLOCK), BLOCK))

    return run


def times_turned(store, left, weight):
    value = left[...]

    @tiles(weight.shape[0])
    def _(part):
        store(part, outer_rows(value, weight[part, :]))


def times(store, left, weight):
    value = left[...]

    @tiles(weight.shape[1])
    def _(part):
        store(part, product(value, weight[:, part]))


def weight_grad(out, turned, right):
    across = right.shape[1] // BLOCK

    @pl.loop(0, (turned.shape[0] // BLOCK) * across)
    def _(n):
        first = pl.ds(pl.multiple_of((n // across) * BLOCK, BLOCK), BLOCK)
        second = pl.ds(pl.multiple_of((n % across) * BLOCK, BLOCK), BLOCK)
        out[first, second] = product(turned[first, :], right[:, second]).astype(jnp.bfloat16)


def turn(out, source):
    @tiles(source.shape[0])
    def _(part):
        out[:, part] = source[part, :].T


ROW_STEP = 32


def row_steps(count):
    def run(body):
        @pl.loop(0, count // ROW_STEP)
        def _(n):
            body(pl.ds(pl.multiple_of(n * ROW_STEP, ROW_STEP), ROW_STEP))

    return run


def norm_back_rows(values, gain, grad_normed):
    scale = lax.rsqrt(jnp.mean(values * values, axis=-1, keepdims=True) + EPSILON)
    scaled = grad_normed * gain
    along = jnp.mean(values * scaled, axis=-1, keepdims=True)
    grad_values = scale * scaled - values * (scale * scale * scale) * along
    return grad_values, jnp.sum(grad_normed * values * scale, axis=0, keepdims=True)


GATE, UP, DOWN, CROSS, SELF = range(5)


class Space:
    def __init__(self, layout, refs):
        refs = list(refs)
        for name, count in layout.items():
            value = refs.pop(0) if count is None else [refs.pop(0) for _ in range(count)]
            setattr(self, name, value)


def flatten(*tables):
    layout, flat = {}, []
    for table in tables:
        for name, value in table.items():
            many = isinstance(value, list)
            layout[name] = len(value) if many else None
            flat += value if many else [value]
    return layout, flat


class Reduction:
    def __init__(self, kinds, here, r):
        self.kinds, self.here, self.r = kinds, here, r
        self.planes = here.planes
        self.lower = here.planes // 2
        self.started = []
        shape = (4, here.planes, 2, kinds[CROSS].rows, kinds[CROSS].cols)
        self.parts = [
            *r.ffn_parts,
            r.grad_cross.reshape(*shape), r.grad_self.reshape(*shape),
        ]
        self.sums = r.sums

    def send(self, make):
        remote(*make()).start()
        self.started.append(make)

    def arrived(self, target, recv_sem):
        pltpu.make_async_copy(target, target, recv_sem).wait()

    def own_copy(self, g, q):
        stage = (self.r.stage_tall if g == DOWN else self.r.stage_band)
        return pltpu.make_async_copy(
            self.kinds[g].planes(self.parts[g], q, self.here.core), stage.at[q], self.r.own_sem.at[g, q]
        )

    def load_own(self, g):
        for q in range(4):
            self.own_copy(g, q).start()

    def start_pair(self, g):
        r = self.r
        for q in range(4):
            self.send(lambda g=g, q=q: (self.kinds[g].planes(self.parts[g], q, 1 - self.here.core), self.sums[g].at[q],
                r.c_send.at[g, q], r.c_recv.at[g, q], self.here.partner))

    def pair_sum(self, g):
        r, here, sums, planes = self.r, self.here, self.sums[g], self.planes
        for q in range(4):
            self.arrived(sums.at[q], r.c_recv.at[g, q])
            if g <= DOWN:
                self.own_copy(g, q).wait()
        if g <= DOWN:
            stage = r.stage_tall if g == DOWN else r.stage_band

        @pl.loop(0, 4 * planes)
        def _(n):
            q, z = n // planes, n % planes
            own = stage.at[q, z] if g <= DOWN else self.parts[g].at[q, z, here.core]
            add_low(sums.at[q, z], own)

        if g == GATE:
            self.load_own(UP)
        low, high = pl.ds(0, self.lower), pl.ds(self.lower, planes - self.lower)
        for n, quarter in enumerate((here.along_x, here.corner)):
            self.send(lambda g=g, n=n, quarter=quarter: (sums.at[quarter, low], r.side_x[g].at[n],
                r.a_send.at[g, n], r.a_recv.at[g, n], here.to_x))
        for n, quarter in enumerate((here.along_y, here.corner)):
            self.send(lambda g=g, n=n, quarter=quarter: (sums.at[quarter, high], r.side_y[g].at[n],
                r.a_send.at[g, 2 + n], r.a_recv.at[g, 2 + n], here.to_y))

    def first_side(self, g):
        r, here, sums, lower = self.r, self.here, self.sums[g], self.lower
        side_x, side_y, last = r.side_x[g], r.side_y[g], r.last[g]
        for n in range(2):
            self.arrived(side_x.at[n], r.a_recv.at[g, n])
            self.arrived(side_y.at[n], r.a_recv.at[g, 2 + n])

        @pl.loop(0, lower)
        def _(z):
            add_low(sums.at[here.along_y, z], side_x.at[1, z])
            add_low(sums.at[here.along_x, lower + z], side_y.at[1, z])

        self.send(lambda g=g: (sums.at[here.along_y, pl.ds(0, lower)], last.at[0],
            r.b_send.at[g, 0], r.b_recv.at[g, 0], here.to_y))
        self.send(lambda g=g: (sums.at[here.along_x, pl.ds(lower, lower)], last.at[1],
            r.b_send.at[g, 1], r.b_recv.at[g, 1], here.to_x))

    def second_side(self, g):
        r, here, sums, lower = self.r, self.here, self.sums[g], self.lower
        side_x, side_y, last = r.side_x[g], r.side_y[g], r.last[g]
        self.arrived(last.at[0], r.b_recv.at[g, 0])
        self.arrived(last.at[1], r.b_recv.at[g, 1])

        @pl.loop(0, lower)
        def _(z):
            add_low(sums.at[here.seq, z], side_x.at[0, z], last.at[0, z])
            add_low(sums.at[here.seq, lower + z], side_y.at[0, z], last.at[1, z])

        for k in range(1, self.planes):
            self.send(
                lambda k=k: (
                    sums.at[here.seq, here.ahead(k)], r.from_z[g].at[k - 1],
                    r.z_send.at[g, k - 1], r.z_recv.at[g, k - 1], here.at_plane(here.ahead(k)),
                )
            )

    def along_planes(self, g):
        r, here, sums = self.r, self.here, self.sums[g]
        from_z, final = r.from_z[g], r.final[g]
        for k in range(1, self.planes):
            self.arrived(from_z.at[k - 1], r.z_recv.at[g, k - 1])
        step = 32

        @pl.loop(0, self.kinds[g].rows // step)
        def _(n):
            rows = pl.ds(pl.multiple_of(n * step, step), step)
            total = sums[here.seq, here.plane, rows, :].astype(jnp.float32)
            for k in range(1, self.planes):
                total = total + from_z[k - 1, rows, :].astype(jnp.float32)
            final[here.seq, rows, :] = total.astype(jnp.bfloat16)

        for n, device in enumerate((here.to_x, here.to_y)):
            self.send(
                lambda n=n, device=device: (
                    final.at[here.seq], final.at[here.seq], r.g_send.at[g, n], r.g_recv.at[g, n], device
                )
            )

    def spread(self, g):
        r, here, final = self.r, self.here, self.r.final[g]
        half = self.kinds[g].rows // 2
        turns = ((here.along_x, 0, here.to_y), (here.along_y, half, here.to_x))
        for n, (quarter, first, device) in enumerate(turns):
            self.arrived(final.at[quarter], r.g_recv.at[g, n])

            def make(n=n, quarter=quarter, first=first, device=device):
                chunk = final.at[quarter, pl.ds(first, half), :]
                return chunk, chunk, r.g_send.at[g, 2 + n], r.g_recv.at[g, 2 + n], device

            self.send(make)

    def out_copies(self, g):
        r, kind, final = self.r, self.kinds[g], self.r.final[g]
        out = r.out[g]
        if not isinstance(kind, Wide):
            return [pltpu.make_async_copy(final, out, r.out_sem.at[g, 0])]
        return [
            pltpu.make_async_copy(
                final.at[q], out.at[:, pl.ds(q * kind.cols, kind.cols)], r.out_sem.at[g, q]
            )
            for q in range(4)
        ]

    def finish(self, g):
        r, here, final = self.r, self.here, self.r.final[g]
        half = self.kinds[g].rows // 2
        self.arrived(final.at[here.corner, pl.ds(0, half), :], r.g_recv.at[g, 2])
        self.arrived(final.at[here.corner, pl.ds(half, half), :], r.g_recv.at[g, 3])
        for copy in self.out_copies(g):
            copy.start()

    def end(self):
        for g in range(5):
            for copy in self.out_copies(g):
                copy.wait()
        for make in self.started:
            remote(*make()).wait_send()


def backward_kernel(kinds, planes, layout, *refs):
    r = Space(layout, refs)
    bf16, f32 = jnp.bfloat16, jnp.float32
    here = Peers(planes)
    place, length = here.seq, r.length[0]
    red = Reduction(kinds, here, r)
    rows = r.grad_two.shape[0]
    count = r.keys.shape[0]
    enc_count = r.ckeys_in.shape[0]

    ckeys, cvalues = r.dk.at[pl.ds(0, enc_count), :], r.dk.at[pl.ds(enc_count, enc_count), :]
    dck, dcv = r.dv.at[pl.ds(0, enc_count), :], r.dv.at[pl.ds(enc_count, enc_count), :]
    enc_all = r.token_part.at[pl.ds(0, enc_count), :]
    enc_part = r.token_part.at[pl.ds(enc_count, enc_count), :]
    enc_turned = r.rows_turned.at[:, pl.ds(0, enc_count)]

    def load(n, source, target):
        copy = pltpu.make_async_copy(source, target, r.load_sem.at[n])
        copy.start()
        return copy

    here.meet()
    red.start_pair(GATE)
    grad_two_load = load(0, r.grad_two_in, r.grad_two)
    w_cout_load = load(1, r.w_two.at[3], r.weights.at[3])
    mixed_load = load(2, r.mixed_cross_in, r.mixed)
    cqueries_load = load(3, r.cqueries_in, r.queries)
    ckeys_load = load(4, r.ckeys_in, ckeys)
    cvalues_load = load(5, r.cvalues_in, cvalues)
    red.start_pair(UP)
    red.start_pair(DOWN)
    red.load_own(GATE)
    red.load_own(DOWN)
    normed_two_load = load(6, r.normed_two_in, r.normed)
    encoded_load = load(7, r.enc_in, enc_all)
    w_two_loads = [load(8 + m, r.w_two.at[m], r.weights.at[m]) for m in range(3)]
    hidden_load = load(11, r.hidden_one_in, r.hidden)
    w_sout_load = load(12, r.w_one.at[3], r.weights.at[4])
    keys_load = load(13, r.keys_in, r.keys)
    values_load = load(14, r.values_in, r.values)

    fill_pads(r.pads, count)
    fill_fixed_bias(r.bias)

    def to_branch():
        @row_steps(rows)
        def _(part):
            r.branch[part, :] = r.grad_two[part, :].astype(bf16)

    def store_grad_mixed(part, value):
        r.grad_mixed[:, part] = value.astype(bf16)

    def mixed_low():
        @pl.loop(0, r.mixed.shape[0] // PAIR)
        def _(n):
            part = columns(n)
            r.mixed_low[part, :] = r.mixed[part, :].astype(bf16)

    grad_two_load.wait()
    to_branch()
    w_cout_load.wait()
    times_turned(store_grad_mixed, r.branch, r.weights.at[3])
    mixed_load.wait()
    mixed_low()
    weight_grad(r.grad_cross.at[3], r.mixed_low, r.branch)
    for copy in (cqueries_load, ckeys_load, cvalues_load):
        copy.wait()
    cross_steps = {
        1: [lambda: red.pair_sum(GATE)],
        2: [lambda: red.pair_sum(UP)],
        3: [lambda: red.pair_sum(DOWN)],
    }

    @pl.loop(0, PAIRS)
    def _(pair):
        part = columns(pair)
        backward_pair(
            None, None, r.queries.at[:, part], ckeys.at[:, part], cvalues.at[:, part],
            r.grad_mixed.at[:, part], r.mixed.at[part, :], r.log_cross.at[pair],
            r.dq.at[:, part], dck.at[:, part], dcv.at[:, part], None, None, r.pads, None, r.kt_buf, None,
        )
        for when, steps in cross_steps.items():

            @pl.when(pair == when)
            def _(steps=steps):
                for step in steps:
                    step()

    fill_pads(r.pads, length)
    mixed_self_load = load(15, r.mixed_self_in, r.mixed)
    queries_load = load(16, r.queries_in, r.queries)
    w_two_loads[0].wait()

    def store_gy(part, value):
        r.gy[:, part] = value

    times_turned(store_gy, r.dq, r.weights.at[0])
    red.first_side(GATE)
    normed_two_load.wait()
    r.normed_turned[...] = r.normed[...].T
    weight_grad(r.grad_cross.at[0], r.normed_turned, r.dq)
    encoded_load.wait()
    turn(enc_turned, enc_all)
    weight_grad(r.grad_cross.at[1], enc_turned, dck)
    weight_grad(r.grad_cross.at[2], enc_turned, dcv)
    red.start_pair(CROSS)
    w_two_loads[1].wait()
    w_two_loads[2].wait()

    @pl.loop(0, (enc_count // BLOCK) * (enc_all.shape[1] // BLOCK))
    def _(n):
        across = enc_all.shape[1] // BLOCK
        first = pl.ds(pl.multiple_of((n // across) * BLOCK, BLOCK), BLOCK)
        second = pl.ds(pl.multiple_of((n % across) * BLOCK, BLOCK), BLOCK)
        total = outer_rows(dck[first, :], r.weights[1, second, :])
        total = total + outer_rows(dcv[first, :], r.weights[2, second, :])
        enc_part[first, second] = total.astype(bf16)

    quarters = ((here.along_x, here.to_x), (here.along_y, here.to_y), (here.corner, here.to_corner))

    def send_rows(item, source, size):
        makes = []
        for k, (quarter, device) in enumerate(quarters):

            def make(k=k, quarter=quarter, device=device):
                return (
                    source.at[pl.ds(quarter * size, size), :], r.rows_got[item].at[k],
                    r.r_send.at[item, k], r.r_recv.at[item, k], device,
                )

            remote(*make()).start()
            makes.append(make)
        return makes

    def sum_rows(item, source, size, store):
        got = r.rows_got[item]
        for k in range(3):
            red.arrived(got.at[k], r.r_recv.at[item, k])

        @row_steps(size)
        def _(part):
            start = pl.multiple_of(place * size + part.start, ROW_STEP)
            total = source[pl.ds(start, ROW_STEP), :].astype(f32)
            for k in range(3):
                total = total + got[k, part, :].astype(f32)
            store(part, total)

    enc_rows = enc_count // 4
    enc_sends = send_rows(1, enc_part, enc_rows)
    hidden_load.wait()
    r.small[...] = jnp.zeros_like(r.small)
    r.small[2:3, :] = r.grad_gain_three[...]

    @row_steps(rows)
    def _(part):
        grad, gain = norm_back_rows(r.hidden[part, :], r.gain_two[...], r.gy[part, :])
        total = r.grad_two[part, :] + grad
        r.grad_two[part, :] = total
        r.branch[part, :] = total.astype(bf16)
        r.small[1:2, :] += gain

    w_sout_load.wait()
    times_turned(store_grad_mixed, r.branch, r.weights.at[4])
    mixed_self_load.wait()
    mixed_low()
    weight_grad(r.grad_self.at[3], r.mixed_low, r.branch)
    w_one_loads = [load(17 + m, r.w_one.at[m], r.weights.at[m]) for m in range(3)]
    for copy in (queries_load, keys_load, values_load):
        copy.wait()

    def keep_enc(part, total):
        r.enc_total[part, :] = total

    def enc_done():
        sum_rows(1, enc_part, enc_rows, keep_enc)
        for make in enc_sends:
            remote(*make()).wait_send()
        pltpu.make_async_copy(r.enc_total, r.enc_sum, r.load_sem.at[20]).start()

    def load_normed():
        pltpu.make_async_copy(r.normed_all_in, r.token_part, r.load_sem.at[21]).start()

    def turn_normed():
        pltpu.make_async_copy(r.normed_all_in, r.token_part, r.load_sem.at[21]).wait()
        turn(r.rows_turned, r.token_part)

    self_steps = {
        0: [lambda: red.first_side(UP), lambda: red.pair_sum(CROSS)],
        1: [lambda: red.first_side(DOWN), enc_done, load_normed],
        2: [lambda: red.second_side(GATE), turn_normed],
        3: [lambda: red.second_side(UP)],
        4: [lambda: red.second_side(DOWN), lambda: red.along_planes(GATE)],
        5: [lambda: red.first_side(CROSS), lambda: red.along_planes(UP)],
    }

    @pl.loop(0, PAIRS)
    def _(pair):
        part = columns(pair)
        backward_pair(
            place, r.profile.at[pair], r.queries.at[:, part], r.keys.at[:, part],
            r.values.at[:, part], r.grad_mixed.at[:, part], r.mixed.at[part, :],
            r.log_self.at[pair], r.dq.at[:, part], r.dk.at[:, part], r.dv.at[:, part],
            r.near.at[pair], r.far.at[pair], r.pads, r.bias, r.kt_buf, r.grad_buf,
        )
        for when, steps in self_steps.items():

            @pl.when(pair == when)
            def _(steps=steps):
                for step in steps:
                    step()

    tokens_load = load(22, r.tokens_all_in, r.keys)
    own = pl.ds(pl.multiple_of(place * rows, BLOCK), rows)
    weight_grad(r.grad_self.at[0], r.rows_turned.at[:, own], r.dq)
    weight_grad(r.grad_self.at[1], r.rows_turned, r.dk)
    weight_grad(r.grad_self.at[2], r.rows_turned, r.dv)
    red.start_pair(SELF)
    red.spread(GATE)
    for copy in w_one_loads:
        copy.wait()

    @pl.loop(0, (count // BLOCK) * (r.dk.shape[1] // BLOCK))
    def _(n):
        across = r.dk.shape[1] // BLOCK
        first = pl.ds(pl.multiple_of((n // across) * BLOCK, BLOCK), BLOCK)
        second = pl.ds(pl.multiple_of((n % across) * BLOCK, BLOCK), BLOCK)
        total = outer_rows(r.dk[first, :], r.weights[1, second, :])
        total = total + outer_rows(r.dv[first, :], r.weights[2, second, :])
        r.token_part[first, second] = total.astype(bf16)

    times_turned(store_gy, r.dq, r.weights.at[0])
    red.pair_sum(SELF)
    red.started += send_rows(0, r.token_part, rows)
    red.second_side(CROSS)
    red.along_planes(DOWN)
    red.spread(UP)
    tokens_load.wait()

    @row_steps(count)
    def _(part):
        values = r.keys[part, :].astype(f32)
        scale = lax.rsqrt(jnp.mean(values * values, axis=-1, keepdims=True) + EPSILON)
        grad = r.token_part[part, :].astype(f32)
        r.small[0:1, :] += jnp.sum(grad * values * scale, axis=0, keepdims=True)

    @row_steps(rows)
    def _(part):
        values = r.keys[pl.ds(pl.multiple_of(place * rows + part.start, ROW_STEP), ROW_STEP), :].astype(f32)
        scale = lax.rsqrt(jnp.mean(values * values, axis=-1, keepdims=True) + EPSILON)
        r.small[0:1, :] += jnp.sum(r.gy[part, :] * values * scale, axis=0, keepdims=True)

    for pair in range(PAIRS):
        table = jnp.dot(
            r.near[pair], r.one_hot[...], precision=lax.Precision.HIGHEST, preferred_element_type=f32
        )
        last_bucket = iota(table.shape, 1) == BUCKETS - 1
        table = table + jnp.where(last_bucket, jnp.sum(r.far[pair], axis=1, keepdims=True), 0.0)
        r.small[8 + 2 * pair : 10 + 2 * pair, 0 : table.shape[1]] = table

    small, small_core, small_seq, small_plane = r.small, r.small_core, r.small_seq, r.small_plane
    s_send, s_recv = r.s_send, r.s_recv
    red.send(lambda : (small, small_core, s_send.at[0], s_recv.at[0], here.partner))
    red.finish(GATE)
    red.first_side(SELF)
    red.arrived(small_core, s_recv.at[0])
    small_seq[place] = small[...] + small_core[...]
    for k, (_, device) in enumerate(quarters):
        red.send(lambda k=k, device=device: (small_seq.at[place], small_seq.at[place], s_send.at[1 + k], s_recv.at[1 + k], device))
    red.along_planes(CROSS)
    red.spread(DOWN)
    red.finish(UP)
    red.second_side(SELF)
    for k, (quarter, _) in enumerate(quarters):
        red.arrived(small_seq.at[quarter], s_recv.at[1 + k])
    small_plane[here.plane] = (small_seq[0] + small_seq[1]) + (small_seq[2] + small_seq[3])
    for k in range(1, planes):
        red.send(lambda k=k: (small_plane.at[here.plane], small_plane.at[here.plane],
            s_send.at[3 + k], s_recv.at[3 + k], here.at_plane(here.ahead(k))))

    def keep_tokens(part, total):
        values = r.keys[pl.ds(pl.multiple_of(place * rows + part.start, ROW_STEP), ROW_STEP), :].astype(f32)
        grad, _ = norm_back_rows(values, r.gain_one[...], r.gy[part, :] + total)
        r.hidden[part, :] = r.grad_two[part, :] + grad

    sum_rows(0, r.token_part, rows, keep_tokens)
    token_copy = pltpu.make_async_copy(r.hidden, r.grad_tokens, r.load_sem.at[23])
    token_copy.start()
    red.spread(CROSS)
    red.finish(DOWN)
    for k in range(1, planes):
        red.arrived(small_plane.at[here.ahead(planes - k)], s_recv.at[3 + k])
    total = small_plane[0]
    for k in range(1, planes):
        total = total + small_plane[k]
    r.small_out[...] = total
    red.along_planes(SELF)
    red.finish(CROSS)
    red.spread(SELF)
    red.finish(SELF)
    token_copy.wait()
    pltpu.make_async_copy(r.enc_total, r.enc_sum, r.load_sem.at[20]).wait()
    red.end()


def backward_fused(shards, length, small, large):
    kinds = make_kinds(shards)
    planes = lax.axis_size("fsdp") // 2
    lower = planes // 2
    kinds = [kinds[n] for n in (2, 3, 4, 1, 0)]
    shapes = full_shapes(kinds, planes)
    f32, low = jnp.float32, jnp.bfloat16
    rows, width = large["grad_two_in"].shape
    count, enc_count = large["keys_in"].shape[0], large["ckeys_in"].shape[0]
    in_vmem = pl.BlockSpec(memory_space=pltpu.VMEM)
    large["ffn_parts"] = [part.reshape(shape) for part, shape in zip(large["ffn_parts"], shapes)]
    in_layout, operands = flatten(dict(length=length), small, large)
    in_specs = [SCALARS] + [in_vmem] * len(small)
    in_specs += [ANYWHERE] * (len(operands) - len(in_specs))
    small_shape = (24, width)

    def chunks(*lead):
        return [pltpu.VMEM(lead + (kind.rows, kind.cols), low) for kind in kinds]

    results = dict(
        out=[
            shaped((kind.rows, 4 * kind.cols) if isinstance(kind, Wide) else (4, kind.rows, kind.cols), low)
            for kind in kinds
        ],
        grad_tokens=shaped((rows, width), f32),
        enc_sum=shaped((enc_count // 4, width), f32),
        small_out=shaped(small_shape, f32),
    )
    out_layout, out_shapes = flatten(results)
    square = (width, width)
    all_rows = pltpu.VMEM((count, width), low)
    some_rows = pltpu.VMEM((rows, width), low)
    turned_rows = pltpu.VMEM((width, rows), low)
    wide_rows = pltpu.VMEM((rows, width), f32)
    backward_buffers = backward_scratch(count)
    scratch = dict(
        sums=chunks(4, planes),
        side_x=chunks(2, lower),
        side_y=chunks(2, lower),
        last=chunks(2, lower),
        from_z=chunks(planes - 1),
        final=chunks(4),
        stage_band=pltpu.VMEM((4, planes, kinds[GATE].rows, kinds[GATE].cols), low),
        stage_tall=pltpu.VMEM((4, planes, kinds[DOWN].rows, kinds[DOWN].cols), low),
        grad_cross=pltpu.VMEM((4,) + square, low),
        grad_self=pltpu.VMEM((4,) + square, low),
        weights=pltpu.VMEM((5,) + square, low),
        keys=all_rows, values=all_rows, dk=all_rows, dv=all_rows, token_part=all_rows,
        rows_turned=pltpu.VMEM((width, count), low),
        queries=some_rows, normed=some_rows, branch=some_rows, grad_mixed=some_rows, dq=some_rows,
        mixed_low=turned_rows, normed_turned=turned_rows,
        grad_two=wide_rows, hidden=wide_rows, gy=wide_rows,
        mixed=pltpu.VMEM((width, rows), f32),
        enc_total=pltpu.VMEM((enc_count // 4, width), f32),
        rows_got=[pltpu.VMEM((3, rows, width), low), pltpu.VMEM((3, enc_count // 4, width), low)],
        pads=backward_buffers[0], bias=backward_buffers[1], kt_buf=backward_buffers[2],
        grad_buf=backward_buffers[3],
        near=pltpu.VMEM((PAIRS, 2, BLOCK), f32),
        far=pltpu.VMEM((PAIRS, 2, rows), f32),
        small=pltpu.VMEM(small_shape, f32),
        small_core=pltpu.VMEM(small_shape, f32),
        small_seq=pltpu.VMEM((4,) + small_shape, f32),
        small_plane=pltpu.VMEM((planes,) + small_shape, f32),
        own_sem=DMA((3, 4)),
        c_send=DMA((5, 4)), c_recv=DMA((5, 4)),
        a_send=DMA((5, 4)), a_recv=DMA((5, 4)),
        b_send=DMA((5, 2)), b_recv=DMA((5, 2)),
        z_send=DMA((5, planes - 1)), z_recv=DMA((5, planes - 1)),
        g_send=DMA((5, 4)), g_recv=DMA((5, 4)),
        r_send=DMA((2, 3)), r_recv=DMA((2, 3)),
        s_send=DMA((3 + planes,)), s_recv=DMA((3 + planes,)),
        out_sem=DMA((5, 4)), load_sem=DMA((24,)),
    )
    scratch_layout, scratch_shapes = flatten(scratch)
    outs = pl.pallas_call(
        functools.partial(backward_kernel, kinds, planes, in_layout | out_layout | scratch_layout),
        in_specs=in_specs,
        out_specs=[ANYWHERE] * (len(out_shapes) - 1) + [in_vmem],
        out_shape=out_shapes,
        scratch_shapes=scratch_shapes,
        compiler_params=pltpu.CompilerParams(
            collective_id=1, has_side_effects=True, vmem_limit_bytes=66_000_000
        ),
        name="backward_fused",
    )(*operands)
    got = Space(out_layout, outs)
    grads = [got.out[SELF][m] for m in range(4)] + [got.out[CROSS][m] for m in range(4)]
    grads += [got.out[GATE], got.out[UP], got.out[DOWN].reshape(-1, width)]
    return [grad.astype(f32) for grad in grads], got.grad_tokens, got.enc_sum, got.small_out


ONE, TWO, GATE_IN, UP_IN, DOWN_IN = range(5)


class Gathering:
    def __init__(self, kinds, here, r):
        self.kinds, self.here, self.r = kinds, here, r
        self.planes = here.planes
        shape = (4, here.planes, 2, kinds[ONE].rows, kinds[ONE].cols)
        self.full = [r.weights_one.reshape(*shape), r.weights_two.reshape(*shape), *r.ffn_full]
        self.shards = [r.shards[0:4], r.shards[4:8], r.shards[8], r.shards[9], r.shards[10]]
        self.started = []

    def send(self, make):
        remote(*make()).start()
        self.started.append(make)

    def arrived(self, target, recv_sem):
        pltpu.make_async_copy(target, target, recv_sem).wait()

    def plane_copy(self, g, k, source):
        here, r = self.here, self.r
        return remote(
            source, self.kinds[g].part(self.full[g], here.seq, here.plane, here.core),
            r.z_send.at[g, k - 1], r.z_recv.at[g, k - 1], here.at_plane(here.ahead(k)),
        )

    def start_planes(self, g):
        for k in range(1, self.planes):
            if g <= TWO:
                for m in range(4):

                    @pl.when(self.here.seq == m)
                    def _(m=m, k=k):
                        self.plane_copy(g, k, self.shards[g][m]).start()

            else:
                self.plane_copy(g, k, self.kinds[g].own(self.shards[g], self.here.seq)).start()

    def own_copies(self, g):
        here, r, full = self.here, self.r, self.full[g]
        if g <= TWO:
            return [
                pltpu.make_async_copy(
                    self.shards[g][m], full.at[m, here.plane, here.core], r.own_sem.at[g, m]
                )
                for m in range(4)
            ]
        return [
            pltpu.make_async_copy(
                self.shards[g], self.kinds[g].whole(full, here.plane, here.core), r.own_sem.at[g, 0]
            )
        ]

    def start_own(self, g):
        here, r, full = self.here, self.r, self.full[g]
        for copy in self.own_copies(g):
            copy.start()
        if g <= TWO:
            for m in range(4):
                self.send(
                    lambda m=m: (
                        self.shards[g][m], full.at[m, here.plane, here.core],
                        r.p_send.at[g, m], r.p_recv.at[g, m], here.partner,
                    )
                )
        else:
            self.send(
                lambda: (
                    self.shards[g], self.kinds[g].whole(full, here.plane, here.core),
                    r.p_send.at[g, 0], r.p_recv.at[g, 0], here.partner,
                )
            )

    def chunk(self, g, quarter, k, first=0, count=None):
        here = self.here
        return self.kinds[g].part(self.full[g], quarter, here.ahead(self.planes - k), here.core, first, count)

    def from_plane(self, g):
        here, r = self.here, self.r
        for k in range(1, self.planes):
            self.arrived(self.chunk(g, here.seq, k), r.z_recv.at[g, k - 1])
            for n, device in enumerate((here.to_x, here.to_y)):

                def make(k=k, n=n, device=device):
                    chunk = self.chunk(g, here.seq, k)
                    return chunk, chunk, r.x_send.at[n, g, k - 1], r.x_recv.at[n, g, k - 1], device

                self.send(make)

    def from_sides(self, g):
        here, r = self.here, self.r
        half = self.kinds[g].rows // 2
        turns = ((here.along_x, 0, here.to_y), (here.along_y, half, here.to_x))
        for k in range(1, self.planes):
            for n, (quarter, first, device) in enumerate(turns):
                self.arrived(self.chunk(g, quarter, k), r.x_recv.at[n, g, k - 1])

                def make(k=k, n=n, quarter=quarter, first=first, device=device):
                    chunk = self.chunk(g, quarter, k, first, half)
                    return chunk, chunk, r.d_send.at[n, g, k - 1], r.d_recv.at[n, g, k - 1], device

                self.send(make)

    def from_corner(self, g):
        here, r = self.here, self.r
        half = self.kinds[g].rows // 2
        for k in range(1, self.planes):
            self.arrived(self.chunk(g, here.corner, k, 0, half), r.d_recv.at[0, g, k - 1])
            self.arrived(self.chunk(g, here.corner, k, half, half), r.d_recv.at[1, g, k - 1])

            def make(k=k):
                whole = self.kinds[g].whole(self.full[g], here.ahead(self.planes - k), here.core)
                return whole, whole, r.c_send.at[g, k - 1], r.c_recv.at[g, k - 1], here.partner

            self.send(make)

    def complete(self, g):
        here, r, full = self.here, self.r, self.full[g]
        for copy in self.own_copies(g):
            copy.wait()
        if g <= TWO:
            for m in range(4):
                self.arrived(full.at[m, here.plane, 1 - here.core], r.p_recv.at[g, m])
        else:
            self.arrived(self.kinds[g].whole(full, here.plane, 1 - here.core), r.p_recv.at[g, 0])
        for k in range(1, self.planes):
            behind = here.ahead(self.planes - k)
            self.arrived(self.kinds[g].whole(full, behind, 1 - here.core), r.c_recv.at[g, k - 1])

    def end(self):
        for g in range(5):
            for k in range(1, self.planes):
                source = self.shards[g][0] if g <= TWO else self.kinds[g].own(self.shards[g], self.here.seq)
                self.plane_copy(g, k, source).wait_send()
        for make in self.started:
            remote(*make()).wait_send()


def forward_kernel(kinds, planes, layout, *refs):
    r = Space(layout, refs)
    bf16, f32 = jnp.bfloat16, jnp.float32
    here = Peers(planes)
    place, length = here.seq, r.length[0]
    gather = Gathering(kinds, here, r)
    rows, width = r.tokens.shape
    count, enc_count = r.normed.shape[0], r.encoded_rows.shape[0]
    row_ins = (r.tokens, r.encoded)
    row_alls = (r.source_rows, r.encoded_rows)
    stores = []

    def store(n, source, target):
        stores.append((n, source, target))
        pltpu.make_async_copy(source, target, r.store_sem.at[n]).start()

    def block_of(item, quarter, first=0, size=None):
        size_here = row_ins[item].shape[0]
        return row_alls[item].at[pl.ds(quarter * size_here + first, size or size_here), :]

    def rows_start(item):
        for n, device in enumerate((here.to_x, here.to_y)):
            gather.send(
                lambda n=n, device=device: (
                    row_ins[item], block_of(item, place), r.r_send.at[item, n], r.r_recv.at[item, n], device
                )
            )
        pltpu.make_async_copy(row_ins[item], block_of(item, place), r.r_own.at[item]).start()

    def rows_turn(item):
        half = row_ins[item].shape[0] // 2
        turns = ((here.along_x, 0, here.to_y), (here.along_y, half, here.to_x))
        for n, (quarter, first, device) in enumerate(turns):
            gather.arrived(block_of(item, quarter), r.r_recv.at[item, n])

            def make(n=n, quarter=quarter, first=first, device=device):
                chunk = block_of(item, quarter, first, half)
                return chunk, chunk, r.r_send.at[item, 2 + n], r.r_recv.at[item, 2 + n], device

            gather.send(make)

    def rows_done(item):
        half = row_ins[item].shape[0] // 2
        gather.arrived(block_of(item, here.corner, 0, half), r.r_recv.at[item, 2])
        gather.arrived(block_of(item, here.corner, half, half), r.r_recv.at[item, 3])
        pltpu.make_async_copy(row_ins[item], block_of(item, place), r.r_own.at[item]).wait()

    def norm_rows(values, gain):
        scale = lax.rsqrt(jnp.mean(values * values, axis=-1, keepdims=True) + EPSILON)
        return (values * scale * gain[...]).astype(bf16)

    def project(out, left, weight):
        across = weight.shape[1] // BLOCK

        @pl.loop(0, (left.shape[0] // BLOCK) * across)
        def _(n):
            first = pl.ds(pl.multiple_of((n // across) * BLOCK, BLOCK), BLOCK)
            second = pl.ds(pl.multiple_of((n % across) * BLOCK, BLOCK), BLOCK)
            out[first, second] = product(left[first, :], weight[:, second]).astype(out.dtype)

    here.meet()
    rows_start(0)
    gather.start_planes(ONE)
    rows_start(1)
    for g in (TWO, GATE_IN, UP_IN, DOWN_IN):
        gather.start_planes(g)
    for g in range(5):
        gather.start_own(g)
    fill_pads(r.pads, length)
    fill_fixed_bias(r.bias)
    rows_turn(0)
    gather.from_plane(ONE)
    rows_turn(1)
    rows_done(0)

    @row_steps(count)
    def _(part):
        r.normed[part, :] = norm_rows(r.source_rows[part, :].astype(f32), r.gain_one)

    store(0, r.source_rows, r.tokens_all)
    store(1, r.normed, r.normed_all)
    gather.from_sides(ONE)
    gather.from_plane(TWO)
    gather.from_corner(ONE)
    rows_done(1)
    store(2, r.encoded_rows, r.enc_all)
    gather.complete(ONE)
    store(3, r.weights_one, r.w_one)
    own = pl.ds(pl.multiple_of(place * rows, BLOCK), rows)
    project(r.query_rows, r.normed.at[own, :], r.weights_one.at[0])
    project(r.key_rows, r.normed, r.weights_one.at[1])
    project(r.value_rows, r.normed, r.weights_one.at[2])
    store(4, r.query_rows, r.queries)
    store(5, r.key_rows, r.keys)
    store(6, r.value_rows, r.values)
    gather.from_plane(GATE_IN)
    gather.from_sides(TWO)
    self_steps = {2: [lambda: gather.from_plane(UP_IN)], 4: [lambda: gather.from_corner(TWO)]}

    def stepped(table, pair):
        for when, steps in table.items():

            @pl.when(pair == when)
            def _(steps=steps):
                for step in steps:
                    step()

    @pl.loop(0, PAIRS)
    def _(pair):
        part = columns(pair)
        self_forward_pair(
            place, r.profile.at[pair], r.query_rows.at[:, part], r.key_rows.at[:, part],
            r.value_rows.at[:, part], r.mixed.at[:, part], r.turned_one.at[part, :], r.log_self.at[pair],
            r.pads, r.bias, r.s_buf, r.vt_buf,
        )
        stepped(self_steps, pair)

    store(7, r.turned_one, r.mixed_self_turned)
    project(r.hidden, r.mixed, r.weights_one.at[3])

    @row_steps(rows)
    def _(part):
        start = pl.multiple_of(place * rows + part.start, ROW_STEP)
        total = r.hidden[part, :] + r.source_rows[pl.ds(start, ROW_STEP), :].astype(f32)
        r.hidden[part, :] = total
        r.normed_rows[part, :] = norm_rows(total, r.gain_two)

    store(8, r.hidden, r.hidden_one)
    store(9, r.normed_rows, r.normed_two)
    gather.from_plane(DOWN_IN)
    gather.from_sides(GATE_IN)
    gather.complete(TWO)
    store(10, r.weights_two, r.w_two)
    project(r.cquery_rows, r.normed_rows, r.weights_two.at[0])
    project(r.ckey_rows, r.encoded_rows, r.weights_two.at[1])
    project(r.cvalue_rows, r.encoded_rows, r.weights_two.at[2])
    store(11, r.cquery_rows, r.cqueries)
    store(12, r.ckey_rows, r.ckeys)
    store(13, r.cvalue_rows, r.cvalues)
    cross_steps = {
        1: [lambda: gather.from_corner(GATE_IN)],
        3: [lambda: gather.from_sides(UP_IN)],
    }

    @pl.loop(0, PAIRS)
    def _(pair):
        part = columns(pair)
        cross_forward_pair(
            r.cquery_rows.at[:, part], r.ckey_rows.at[:, part], r.cvalue_rows.at[:, part],
            r.cmixed.at[:, part], r.turned_two.at[part, :], r.log_cross.at[pair],
        )
        stepped(cross_steps, pair)

    store(14, r.turned_two, r.mixed_cross_turned)
    gather.from_sides(DOWN_IN)
    project(r.hidden_last, r.cmixed, r.weights_two.at[3])

    @row_steps(rows)
    def _(part):
        total = r.hidden_last[part, :] + r.hidden[part, :]
        r.hidden_last[part, :] = total
        r.normed_last[part, :] = norm_rows(total, r.gain_three)

    store(15, r.hidden_last, r.hidden_two)
    store(16, r.normed_last, r.normed_three)
    gather.from_corner(UP_IN)
    gather.from_corner(DOWN_IN)
    for g in (GATE_IN, UP_IN, DOWN_IN):
        gather.complete(g)
    gather.end()
    for n, source, target in stores:
        pltpu.make_async_copy(source, target, r.store_sem.at[n]).wait()


def forward_fused(shards, length, tokens, encoded, small):
    kinds = make_kinds(shards)
    planes = lax.axis_size("fsdp") // 2
    f32, low = jnp.float32, jnp.bfloat16
    rows, width = tokens.shape
    enc_rows = encoded.shape[0]
    count, enc_count = 4 * rows, 4 * enc_rows
    square = (4, width, width)
    in_vmem = pl.BlockSpec(memory_space=pltpu.VMEM)
    in_layout, operands = flatten(
        dict(length=length), small, dict(tokens=tokens, encoded=encoded, shards=list(shards))
    )
    in_specs = [SCALARS] + [in_vmem] * len(small)
    in_specs += [ANYWHERE] * (len(operands) - len(in_specs))
    shapes = full_shapes(kinds, planes)
    large_outs = dict(
        w_one=shaped(square, low), w_two=shaped(square, low),
        ffn_full=[shaped(shape, low) for shape in shapes[2:]],
        tokens_all=shaped((count, width), low), normed_all=shaped((count, width), low),
        enc_all=shaped((enc_count, width), low),
        queries=shaped((rows, width), low), keys=shaped((count, width), low),
        values=shaped((count, width), low), mixed_self_turned=shaped((width, rows), f32),
        hidden_one=shaped((rows, width), f32), normed_two=shaped((rows, width), low),
        cqueries=shaped((rows, width), low), ckeys=shaped((enc_count, width), low),
        cvalues=shaped((enc_count, width), low), mixed_cross_turned=shaped((width, rows), f32),
        hidden_two=shaped((rows, width), f32), normed_three=shaped((rows, width), low),
    )
    small_outs = dict(
        log_self=shaped((PAIRS, 2, rows), f32), log_cross=shaped((PAIRS, 2, rows), f32)
    )
    out_layout, out_shapes = flatten(large_outs, small_outs)
    all_rows = pltpu.VMEM((count, width), low)
    enc_all = pltpu.VMEM((enc_count, width), low)
    some_rows = pltpu.VMEM((rows, width), low)
    wide_rows = pltpu.VMEM((rows, width), f32)
    turned = pltpu.VMEM((width, rows), f32)
    buffers = forward_scratch(count, rows)
    steps = planes - 1
    scratch = dict(
        weights_one=pltpu.VMEM(square, low), weights_two=pltpu.VMEM(square, low),
        source_rows=all_rows, normed=all_rows, key_rows=all_rows, value_rows=all_rows,
        encoded_rows=enc_all, ckey_rows=enc_all, cvalue_rows=enc_all,
        query_rows=some_rows, cquery_rows=some_rows, mixed=some_rows, cmixed=some_rows,
        normed_rows=some_rows, normed_last=some_rows,
        hidden=wide_rows, hidden_last=wide_rows, turned_one=turned, turned_two=turned,
        pads=buffers[0], bias=buffers[1], s_buf=buffers[2], vt_buf=buffers[3],
        z_send=DMA((5, steps)), z_recv=DMA((5, steps)),
        own_sem=DMA((5, 4)), p_send=DMA((5, 4)), p_recv=DMA((5, 4)),
        x_send=DMA((2, 5, steps)), x_recv=DMA((2, 5, steps)),
        d_send=DMA((2, 5, steps)), d_recv=DMA((2, 5, steps)),
        c_send=DMA((5, steps)), c_recv=DMA((5, steps)),
        r_send=DMA((2, 4)), r_recv=DMA((2, 4)), r_own=DMA((2,)), store_sem=DMA((17,)),
    )
    scratch_layout, scratch_shapes = flatten(scratch)
    outs = pl.pallas_call(
        functools.partial(forward_kernel, kinds, planes, in_layout | out_layout | scratch_layout),
        in_specs=in_specs,
        out_specs=[ANYWHERE] * (len(out_shapes) - 2) + [in_vmem] * 2,
        out_shape=out_shapes,
        scratch_shapes=scratch_shapes,
        compiler_params=pltpu.CompilerParams(
            collective_id=0, has_side_effects=True, vmem_limit_bytes=66_000_000
        ),
        name="forward_fused",
    )(*operands)
    return Space(out_layout, outs)


def local(
    tokens, encoded, lengths, cotangent, gain_self, gain_cross, gain_ff, bucket_table,
    self_query, self_key, self_value, self_out, cross_query, cross_key, cross_value, cross_out,
    ff_gate, ff_up, ff_down,
):
    rows_here = tokens.shape[1]
    seq_place = lax.axis_index("seq")
    length = lengths[0]
    bf16, f32 = jnp.bfloat16, jnp.float32
    gain_one = gain_self.astype(f32)
    gain_two = gain_cross.astype(f32)
    gain_three = gain_ff.astype(f32)
    shards = (
        self_query, self_key, self_value, self_out, cross_query, cross_key, cross_value, cross_out,
        ff_gate, ff_up, ff_down,
    )
    one_hot = (
        bucket_ids(BLOCK)[:, None] == jnp.arange(BUCKETS, dtype=jnp.int32)[None, :]
    ).astype(bf16)
    profile = inner_rows(bucket_table, one_hot.T).reshape(PAIRS, 2, BLOCK)
    place = jnp.stack([seq_place.astype(jnp.int32), length])

    source = tokens[0].astype(f32)
    fit = kernels_fit(shards)
    if fit:
        forward = forward_fused(
            shards, lengths, tokens[0], encoded[0],
            dict(
                profile=profile, gain_one=gain_one[None], gain_two=gain_two[None], gain_three=gain_three[None]
            ),
        )
        width = source.shape[1]
        hidden_two, normed_three = forward.hidden_two, forward.normed_three
        w_gate, w_up, w_down = (full.reshape(-1, full.shape[-1]) for full in forward.ffn_full)
    else:
        weights, tokens_all, enc_all = gather_plain(shards, tokens[0], encoded[0])
        (w_query, w_key, w_value, w_sout, w_cquery, w_ckey, w_cvalue, w_cout, w_gate, w_up, w_down) = weights
        normed_all = rms_scale(tokens_all.astype(f32), gain_one).astype(bf16)
        normed_one = rms_scale(source, gain_one).astype(bf16)
        queries = product(normed_one, w_query).astype(bf16)
        keys = product(normed_all, w_key).astype(bf16)
        values = product(normed_all, w_value).astype(bf16)
        mixed_self, mixed_self_turned, log_self = self_forward(place, profile, queries, keys, values)
        hidden_one = source + product(mixed_self, w_sout)
        normed_two = rms_scale(hidden_one, gain_two).astype(bf16)
        cqueries = product(normed_two, w_cquery).astype(bf16)
        ckeys = product(enc_all, w_ckey).astype(bf16)
        cvalues = product(enc_all, w_cvalue).astype(bf16)
        mixed_cross, mixed_cross_turned, log_cross = cross_forward(cqueries, ckeys, cvalues)
        hidden_two = hidden_one + product(mixed_cross, w_cout)
        normed_three = rms_scale(hidden_two, gain_three).astype(bf16)
    gate = product(normed_three, w_gate)
    up = product(normed_three, w_up)

    def gated(gate_rows, up_rows):
        return jax.nn.gelu(gate_rows, approximate=True) * up_rows

    activated_f, pull_gate = jax.vjp(gated, gate, up)
    activated = activated_f.astype(bf16)
    slot_ids = seq_place * rows_here + jnp.arange(rows_here, dtype=jnp.int32)
    valid = (slot_ids < length).astype(f32)[:, None]
    result = (valid * (hidden_two + product(activated, w_down))).astype(bf16)

    grad_result = valid * cotangent[0].astype(f32)
    branch_ff = grad_result.astype(bf16)
    grad_gate_f, grad_up_f = pull_gate(outer_rows(branch_ff, w_down))
    grad_gate = grad_gate_f.astype(bf16)
    grad_up = grad_up_f.astype(bf16)
    g_down = inner_rows(activated, branch_ff).astype(bf16)
    g_gate = inner_rows(normed_three, grad_gate).astype(bf16)
    g_up = inner_rows(normed_three, grad_up).astype(bf16)
    grad_three, grad_gain_three = norm_back(
        hidden_two, gain_three, outer_rows(grad_gate, w_gate) + outer_rows(grad_up, w_up)
    )
    grad_two = grad_result + grad_three
    if fit:
        one_hot_wide = jnp.pad(one_hot.astype(f32), ((0, 0), (0, PAIR - BUCKETS)))
        grads, grad_tokens, enc_sum, small = backward_fused(
            shards, lengths,
            dict(
                profile=profile, log_cross=forward.log_cross, log_self=forward.log_self,
                gain_one=gain_one[None], gain_two=gain_two[None], grad_gain_three=grad_gain_three[None],
                one_hot=one_hot_wide,
            ),
            dict(
                ffn_parts=[g_gate, g_up, g_down], w_one=forward.w_one, w_two=forward.w_two,
                grad_two_in=grad_two, mixed_cross_in=forward.mixed_cross_turned,
                cqueries_in=forward.cqueries, ckeys_in=forward.ckeys, cvalues_in=forward.cvalues,
                normed_two_in=forward.normed_two, enc_in=forward.enc_all, hidden_one_in=forward.hidden_one,
                mixed_self_in=forward.mixed_self_turned, queries_in=forward.queries, keys_in=forward.keys,
                values_in=forward.values, normed_all_in=forward.normed_all,
                tokens_all_in=forward.tokens_all,
            ),
        )
        table_sum = small[8 : 8 + HEADS, :BUCKETS].T
        return (
            result[None], grad_tokens[None], enc_sum[None], small[0], small[1], small[2], table_sum, *grads
        )
    branch_cross = grad_two.astype(bf16)
    g_cout = inner_rows(mixed_cross, branch_cross).astype(bf16)
    grad_mixed_cross = outer_rows(branch_cross, w_cout).astype(bf16)
    grad_cq, grad_ck, grad_cv = cross_backward(
        cqueries, ckeys, cvalues, grad_mixed_cross, mixed_cross_turned, log_cross
    )
    g_cquery = inner_rows(normed_two, grad_cq).astype(bf16)
    g_ckey = inner_rows(enc_all, grad_ck).astype(bf16)
    g_cvalue = inner_rows(enc_all, grad_cv).astype(bf16)
    enc_part = (outer_rows(grad_ck, w_ckey) + outer_rows(grad_cv, w_cvalue)).astype(bf16)
    grad_two_back, grad_gain_two = norm_back(hidden_one, gain_two, outer_rows(grad_cq, w_cquery))
    grad_one = grad_two + grad_two_back
    branch_self = grad_one.astype(bf16)
    g_sout = inner_rows(mixed_self, branch_self).astype(bf16)
    grad_mixed_self = outer_rows(branch_self, w_sout).astype(bf16)
    grad_q, grad_k, grad_v, near_part, far_part = self_backward(
        place, profile, queries, keys, values, grad_mixed_self, mixed_self_turned, log_self
    )
    g_query = inner_rows(normed_one, grad_q).astype(bf16)
    g_key = inner_rows(normed_all, grad_k).astype(bf16)
    g_value = inner_rows(normed_all, grad_v).astype(bf16)
    token_part = (outer_rows(grad_k, w_key) + outer_rows(grad_v, w_value)).astype(bf16)
    query_part = outer_rows(grad_q, w_query)

    near_rows = near_part.reshape(HEADS, BLOCK)
    far_rows = jnp.sum(far_part, axis=-1).reshape(HEADS)
    table_part = lax.dot_general(
        one_hot.astype(f32), near_rows, (((0,), (1,)), ((), ())),
        precision=lax.Precision.HIGHEST, preferred_element_type=f32,
    )
    table_part = table_part.at[BUCKETS - 1].add(far_rows)

    hat_all = rms_scale(tokens_all.astype(f32), jnp.ones_like(gain_one))
    hat_one = rms_scale(source, jnp.ones_like(gain_one))
    grad_gain_one = jnp.sum(token_part.astype(f32) * hat_all, axis=0) + jnp.sum(
        query_part * hat_one, axis=0
    )
    table_row = jnp.zeros((gain_one.shape[0],), f32).at[: BUCKETS * HEADS].set(table_part.reshape(-1))
    small = jnp.stack([grad_gain_one, grad_gain_two, grad_gain_three, table_row] + [jnp.zeros_like(gain_one)] * 4)
    reduced, token_sum, enc_sum, small = reduce_plain(
        (g_query, g_key, g_value, g_sout, g_cquery, g_ckey, g_cvalue, g_cout, g_gate, g_up, g_down),
        token_part, enc_part, small,
    )
    grad_zero, _ = norm_back(source, gain_one, query_part + token_sum)
    grad_tokens = grad_one + grad_zero
    table_sum = small[3, : BUCKETS * HEADS].reshape(BUCKETS, HEADS)
    small = (small[0], small[1], small[2], table_sum)
    return (result[None], grad_tokens[None], enc_sum[None], *small, *reduced)


def solution(mesh):
    rows3 = P("fsdp", "seq", None)
    rows2 = P("fsdp", None)
    return jax.shard_map(
        local,
        mesh=mesh,
        in_specs=(rows3, rows3, P("fsdp"), rows3, P(), P(), P(), P(), *([rows2] * 11)),
        out_specs=(rows3, rows3, rows3, P(), P(), P(), P(), *([rows2] * 11)),
        check_vma=False,
    )
```

time: 420 us -> 305 us (0.73); the launches traced: 415 us -> 304 us
  Pallas kernels: 308 us -> 261 us
  matrix products: 64.3 us -> 23.9 us
  other arithmetic: 21.4 us -> 7.79 us
  local copies, waits for them, and re-layouts: 19.2 us -> 10.2 us
    pallas_call x6 -> x2, Pallas kernels: 308 us -> 261 us  [the longest x1 167 us: backward_fused(): pl.pallas_call(functools.partial(backward_kernel, kinds, planes, in_layou...]
    dot_general x11 -> x3, matrix products: 25.6 us -> 8.16 us  [outer_rows(): lax.dot_general(left, right, (((1,), (1,)), ((), ())), preferred_element_...]
    dot_general x11 -> x3, matrix products: 23.3 us -> 7.22 us  [product(): return jnp.dot(left, right, preferred_element_type=jnp.float32)]
    another operation x5 -> x0, other arithmetic: 9.71 us -> none  [the longest x2 5.09 us: reduce_all(): whole = [jnp.stack(grads[:4]), jnp.stack(grads[4:8]), *grads[8:]]]
    slice x3 -> x1, local copies, waits for them, and re-layouts: 8.86 us -> 1.49 us  [local(): small[2]]
    dot_general x12 -> x4, matrix products: 15.3 us -> 8.52 us  [inner_rows(): lax.dot_general(left, right, (((0,), (0,)), ((), ())), preferred_element_...]
    unnamed x115 -> x30, local copies, waits for them, and re-layouts: 7.67 us -> 2.43 us
where the time goes in v2:
time: 305 us; the launch traced here: 304 us
  Pallas kernels  261 us (86%)
  matrix products  23.9 us (8%)
  local copies, waits for them, and re-layouts  10.2 us (3%)
  other arithmetic  7.79 us (3%)
    pallas_call x1, Pallas kernels, backward_fused(): pl.pallas_call(functools.partial(backward_kernel, kinds, planes, in_layou...  167 us
    pallas_call x1, Pallas kernels, forward_fused(): pl.pallas_call(functools.partial(forward_kernel, kinds, planes, in_layout...  94 us
    dot_general x4, matrix products, inner_rows(): lax.dot_general(left, right, (((0,), (0,)), ((), ())), preferred_element_...  8.52 us
    dot_general x3, matrix products, outer_rows(): lax.dot_general(left, right, (((1,), (1,)), ((), ())), preferred_element_...  8.16 us
    dot_general x3, matrix products, product(): return jnp.dot(left, right, preferred_element_type=jnp.float32)  7.22 us

profile of v2, /device:TPU:0, one launch (start us, length us, event | category | flops | bytes accessed | tf_op | source)
XLA Modules:
  0.0 304.4 jit_solution(349827724996367411)
XLA Ops:
  0.7 0.0 copy-start
  1.4 0.0 copy-done
  1.4 0.2 convolution_bitcast_fusion
  1.6 0.6 reshape.180.refs_1_
  2.2 1.3 reshape.188.refs_2_.refs_4_
  3.5 1.3 reshape.189.refs_3_.refs_5_
  4.7 1.3 broadcast_in_dim.37.refs_4_
  6.0 94.0 %forward_fused.1 = (bf16[4,768,768]{2,1,0:T(8,128)(2,1)}, bf16[4,768,768]{2,1,0:T(8,128)(2,1)}, bf16[4,2,96,2048]{3,2,1,0:T(8,128)(2,1)}, bf16[4,2,96,2048]{3,2,...) custom-call(s32[1]{0:T(128)} %copy.39.refs_0_, ...), custom_call_target="tpu_custom_call" | custom-call | tf_op jit(solution)/shard_map/forward_fused/pallas_call | solution.py:1603
  100.0 0.0 copy-start.1
  100.0 0.0 copy-start.3
  100.0 3.1 %fusion.53 = f32[256,2048]{1,0:T(8,128)S(1)} fusion(bf16[256,768]{1,0:T(8,128)(2,1)} %get-tuple-element.49, bf16[768,2048]{1,0:T(8,128)(2,1)} %bitcast.81), kind=kOutput, calls=%fused_computation.103 | convolution fusion | flops 805306368 | bytes 5636096 | tf_op jit(solution)/shard_map/dot_general | solution.py:49
  103.2 0.0 copy-done.1
  103.2 0.0 copy-done.3
  103.2 0.0 copy-start.6
  103.2 2.3 fusion.54
  105.5 0.0 copy-done.6
  105.6 0.0 copy-start.13
  105.6 5.7 %multiply_convert_fusion = (bf16[256,2048]{1,0:T(8,128)(2,1)S(1)}, bf16[256,2048]{1,0:T(8,128)(2,1)S(1)}, bf16[256,2048]{1,0:T(8,128)(2,1)S(1)}) fusion(f32[256,2048]{1,0:T(8,128)S(1)} %fusion.53, f32[256,2048]{1,0:T(8,128)} %fusion.54, bf16[2048,768]{1,0:T(8,128)(2,1)} %bitcast.87, bf16[1,256,768]{2,1,0:T(8,128)(2,1)S(1)} %copy-done.6, ...), kind=kOutput, calls=%fused_computation.12 | convolution fusion | flops 819527680 | bytes 10880000 | tf_op jit(solution)/shard_map/dot_general | solution.py:59
  111.2 0.0 copy-done.4
  111.2 0.0 copy-done.13
  111.3 0.0 copy-start.12
  111.3 0.0 copy-start.5
  111.3 1.7 fusion.9
  113.0 0.0 copy-done.12
  113.0 0.1 multiply_reduce_fusion.2
  113.2 0.0 copy-done.5
  113.2 0.0 copy-start.2
  113.2 1.1 fusion.55
  114.3 0.7 copy-done.2
  115.1 1.4 multiply_reduce_fusion
  116.4 0.6 reshape.184.refs_6_
  117.0 0.1 fusion.20
  117.1 0.7 pad_convert_fusion.refs_7_
  117.8 2.7 convolution_convert_fusion.2
  120.5 2.8 convolution_convert_fusion.1
  123.2 2.9 convolution_convert_fusion
  126.1 1.2 fusion.12.refs_13_
  127.3 167.0 %backward_fused.1 = (bf16[96,2048]{1,0:T(8,128)(2,1)}, bf16[96,2048]{1,0:T(8,128)(2,1)}, bf16[4,64,768]{2,1,0:T(8,128)(2,1)}, bf16[4,96,768]{2,1,0:T(8,128)(2,1)...) custom-call(s32[1]{0:T(128)} %copy.39.refs_0_, ...), custom_call_target="tpu_custom_call" | custom-call | tf_op jit(solution)/shard_map/backward_fused/pallas_call | solution.py:1220
  294.3 0.0 copy-start.11
  294.3 1.5 slice_reduce_fusion
  295.8 1.3 slice_bitcast_fusion
  297.1 2.8 bitcast_convert_fusion.1
  299.9 0.0 copy-done.11
  299.9 1.0 convert_element_type.298
  300.9 1.0 convert_element_type.299
  301.8 1.0 bitcast_convert_fusion
  302.8 0.9 copy.40
  303.7 0.7 copy.41
  (14 shorter events, 0.1 us)
Async XLA Ops:
  0.7 0.7 copy-start
  100.0 3.2 %copy-start.1 = (bf16[4,2,96,2048]{3,2,1,0:T(8,128)(2,1)S(1)}, bf16[4,2,96,2048]{3,2,1,0:T(8,128)(2,1)}, u32[]{:S(2)}) copy-start(bf16[4,2,96,2048]{3,2,1,0:T(8,128)(2,1)} %get-tuple-element.51) | copy-start | bytes 9437188
  100.0 3.2 %copy-start.3 = (bf16[256,768]{1,0:T(8,128)(2,1)S(1)}, bf16[256,768]{1,0:T(8,128)(2,1)}, u32[]{:S(2)}) copy-start(bf16[256,768]{1,0:T(8,128)(2,1)} %get-tuple-element.49) | copy-start | bytes 1179652
  103.2 2.4 copy-start.6
  105.5 5.7 %copy-start.4 = (f32[256,768]{1,0:T(8,128)S(1)}, f32[256,768]{1,0:T(8,128)}, u32[]{:S(2)}) copy-start(f32[256,768]{1,0:T(8,128)} %get-tuple-element.48) | copy-start | bytes 2359300
  105.6 5.7 %copy-start.13 = (bf16[4,2,256,768]{3,2,1,0:T(8,128)(2,1)S(1)}, bf16[4,2,256,768]{3,2,1,0:T(8,128)(2,1)}, u32[]{:S(2)}) copy-start(bf16[4,2,256,768]{3,2,1,0:T(8,128)(2,1)} %get-tuple-element.52) | copy-start | bytes 9437188
  111.3 1.8 copy-start.12
  111.3 1.9 copy-start.5
  113.2 1.9 copy-start.2
  294.3 5.6 %copy-start.11 = (bf16[96,2048]{1,0:T(8,128)(2,1)S(1)}, bf16[96,2048]{1,0:T(8,128)(2,1)}, u32[]{:S(2)}) copy-start(bf16[96,2048]{1,0:T(8,128)(2,1)} %get-tuple-element.75) | copy-start | bytes 1179652
  297.1 3.8 %copy-start.10 = (bf16[96,2048]{1,0:T(8,128)(2,1)S(1)}, bf16[96,2048]{1,0:T(8,128)(2,1)}, u32[]{:S(2)}) copy-start(bf16[96,2048]{1,0:T(8,128)(2,1)} %get-tuple-element.76) | copy-start | bytes 1179652
  297.1 4.7 %copy-start.9 = (bf16[4,64,768]{2,1,0:T(8,128)(2,1)S(1)}, bf16[4,64,768]{2,1,0:T(8,128)(2,1)}, u32[]{:S(2)}) copy-start(bf16[4,64,768]{2,1,0:T(8,128)(2,1)} %get-tuple-element.77) | copy-start | bytes 1179652
  299.9 2.9 copy-start.7
  300.9 2.8 copy-start.8

commit v3 on v2

--- a/solution.py
+++ b/solution.py
@@ -597,57 +597,25 @@
     return pl.ds(pl.multiple_of(pair * PAIR, PAIR), PAIR)
 
 
-def tiles(count):
+def row_steps(count, step):
     def run(body):
-        @pl.loop(0, count // BLOCK)
+        @pl.loop(0, count // step)
         def _(n):
-            body(pl.ds(pl.multiple_of(n * BLOCK, BLOCK), BLOCK))
+            body(pl.ds(pl.multiple_of(n * step, step), step))
 
     return run
 
 
-def times_turned(store, left, weight):
-    value = left[...]
-
-    @tiles(weight.shape[0])
+def weight_grad(out, left, right):
+    @row_steps(out.shape[0], 384)
     def _(part):
-        store(part, outer_rows(value, weight[part, :]))
-
-
-def times(store, left, weight):
-    value = left[...]
-
-    @tiles(weight.shape[1])
+        out[part, :] = inner_rows(left[:, part], right[...]).astype(jnp.bfloat16)
+
+
+def weight_grad_turned(out, turned, right):
+    @row_steps(out.shape[0], 384)
     def _(part):
-        store(part, product(value, weight[:, part]))
-
-
-def weight_grad(out, turned, right):
-    across = right.shape[1] // BLOCK
-
-    @pl.loop(0, (turned.shape[0] // BLOCK) * across)
-    def _(n):
-        first = pl.ds(pl.multiple_of((n // across) * BLOCK, BLOCK), BLOCK)
-        second = pl.ds(pl.multiple_of((n % across) * BLOCK, BLOCK), BLOCK)
-        out[first, second] = product(turned[first, :], right[:, second]).astype(jnp.bfloat16)
-
-
-def turn(out, source):
-    @tiles(source.shape[0])
-    def _(part):
-        out[:, part] = source[part, :].T
-
-
-ROW_STEP = 32
-
-
-def row_steps(count):
-    def run(body):
-        @pl.loop(0, count // ROW_STEP)
-        def _(n):
-            body(pl.ds(pl.multiple_of(n * ROW_STEP, ROW_STEP), ROW_STEP))
-
-    return run
+        out[part, :] = product(turned[part, :].astype(jnp.bfloat16), right[...]).astype(jnp.bfloat16)
 
 
 def norm_back_rows(values, gain, grad_normed):
@@ -656,9 +624,6 @@
     along = jnp.mean(values * scaled, axis=-1, keepdims=True)
     grad_values = scale * scaled - values * (scale * scale * scale) * along
     return grad_values, jnp.sum(grad_normed * values * scale, axis=0, keepdims=True)
-
-
-GATE, UP, DOWN, CROSS, SELF = range(5)
 
 
 class Space:
@@ -679,18 +644,29 @@
     return layout, flat
 
 
-class Reduction:
-    def __init__(self, kinds, here, r):
-        self.kinds, self.here, self.r = kinds, here, r
+class StackRows(Stack):
+    def __init__(self, first, rows, cols):
+        super().__init__(rows, cols)
+        self.first = first
+
+    def planes(self, ref, quarter, core):
+        return ref.at[quarter, :, core, pl.ds(self.first, self.rows), :]
+
+
+DOWN, GATE, UP, CROSS, SELF, SELF_REST = range(6)
+GROUPS = 6
+
+
+class Sum:
+    planes_first = False
+
+    def __init__(self, g, kind, here, r, part):
+        self.g, self.kind, self.here, self.r = g, kind, here, r
+        self.part = part
         self.planes = here.planes
-        self.lower = here.planes // 2
+        self.sums, self.final = r.sums[g], r.final[g]
+        self.side_x, self.side_y, self.last, self.from_z = r.side_x[g], r.side_y[g], r.last[g], r.from_z[g]
         self.started = []
-        shape = (4, here.planes, 2, kinds[CROSS].rows, kinds[CROSS].cols)
-        self.parts = [
-            *r.ffn_parts,
-            r.grad_cross.reshape(*shape), r.grad_self.reshape(*shape),
-        ]
-        self.sums = r.sums
 
     def send(self, make):
         remote(*make()).start()
@@ -699,144 +675,242 @@
     def arrived(self, target, recv_sem):
         pltpu.make_async_copy(target, target, recv_sem).wait()
 
-    def own_copy(self, g, q):
-        stage = (self.r.stage_tall if g == DOWN else self.r.stage_band)
-        return pltpu.make_async_copy(
-            self.kinds[g].planes(self.parts[g], q, self.here.core), stage.at[q], self.r.own_sem.at[g, q]
-        )
-
-    def load_own(self, g):
-        for q in range(4):
-            self.own_copy(g, q).start()
-
-    def start_pair(self, g):
-        r = self.r
-        for q in range(4):
-            self.send(lambda g=g, q=q: (self.kinds[g].planes(self.parts[g], q, 1 - self.here.core), self.sums[g].at[q],
-                r.c_send.at[g, q], r.c_recv.at[g, q], self.here.partner))
-
-    def pair_sum(self, g):
-        r, here, sums, planes = self.r, self.here, self.sums[g], self.planes
-        for q in range(4):
-            self.arrived(sums.at[q], r.c_recv.at[g, q])
-            if g <= DOWN:
-                self.own_copy(g, q).wait()
-        if g <= DOWN:
-            stage = r.stage_tall if g == DOWN else r.stage_band
-
-        @pl.loop(0, 4 * planes)
-        def _(n):
-            q, z = n // planes, n % planes
-            own = stage.at[q, z] if g <= DOWN else self.parts[g].at[q, z, here.core]
-            add_low(sums.at[q, z], own)
-
-        if g == GATE:
-            self.load_own(UP)
-        low, high = pl.ds(0, self.lower), pl.ds(self.lower, planes - self.lower)
+    def pair_source(self, n, core):
+        return self.kind.planes(self.part, n, core), self.sums.at[n]
+
+    def start_pair(self, n):
+        r, g = self.r, self.g
+        source, target = self.pair_source(n, 1 - self.here.core)
+        remote(source, target, r.c_send.at[g, n], r.c_recv.at[g, n], self.here.partner).start()
+
+    def pair_sum(self):
+        for n in range(4):
+            source, target = self.pair_source(n, self.here.core)
+            self.arrived(target, self.r.c_recv.at[self.g, n])
+
+            @pl.loop(0, 4)
+            def _(m, n=n, source=source, target=target):
+                add_low(target.at[m], source.at[m])
+
+    def pair_sent(self):
+        for n in range(4):
+            source, target = self.pair_source(n, 1 - self.here.core)
+            remote(
+                source, target, self.r.c_send.at[self.g, n], self.r.c_recv.at[self.g, n], self.here.partner
+            ).wait_send()
+
+    def half(self, quarter, second):
+        size = self.planes // 2
+        return self.sums.at[quarter, pl.ds(second * size, size)]
+
+    def sides(self):
+        r, g, here = self.r, self.g, self.here
         for n, quarter in enumerate((here.along_x, here.corner)):
-            self.send(lambda g=g, n=n, quarter=quarter: (sums.at[quarter, low], r.side_x[g].at[n],
-                r.a_send.at[g, n], r.a_recv.at[g, n], here.to_x))
+            self.send(
+                lambda n=n, quarter=quarter: (
+                    self.half(quarter, 0), self.side_x.at[n], r.a_send.at[g, n], r.a_recv.at[g, n], here.to_x
+                )
+            )
         for n, quarter in enumerate((here.along_y, here.corner)):
-            self.send(lambda g=g, n=n, quarter=quarter: (sums.at[quarter, high], r.side_y[g].at[n],
-                r.a_send.at[g, 2 + n], r.a_recv.at[g, 2 + n], here.to_y))
-
-    def first_side(self, g):
-        r, here, sums, lower = self.r, self.here, self.sums[g], self.lower
-        side_x, side_y, last = r.side_x[g], r.side_y[g], r.last[g]
+            self.send(
+                lambda n=n, quarter=quarter: (
+                    self.half(quarter, 1), self.side_y.at[n],
+                    r.a_send.at[g, 2 + n], r.a_recv.at[g, 2 + n], here.to_y,
+                )
+            )
+
+    def add_half(self, quarter, second, terms, out=None):
+        size = self.planes // 2
+
+        @pl.loop(0, size)
+        def _(z):
+            add_low(self.sums.at[quarter, second * size + z], *[term.at[z] for term in terms])
+
+    def first_side(self):
+        r, g, here = self.r, self.g, self.here
         for n in range(2):
-            self.arrived(side_x.at[n], r.a_recv.at[g, n])
-            self.arrived(side_y.at[n], r.a_recv.at[g, 2 + n])
-
-        @pl.loop(0, lower)
-        def _(z):
-            add_low(sums.at[here.along_y, z], side_x.at[1, z])
-            add_low(sums.at[here.along_x, lower + z], side_y.at[1, z])
-
-        self.send(lambda g=g: (sums.at[here.along_y, pl.ds(0, lower)], last.at[0],
-            r.b_send.at[g, 0], r.b_recv.at[g, 0], here.to_y))
-        self.send(lambda g=g: (sums.at[here.along_x, pl.ds(lower, lower)], last.at[1],
-            r.b_send.at[g, 1], r.b_recv.at[g, 1], here.to_x))
-
-    def second_side(self, g):
-        r, here, sums, lower = self.r, self.here, self.sums[g], self.lower
-        side_x, side_y, last = r.side_x[g], r.side_y[g], r.last[g]
-        self.arrived(last.at[0], r.b_recv.at[g, 0])
-        self.arrived(last.at[1], r.b_recv.at[g, 1])
-
-        @pl.loop(0, lower)
-        def _(z):
-            add_low(sums.at[here.seq, z], side_x.at[0, z], last.at[0, z])
-            add_low(sums.at[here.seq, lower + z], side_y.at[0, z], last.at[1, z])
-
+            self.arrived(self.side_x.at[n], r.a_recv.at[g, n])
+            self.arrived(self.side_y.at[n], r.a_recv.at[g, 2 + n])
+        self.add_half(here.along_y, 0, [self.side_x.at[1]])
+        self.add_half(here.along_x, 1, [self.side_y.at[1]])
+        for n, (quarter, device) in enumerate(((here.along_y, here.to_y), (here.along_x, here.to_x))):
+            self.send(
+                lambda n=n, quarter=quarter, device=device: (
+                    self.half(quarter, n), self.last.at[n], r.b_send.at[g, n], r.b_recv.at[g, n], device
+                )
+            )
+
+    def second_side(self):
+        r, g, here = self.r, self.g, self.here
+        for n in range(2):
+            self.arrived(self.last.at[n], r.b_recv.at[g, n])
+        self.add_half(here.seq, 0, [self.side_x.at[0], self.last.at[0]])
+        self.add_half(here.seq, 1, [self.side_y.at[0], self.last.at[1]])
+        self.after_square()
+
+    def after_square(self):
+        self.start_planes()
+
+    def plane_share(self, plane):
+        return self.sums.at[self.here.seq, plane]
+
+    def start_planes(self):
+        r, g, here = self.r, self.g, self.here
         for k in range(1, self.planes):
             self.send(
                 lambda k=k: (
-                    sums.at[here.seq, here.ahead(k)], r.from_z[g].at[k - 1],
+                    self.plane_share(here.ahead(k)), self.from_z.at[k - 1],
                     r.z_send.at[g, k - 1], r.z_recv.at[g, k - 1], here.at_plane(here.ahead(k)),
                 )
             )
 
-    def along_planes(self, g):
-        r, here, sums = self.r, self.here, self.sums[g]
-        from_z, final = r.from_z[g], r.final[g]
+    def along_planes(self):
+        r, g, here = self.r, self.g, self.here
         for k in range(1, self.planes):
-            self.arrived(from_z.at[k - 1], r.z_recv.at[g, k - 1])
-        step = 32
-
-        @pl.loop(0, self.kinds[g].rows // step)
+            self.arrived(self.from_z.at[k - 1], r.z_recv.at[g, k - 1])
+        step = 16
+
+        @pl.loop(0, self.kind.rows // step)
         def _(n):
             rows = pl.ds(pl.multiple_of(n * step, step), step)
-            total = sums[here.seq, here.plane, rows, :].astype(jnp.float32)
+            total = self.sums[here.seq, here.plane, rows, :].astype(jnp.float32)
             for k in range(1, self.planes):
-                total = total + from_z[k - 1, rows, :].astype(jnp.float32)
-            final[here.seq, rows, :] = total.astype(jnp.bfloat16)
-
+                total = total + self.from_z[k - 1, rows, :].astype(jnp.float32)
+            self.final[here.seq, rows, :] = total.astype(jnp.bfloat16)
+
+        self.start_spread()
+
+    def start_spread(self):
+        r, g, here = self.r, self.g, self.here
         for n, device in enumerate((here.to_x, here.to_y)):
             self.send(
                 lambda n=n, device=device: (
-                    final.at[here.seq], final.at[here.seq], r.g_send.at[g, n], r.g_recv.at[g, n], device
+                    self.final.at[here.seq], self.final.at[here.seq], r.g_send.at[g, n], r.g_recv.at[g, n], device
                 )
             )
 
-    def spread(self, g):
-        r, here, final = self.r, self.here, self.r.final[g]
-        half = self.kinds[g].rows // 2
-        turns = ((here.along_x, 0, here.to_y), (here.along_y, half, here.to_x))
-        for n, (quarter, first, device) in enumerate(turns):
-            self.arrived(final.at[quarter], r.g_recv.at[g, n])
-
-            def make(n=n, quarter=quarter, first=first, device=device):
-                chunk = final.at[quarter, pl.ds(first, half), :]
-                return chunk, chunk, r.g_send.at[g, 2 + n], r.g_recv.at[g, 2 + n], device
-
-            self.send(make)
-
-    def out_copies(self, g):
-        r, kind, final = self.r, self.kinds[g], self.r.final[g]
-        out = r.out[g]
-        if not isinstance(kind, Wide):
-            return [pltpu.make_async_copy(final, out, r.out_sem.at[g, 0])]
-        return [
-            pltpu.make_async_copy(
-                final.at[q], out.at[:, pl.ds(q * kind.cols, kind.cols)], r.out_sem.at[g, q]
+    def across(self, quarter, second):
+        size = self.kind.cols // 2
+        return self.final.at[quarter, :, pl.ds(second * size, size)]
+
+    def spread(self):
+        r, g, here = self.r, self.g, self.here
+        for n, (quarter, device) in enumerate(((here.along_x, here.to_y), (here.along_y, here.to_x))):
+            self.arrived(self.final.at[quarter], r.g_recv.at[g, n])
+            self.send(
+                lambda n=n, quarter=quarter, device=device: (
+                    self.across(quarter, n), self.across(quarter, n),
+                    r.g_send.at[g, 2 + n], r.g_recv.at[g, 2 + n], device,
+                )
             )
-            for q in range(4)
-        ]
-
-    def finish(self, g):
-        r, here, final = self.r, self.here, self.r.final[g]
-        half = self.kinds[g].rows // 2
-        self.arrived(final.at[here.corner, pl.ds(0, half), :], r.g_recv.at[g, 2])
-        self.arrived(final.at[here.corner, pl.ds(half, half), :], r.g_recv.at[g, 3])
-        for copy in self.out_copies(g):
+
+    def out_copies(self):
+        r, g, kind = self.r, self.g, self.kind
+        if isinstance(kind, Wide):
+            return [
+                pltpu.make_async_copy(
+                    self.final.at[q], r.out[g].at[:, pl.ds(q * kind.cols, kind.cols)], r.out_sem.at[g, q]
+                )
+                for q in range(4)
+            ]
+        out = r.out[min(g, SELF)]
+        if isinstance(kind, StackRows):
+            out = out.at[:, pl.ds(kind.first, kind.rows), :]
+        return [pltpu.make_async_copy(self.final, out, r.out_sem.at[g, 0])]
+
+    def finish(self):
+        r, g, here = self.r, self.g, self.here
+        for n in range(2):
+            self.arrived(self.across(here.corner, n), r.g_recv.at[g, 2 + n])
+        for copy in self.out_copies():
             copy.start()
 
     def end(self):
-        for g in range(5):
-            for copy in self.out_copies(g):
-                copy.wait()
+        for copy in self.out_copies():
+            copy.wait()
+        if self.g not in (DOWN, CROSS):
+            self.pair_sent()
         for make in self.started:
             remote(*make()).wait_send()
+
+
+class PlanesFirst(Sum):
+    planes_first = True
+
+    def pair_source(self, n, core):
+        return self.part.at[n, core], self.sums.at[:, n]
+
+    def half(self, quarter, second):
+        size = self.kind.cols // 2
+        return self.sums.at[quarter, self.here.plane, :, pl.ds(second * size, size)]
+
+    def plane_share(self, plane):
+        return self.sums.at[:, plane]
+
+    def along_planes(self):
+        r, g, here = self.r, self.g, self.here
+        for k in range(1, self.planes):
+            self.arrived(self.from_z.at[k - 1], r.z_recv.at[g, k - 1])
+
+        @pl.loop(0, 4)
+        def _(q):
+            add_low(self.sums.at[q, here.plane], *[self.from_z.at[k - 1, q] for k in range(1, self.planes)])
+
+        self.sides()
+
+    def add_half(self, quarter, second, terms, out=None):
+        size = self.kind.cols // 2
+        add_low(self.half(quarter, second), *terms)
+
+    def after_square(self):
+        self.final[self.here.seq] = self.sums[self.here.seq, self.here.plane]
+        self.start_spread()
+
+
+class BandSum(Sum):
+    def pair_source(self, n, core):
+        return self.part.at[n, :, core], self.sums.at[n]
+
+
+class RowSum(Sum):
+    def __init__(self, g, here, r, source, n):
+        self.g, self.here, self.r, self.source = g, here, r, source
+        self.size, self.cols = source.shape[0] // 4, source.shape[1] // 2
+        self.side_x, self.side_y, self.last = r.row_x[n], r.row_y[n], r.row_last[n]
+        self.started = []
+
+    def half(self, quarter, second):
+        return self.source.at[pl.ds(quarter * self.size, self.size), pl.ds(second * self.cols, self.cols)]
+
+    def add_half(self, quarter, second, terms):
+        @row_steps(self.size, 64)
+        def _(part):
+            add_low(self.half(quarter, second).at[part, :], *[term.at[part, :] for term in terms])
+
+    def total(self, keep):
+        r, g, here = self.r, self.g, self.here
+        for n in range(2):
+            self.arrived(self.last.at[n], r.b_recv.at[g, n])
+        step = 64
+
+        @row_steps(self.size, step)
+        def _(part):
+            halves = []
+            for second, side in enumerate((self.side_x, self.side_y)):
+                value = self.half(here.seq, second)[part, :].astype(jnp.float32)
+                halves.append(
+                    value + side[0, part, :].astype(jnp.float32) + self.last[second, part, :].astype(jnp.float32)
+                )
+            keep(part, jnp.concatenate(halves, axis=1))
+
+    def sent(self):
+        for make in self.started:
+            remote(*make()).wait_send()
+
+
+GELU_SCALE = math.sqrt(2.0 / math.pi)
+GELU_CUBE = 0.044715
+TOKENS, ENCODED = GROUPS, GROUPS + 1
 
 
 def backward_kernel(kinds, planes, layout, *refs):
@@ -844,73 +918,171 @@
     bf16, f32 = jnp.bfloat16, jnp.float32
     here = Peers(planes)
     place, length = here.seq, r.length[0]
-    red = Reduction(kinds, here, r)
-    rows = r.grad_two.shape[0]
-    count = r.keys.shape[0]
-    enc_count = r.ckeys_in.shape[0]
+    rows, width = r.grad_two.shape
+    count, enc_count = r.rows_both.shape[0] // 2, r.ckeys_in.shape[0]
+    owner_rows = width // (2 * planes)
+    shape = (4, planes, 2, owner_rows, width)
+    band = kinds[GATE].cols
+    band_shape = (4, planes, 2, owner_rows, band)
+    tall_shape = (planes, 2, 4, kinds[DOWN].rows, width)
+    keys, values = r.rows_both.at[pl.ds(0, count), :], r.rows_both.at[pl.ds(count, count), :]
+    down = PlanesFirst(DOWN, kinds[DOWN], here, r, r.rows_both.reshape(*tall_shape))
+    gate = BandSum(GATE, kinds[GATE], here, r, r.grad_gate.reshape(*band_shape))
+    up = BandSum(UP, kinds[UP], here, r, r.grad_up.reshape(*band_shape))
+    cross = Sum(CROSS, kinds[CROSS], here, r, r.grad_cross.reshape(*shape))
+    self_one = Sum(SELF, kinds[SELF], here, r, r.grad_self.reshape(*shape))
+    self_two = Sum(SELF_REST, kinds[SELF_REST], here, r, r.grad_self.reshape(*shape))
+    sums = (down, gate, up, cross, self_one, self_two)
+    others = []
 
     ckeys, cvalues = r.dk.at[pl.ds(0, enc_count), :], r.dk.at[pl.ds(enc_count, enc_count), :]
     dck, dcv = r.dv.at[pl.ds(0, enc_count), :], r.dv.at[pl.ds(enc_count, enc_count), :]
     enc_all = r.token_part.at[pl.ds(0, enc_count), :]
     enc_part = r.token_part.at[pl.ds(enc_count, enc_count), :]
-    enc_turned = r.rows_turned.at[:, pl.ds(0, enc_count)]
+    token_sum = RowSum(TOKENS, here, r, r.token_part, 0)
+    enc_sum = RowSum(ENCODED, here, r, enc_part, 1)
+    act, d_gate, d_up = (r.token_part.at[pl.ds(n * rows, rows), pl.ds(0, band)] for n in range(3))
+
+    def send(make):
+        remote(*make()).start()
+        others.append(make)
+
+    def arrived(target, recv_sem):
+        pltpu.make_async_copy(target, target, recv_sem).wait()
 
     def load(n, source, target):
         copy = pltpu.make_async_copy(source, target, r.load_sem.at[n])
         copy.start()
         return copy
 
-    here.meet()
-    red.start_pair(GATE)
-    grad_two_load = load(0, r.grad_two_in, r.grad_two)
-    w_cout_load = load(1, r.w_two.at[3], r.weights.at[3])
+    def ffn_copies(n):
+        slot, part = n % 2, pl.ds(pl.multiple_of(n * band, band), band)
+        return [
+            pltpu.make_async_copy(r.w_gate.at[:, part], r.grad_self.at[slot, :, pl.ds(0, band)], r.f_sem.at[0, slot]),
+            pltpu.make_async_copy(r.w_up.at[:, part], r.grad_self.at[2 + slot, :, pl.ds(0, band)], r.f_sem.at[1, slot]),
+            pltpu.make_async_copy(r.w_down.at[part, :], r.grad_cross.at[slot, pl.ds(0, band), :], r.f_sem.at[2, slot]),
+        ]
+
+    def start_ffn(n):
+        for copy in ffn_copies(n):
+            copy.start()
+
+    cotangent_load = load(0, r.cotangent, r.grad_mixed)
+    normed_three_load = load(6, r.normed_three_in, r.normed)
+    start_ffn(0)
+    start_ffn(1)
+    hidden_two_load = load(11, r.hidden_two_in, r.hidden)
     mixed_load = load(2, r.mixed_cross_in, r.mixed)
     cqueries_load = load(3, r.cqueries_in, r.queries)
     ckeys_load = load(4, r.ckeys_in, ckeys)
     cvalues_load = load(5, r.cvalues_in, cvalues)
-    red.start_pair(UP)
-    red.start_pair(DOWN)
-    red.load_own(GATE)
-    red.load_own(DOWN)
+    here.meet()
+
+    def grad_result(part, step):
+        slots = place * rows + part.start + iota((step, 1), 0)
+        return jnp.where(slots < length, r.grad_mixed[part, :].astype(f32), 0.0)
+
+    cotangent_load.wait()
+
+    @row_steps(rows, 64)
+    def _(part):
+        r.branch[part, :] = grad_result(part, 64).astype(bf16)
+
+    normed_three_load.wait()
+
+    @pl.loop(0, 4)
+    def _(n):
+        slot = n % 2
+        for copy in ffn_copies(n):
+            copy.wait()
+        normed = r.normed[...]
+        branch = r.branch[...]
+        w_gate = r.grad_self[slot, :, 0:band]
+        w_up = r.grad_self[2 + slot, :, 0:band]
+        w_down = r.grad_cross[slot, 0:band, :]
+        gate_band = product(normed, w_gate)
+        up_band = product(normed, w_up)
+        inner = jnp.tanh(GELU_SCALE * (gate_band + GELU_CUBE * (gate_band * gate_band * gate_band)))
+        lifted = 0.5 * (1.0 + inner)
+        gelu = gate_band * lifted
+        slope = lifted + (0.5 * GELU_SCALE) * gate_band * (1.0 - inner * inner) * (
+            1.0 + (3.0 * GELU_CUBE) * (gate_band * gate_band)
+        )
+        act[...] = (gelu * up_band).astype(bf16)
+        grad_act = outer_rows(branch, w_down)
+        d_gate[...] = (grad_act * up_band * slope).astype(bf16)
+        d_up[...] = (grad_act * gelu).astype(bf16)
+        first = pl.ds(pl.multiple_of(n * band, band), band)
+        r.rows_both[first, :] = inner_rows(act[...], branch).astype(bf16)
+        r.grad_gate[n] = inner_rows(normed, d_gate[...]).astype(bf16)
+        r.grad_up[n] = inner_rows(normed, d_up[...]).astype(bf16)
+        down.start_pair(n)
+        gate.start_pair(n)
+        up.start_pair(n)
+        out = product(act[...], w_down)
+        gy = outer_rows(d_gate[...], w_gate) + outer_rows(d_up[...], w_up)
+
+        @pl.when(n == 0)
+        def _():
+            r.grad_two[...] = out
+            r.gy[...] = gy
+
+        @pl.when(n > 0)
+        def _():
+            r.grad_two[...] += out
+            r.gy[...] += gy
+
+        @pl.when(n < 2)
+        def _():
+            start_ffn(n + 2)
+
+    w_cout_load = load(1, r.w_two.at[3], r.grad_self.at[3])
+    w_two_loads = [load(8 + m, r.w_two.at[m], r.grad_self.at[m]) for m in range(3)]
+    encoded_load = load(7, r.enc_in, enc_all)
+    hidden_two_load.wait()
+    r.small[...] = jnp.zeros_like(r.small)
+
+    @row_steps(rows, 64)
+    def _(part):
+        hidden = r.hidden[part, :]
+        slots = place * rows + part.start + iota((64, 1), 0)
+        r.dq[part, :] = jnp.where(slots < length, hidden + r.grad_two[part, :], 0.0).astype(bf16)
+        grad, gain = norm_back_rows(hidden, r.gain_three[...], r.gy[part, :])
+        total = grad_result(part, 64) + grad
+        r.grad_two[part, :] = total
+        r.branch[part, :] = total.astype(bf16)
+        r.small[2:3, :] += gain
+
+    result_copy = load(13, r.dq, r.layer_out)
     normed_two_load = load(6, r.normed_two_in, r.normed)
-    encoded_load = load(7, r.enc_in, enc_all)
-    w_two_loads = [load(8 + m, r.w_two.at[m], r.weights.at[m]) for m in range(3)]
     hidden_load = load(11, r.hidden_one_in, r.hidden)
-    w_sout_load = load(12, r.w_one.at[3], r.weights.at[4])
-    keys_load = load(13, r.keys_in, r.keys)
-    values_load = load(14, r.values_in, r.values)
-
     fill_pads(r.pads, count)
     fill_fixed_bias(r.bias)
-
-    def to_branch():
-        @row_steps(rows)
-        def _(part):
-            r.branch[part, :] = r.grad_two[part, :].astype(bf16)
-
-    def store_grad_mixed(part, value):
-        r.grad_mixed[:, part] = value.astype(bf16)
-
-    def mixed_low():
-        @pl.loop(0, r.mixed.shape[0] // PAIR)
-        def _(n):
-            part = columns(n)
-            r.mixed_low[part, :] = r.mixed[part, :].astype(bf16)
-
-    grad_two_load.wait()
-    to_branch()
+    down.pair_sum()
+    down.start_planes()
     w_cout_load.wait()
-    times_turned(store_grad_mixed, r.branch, r.weights.at[3])
+    r.grad_mixed[...] = outer_rows(r.branch[...], r.grad_self[3]).astype(bf16)
+    w_sout_load = load(12, r.w_one.at[3], r.grad_self.at[3])
     mixed_load.wait()
-    mixed_low()
-    weight_grad(r.grad_cross.at[3], r.mixed_low, r.branch)
+    weight_grad_turned(r.grad_cross.at[3], r.mixed, r.branch)
+    gate.pair_sum()
+    gate.sides()
+    up.pair_sum()
+    up.sides()
     for copy in (cqueries_load, ckeys_load, cvalues_load):
         copy.wait()
-    cross_steps = {
-        1: [lambda: red.pair_sum(GATE)],
-        2: [lambda: red.pair_sum(UP)],
-        3: [lambda: red.pair_sum(DOWN)],
-    }
+    result_copy.wait()
+    down.pair_sent()
+    keys_load = load(13, r.keys_in, keys)
+    values_load = load(14, r.values_in, values)
+
+    def stepped(table, pair):
+        for when, steps in table.items():
+
+            @pl.when(pair == when)
+            def _(steps=steps):
+                for step in steps:
+                    step()
 
     @pl.loop(0, PAIRS)
     def _(pair):
@@ -920,79 +1092,32 @@
             r.grad_mixed.at[:, part], r.mixed.at[part, :], r.log_cross.at[pair],
             r.dq.at[:, part], dck.at[:, part], dcv.at[:, part], None, None, r.pads, None, r.kt_buf, None,
         )
-        for when, steps in cross_steps.items():
-
-            @pl.when(pair == when)
-            def _(steps=steps):
-                for step in steps:
-                    step()
 
     fill_pads(r.pads, length)
     mixed_self_load = load(15, r.mixed_self_in, r.mixed)
     queries_load = load(16, r.queries_in, r.queries)
     w_two_loads[0].wait()
-
-    def store_gy(part, value):
-        r.gy[:, part] = value
-
-    times_turned(store_gy, r.dq, r.weights.at[0])
-    red.first_side(GATE)
+    r.gy[...] = outer_rows(r.dq[...], r.grad_self[0])
     normed_two_load.wait()
-    r.normed_turned[...] = r.normed[...].T
-    weight_grad(r.grad_cross.at[0], r.normed_turned, r.dq)
+    weight_grad(r.grad_cross.at[0], r.normed, r.dq)
+    gate.first_side()
     encoded_load.wait()
-    turn(enc_turned, enc_all)
-    weight_grad(r.grad_cross.at[1], enc_turned, dck)
-    weight_grad(r.grad_cross.at[2], enc_turned, dcv)
-    red.start_pair(CROSS)
+    weight_grad(r.grad_cross.at[1], enc_all, dck)
+    weight_grad(r.grad_cross.at[2], enc_all, dcv)
+    for n in range(4):
+        cross.start_pair(n)
     w_two_loads[1].wait()
     w_two_loads[2].wait()
-
-    @pl.loop(0, (enc_count // BLOCK) * (enc_all.shape[1] // BLOCK))
-    def _(n):
-        across = enc_all.shape[1] // BLOCK
-        first = pl.ds(pl.multiple_of((n // across) * BLOCK, BLOCK), BLOCK)
-        second = pl.ds(pl.multiple_of((n % across) * BLOCK, BLOCK), BLOCK)
-        total = outer_rows(dck[first, :], r.weights[1, second, :])
-        total = total + outer_rows(dcv[first, :], r.weights[2, second, :])
-        enc_part[first, second] = total.astype(bf16)
-
+    enc_part[...] = (outer_rows(dck[...], r.grad_self[1]) + outer_rows(dcv[...], r.grad_self[2])).astype(bf16)
     quarters = ((here.along_x, here.to_x), (here.along_y, here.to_y), (here.corner, here.to_corner))
 
-    def send_rows(item, source, size):
-        makes = []
-        for k, (quarter, device) in enumerate(quarters):
-
-            def make(k=k, quarter=quarter, device=device):
-                return (
-                    source.at[pl.ds(quarter * size, size), :], r.rows_got[item].at[k],
-                    r.r_send.at[item, k], r.r_recv.at[item, k], device,
-                )
-
-            remote(*make()).start()
-            makes.append(make)
-        return makes
-
-    def sum_rows(item, source, size, store):
-        got = r.rows_got[item]
-        for k in range(3):
-            red.arrived(got.at[k], r.r_recv.at[item, k])
-
-        @row_steps(size)
-        def _(part):
-            start = pl.multiple_of(place * size + part.start, ROW_STEP)
-            total = source[pl.ds(start, ROW_STEP), :].astype(f32)
-            for k in range(3):
-                total = total + got[k, part, :].astype(f32)
-            store(part, total)
-
-    enc_rows = enc_count // 4
-    enc_sends = send_rows(1, enc_part, enc_rows)
+    def own_rows(ref, size, part, step):
+        return ref[pl.ds(pl.multiple_of(place * size + part.start, step), step), :].astype(f32)
+
+    enc_sum.sides()
     hidden_load.wait()
-    r.small[...] = jnp.zeros_like(r.small)
-    r.small[2:3, :] = r.grad_gain_three[...]
-
-    @row_steps(rows)
+
+    @row_steps(rows, 64)
     def _(part):
         grad, gain = norm_back_rows(r.hidden[part, :], r.gain_two[...], r.gy[part, :])
         total = r.grad_two[part, :] + grad
@@ -1001,11 +1126,9 @@
         r.small[1:2, :] += gain
 
     w_sout_load.wait()
-    times_turned(store_grad_mixed, r.branch, r.weights.at[4])
+    r.grad_mixed[...] = outer_rows(r.branch[...], r.grad_self[3]).astype(bf16)
     mixed_self_load.wait()
-    mixed_low()
-    weight_grad(r.grad_self.at[3], r.mixed_low, r.branch)
-    w_one_loads = [load(17 + m, r.w_one.at[m], r.weights.at[m]) for m in range(3)]
+    weight_grad_turned(r.grad_self.at[3], r.mixed, r.branch)
     for copy in (queries_load, keys_load, values_load):
         copy.wait()
 
@@ -1013,80 +1136,87 @@
         r.enc_total[part, :] = total
 
     def enc_done():
-        sum_rows(1, enc_part, enc_rows, keep_enc)
-        for make in enc_sends:
-            remote(*make()).wait_send()
+        enc_sum.total(keep_enc)
         pltpu.make_async_copy(r.enc_total, r.enc_sum, r.load_sem.at[20]).start()
 
+    def cross_sides():
+        cross.pair_sum()
+        cross.sides()
+
     def load_normed():
+        enc_sum.sent()
         pltpu.make_async_copy(r.normed_all_in, r.token_part, r.load_sem.at[21]).start()
 
-    def turn_normed():
-        pltpu.make_async_copy(r.normed_all_in, r.token_part, r.load_sem.at[21]).wait()
-        turn(r.rows_turned, r.token_part)
+    def w_one_copies():
+        return [
+            pltpu.make_async_copy(r.w_one.at[m], r.grad_cross.at[m], r.load_sem.at[17 + m]) for m in range(3)
+        ]
+
+    def load_w_one():
+        cross.pair_sent()
+        for copy in w_one_copies():
+            copy.start()
 
     self_steps = {
-        0: [lambda: red.first_side(UP), lambda: red.pair_sum(CROSS)],
-        1: [lambda: red.first_side(DOWN), enc_done, load_normed],
-        2: [lambda: red.second_side(GATE), turn_normed],
-        3: [lambda: red.second_side(UP)],
-        4: [lambda: red.second_side(DOWN), lambda: red.along_planes(GATE)],
-        5: [lambda: red.first_side(CROSS), lambda: red.along_planes(UP)],
+        0: [up.first_side, cross_sides],
+        1: [enc_sum.first_side, gate.second_side],
+        2: [down.along_planes, up.second_side],
+        3: [enc_done, load_normed],
+        4: [down.first_side, load_w_one],
+        5: [cross.first_side],
     }
 
     @pl.loop(0, PAIRS)
     def _(pair):
         part = columns(pair)
         backward_pair(
-            place, r.profile.at[pair], r.queries.at[:, part], r.keys.at[:, part],
-            r.values.at[:, part], r.grad_mixed.at[:, part], r.mixed.at[part, :],
+            place, r.profile.at[pair], r.queries.at[:, part], keys.at[:, part],
+            values.at[:, part], r.grad_mixed.at[:, part], r.mixed.at[part, :],
             r.log_self.at[pair], r.dq.at[:, part], r.dk.at[:, part], r.dv.at[:, part],
             r.near.at[pair], r.far.at[pair], r.pads, r.bias, r.kt_buf, r.grad_buf,
         )
-        for when, steps in self_steps.items():
-
-            @pl.when(pair == when)
-            def _(steps=steps):
-                for step in steps:
-                    step()
-
-    tokens_load = load(22, r.tokens_all_in, r.keys)
+        stepped(self_steps, pair)
+
+    tokens_load = load(22, r.tokens_all_in, keys)
+    pltpu.make_async_copy(r.normed_all_in, r.token_part, r.load_sem.at[21]).wait()
     own = pl.ds(pl.multiple_of(place * rows, BLOCK), rows)
-    weight_grad(r.grad_self.at[0], r.rows_turned.at[:, own], r.dq)
-    weight_grad(r.grad_self.at[1], r.rows_turned, r.dk)
-    weight_grad(r.grad_self.at[2], r.rows_turned, r.dv)
-    red.start_pair(SELF)
-    red.spread(GATE)
-    for copy in w_one_loads:
+    weight_grad(r.grad_self.at[0], r.token_part.at[own, :], r.dq)
+    weight_grad(r.grad_self.at[1], r.token_part, r.dk)
+    weight_grad(r.grad_self.at[2], r.token_part, r.dv)
+    for n in range(4):
+        self_one.start_pair(n)
+    for n in range(4):
+        self_two.start_pair(n)
+    for copy in w_one_copies():
         copy.wait()
 
-    @pl.loop(0, (count // BLOCK) * (r.dk.shape[1] // BLOCK))
-    def _(n):
-        across = r.dk.shape[1] // BLOCK
-        first = pl.ds(pl.multiple_of((n // across) * BLOCK, BLOCK), BLOCK)
-        second = pl.ds(pl.multiple_of((n % across) * BLOCK, BLOCK), BLOCK)
-        total = outer_rows(r.dk[first, :], r.weights[1, second, :])
-        total = total + outer_rows(r.dv[first, :], r.weights[2, second, :])
-        r.token_part[first, second] = total.astype(bf16)
-
-    times_turned(store_gy, r.dq, r.weights.at[0])
-    red.pair_sum(SELF)
-    red.started += send_rows(0, r.token_part, rows)
-    red.second_side(CROSS)
-    red.along_planes(DOWN)
-    red.spread(UP)
+    @row_steps(count, 512)
+    def _(part):
+        total = outer_rows(r.dk[part, :], r.grad_cross[1]) + outer_rows(r.dv[part, :], r.grad_cross[2])
+        r.token_part[part, :] = total.astype(bf16)
+
+    self_one.pair_sum()
+    self_one.sides()
+    self_two.pair_sum()
+    self_two.sides()
+    gate.along_planes()
+    down.second_side()
+    cross.second_side()
+    token_sum.sides()
+    r.gy[...] = outer_rows(r.dq[...], r.grad_cross[0])
+    up.along_planes()
     tokens_load.wait()
 
-    @row_steps(count)
+    @row_steps(count, 64)
     def _(part):
-        values = r.keys[part, :].astype(f32)
+        values = keys[part, :].astype(f32)
         scale = lax.rsqrt(jnp.mean(values * values, axis=-1, keepdims=True) + EPSILON)
         grad = r.token_part[part, :].astype(f32)
         r.small[0:1, :] += jnp.sum(grad * values * scale, axis=0, keepdims=True)
 
-    @row_steps(rows)
+    @row_steps(rows, 64)
     def _(part):
-        values = r.keys[pl.ds(pl.multiple_of(place * rows + part.start, ROW_STEP), ROW_STEP), :].astype(f32)
+        values = own_rows(keys, rows, part, 64)
         scale = lax.rsqrt(jnp.mean(values * values, axis=-1, keepdims=True) + EPSILON)
         r.small[0:1, :] += jnp.sum(r.gy[part, :] * values * scale, axis=0, keepdims=True)
 
@@ -1099,74 +1229,94 @@
         r.small[8 + 2 * pair : 10 + 2 * pair, 0 : table.shape[1]] = table
 
     small, small_core, small_seq, small_plane = r.small, r.small_core, r.small_seq, r.small_plane
-    s_send, s_recv = r.s_send, r.s_recv
-    red.send(lambda : (small, small_core, s_send.at[0], s_recv.at[0], here.partner))
-    red.finish(GATE)
-    red.first_side(SELF)
-    red.arrived(small_core, s_recv.at[0])
+    send(lambda: (small, small_core, r.s_send.at[0], r.s_recv.at[0], here.partner))
+    down.spread()
+    gate.spread()
+    self_one.first_side()
+    arrived(small_core, r.s_recv.at[0])
     small_seq[place] = small[...] + small_core[...]
     for k, (_, device) in enumerate(quarters):
-        red.send(lambda k=k, device=device: (small_seq.at[place], small_seq.at[place], s_send.at[1 + k], s_recv.at[1 + k], device))
-    red.along_planes(CROSS)
-    red.spread(DOWN)
-    red.finish(UP)
-    red.second_side(SELF)
+        send(
+            lambda k=k, device=device: (
+                small_seq.at[place], small_seq.at[place], r.s_send.at[1 + k], r.s_recv.at[1 + k], device
+            )
+        )
+    down.finish()
+    self_two.first_side()
+    token_sum.first_side()
+    cross.along_planes()
+    up.spread()
+    self_one.second_side()
     for k, (quarter, _) in enumerate(quarters):
-        red.arrived(small_seq.at[quarter], s_recv.at[1 + k])
+        arrived(small_seq.at[quarter], r.s_recv.at[1 + k])
     small_plane[here.plane] = (small_seq[0] + small_seq[1]) + (small_seq[2] + small_seq[3])
     for k in range(1, planes):
-        red.send(lambda k=k: (small_plane.at[here.plane], small_plane.at[here.plane],
-            s_send.at[3 + k], s_recv.at[3 + k], here.at_plane(here.ahead(k))))
+        send(
+            lambda k=k: (
+                small_plane.at[here.plane], small_plane.at[here.plane],
+                r.s_send.at[3 + k], r.s_recv.at[3 + k], here.at_plane(here.ahead(k)),
+            )
+        )
+    gate.finish()
+    self_two.second_side()
+    cross.spread()
+    up.finish()
+    self_one.along_planes()
+    cross.finish()
 
     def keep_tokens(part, total):
-        values = r.keys[pl.ds(pl.multiple_of(place * rows + part.start, ROW_STEP), ROW_STEP), :].astype(f32)
+        values = own_rows(keys, rows, part, 64)
         grad, _ = norm_back_rows(values, r.gain_one[...], r.gy[part, :] + total)
         r.hidden[part, :] = r.grad_two[part, :] + grad
 
-    sum_rows(0, r.token_part, rows, keep_tokens)
+    token_sum.total(keep_tokens)
     token_copy = pltpu.make_async_copy(r.hidden, r.grad_tokens, r.load_sem.at[23])
     token_copy.start()
-    red.spread(CROSS)
-    red.finish(DOWN)
     for k in range(1, planes):
-        red.arrived(small_plane.at[here.ahead(planes - k)], s_recv.at[3 + k])
+        arrived(small_plane.at[here.ahead(planes - k)], r.s_recv.at[3 + k])
     total = small_plane[0]
     for k in range(1, planes):
         total = total + small_plane[k]
     r.small_out[...] = total
-    red.along_planes(SELF)
-    red.finish(CROSS)
-    red.spread(SELF)
-    red.finish(SELF)
+    self_two.along_planes()
+    self_one.spread()
+    self_one.finish()
+    self_two.spread()
+    self_two.finish()
     token_copy.wait()
     pltpu.make_async_copy(r.enc_total, r.enc_sum, r.load_sem.at[20]).wait()
-    red.end()
+    for group in sums:
+        group.end()
+    token_sum.sent()
+    for make in others:
+        remote(*make()).wait_send()
 
 
 def backward_fused(shards, length, small, large):
-    kinds = make_kinds(shards)
+    stack, _, band, _, tall = make_kinds(shards)
     planes = lax.axis_size("fsdp") // 2
     lower = planes // 2
-    kinds = [kinds[n] for n in (2, 3, 4, 1, 0)]
-    shapes = full_shapes(kinds, planes)
+    first_rows = stack.rows // 2
+    parts = [StackRows(n * first_rows, first_rows, stack.cols) for n in range(2)]
+    kinds = [tall, band, band, stack, *parts]
     f32, low = jnp.float32, jnp.bfloat16
-    rows, width = large["grad_two_in"].shape
+    rows, width = large["cotangent"].shape
     count, enc_count = large["keys_in"].shape[0], large["ckeys_in"].shape[0]
     in_vmem = pl.BlockSpec(memory_space=pltpu.VMEM)
-    large["ffn_parts"] = [part.reshape(shape) for part, shape in zip(large["ffn_parts"], shapes)]
     in_layout, operands = flatten(dict(length=length), small, large)
     in_specs = [SCALARS] + [in_vmem] * len(small)
     in_specs += [ANYWHERE] * (len(operands) - len(in_specs))
     small_shape = (24, width)
 
-    def chunks(*lead):
-        return [pltpu.VMEM(lead + (kind.rows, kind.cols), low) for kind in kinds]
+    def chunk(kind, *lead):
+        return pltpu.VMEM(lead + (kind.rows, kind.cols), low)
 
     results = dict(
         out=[
             shaped((kind.rows, 4 * kind.cols) if isinstance(kind, Wide) else (4, kind.rows, kind.cols), low)
-            for kind in kinds
+            for kind in (tall, band, band, stack, stack)
         ],
+        layer_out=shaped((rows, width), low),
         grad_tokens=shaped((rows, width), f32),
         enc_sum=shaped((enc_count // 4, width), f32),
         small_out=shaped(small_shape, f32),
@@ -1175,46 +1325,43 @@
     square = (width, width)
     all_rows = pltpu.VMEM((count, width), low)
     some_rows = pltpu.VMEM((rows, width), low)
-    turned_rows = pltpu.VMEM((width, rows), low)
     wide_rows = pltpu.VMEM((rows, width), f32)
-    backward_buffers = backward_scratch(count)
+    half_tall = pltpu.VMEM((2, tall.rows, tall.cols // 2), low)
+    later = kinds[1:]
+    sides = [half_tall] + [chunk(kind, 2, lower) for kind in later]
+    row_sides = [pltpu.VMEM((2, size, width // 2), low) for size in (rows, enc_count // 4)]
+    buffers = backward_scratch(count)
     scratch = dict(
-        sums=chunks(4, planes),
-        side_x=chunks(2, lower),
-        side_y=chunks(2, lower),
-        last=chunks(2, lower),
-        from_z=chunks(planes - 1),
-        final=chunks(4),
-        stage_band=pltpu.VMEM((4, planes, kinds[GATE].rows, kinds[GATE].cols), low),
-        stage_tall=pltpu.VMEM((4, planes, kinds[DOWN].rows, kinds[DOWN].cols), low),
+        sums=[chunk(kind, 4, planes) for kind in kinds],
+        side_x=sides, side_y=sides, last=sides,
+        from_z=[chunk(tall, planes - 1, 4)] + [chunk(kind, planes - 1) for kind in later],
+        final=[chunk(kind, 4) for kind in kinds],
+        grad_gate=pltpu.VMEM((4, width, band.cols), low),
+        grad_up=pltpu.VMEM((4, width, band.cols), low),
         grad_cross=pltpu.VMEM((4,) + square, low),
         grad_self=pltpu.VMEM((4,) + square, low),
-        weights=pltpu.VMEM((5,) + square, low),
-        keys=all_rows, values=all_rows, dk=all_rows, dv=all_rows, token_part=all_rows,
-        rows_turned=pltpu.VMEM((width, count), low),
+        rows_both=pltpu.VMEM((2 * count, width), low),
+        dk=all_rows, dv=all_rows, token_part=all_rows,
         queries=some_rows, normed=some_rows, branch=some_rows, grad_mixed=some_rows, dq=some_rows,
-        mixed_low=turned_rows, normed_turned=turned_rows,
         grad_two=wide_rows, hidden=wide_rows, gy=wide_rows,
         mixed=pltpu.VMEM((width, rows), f32),
         enc_total=pltpu.VMEM((enc_count // 4, width), f32),
-        rows_got=[pltpu.VMEM((3, rows, width), low), pltpu.VMEM((3, enc_count // 4, width), low)],
-        pads=backward_buffers[0], bias=backward_buffers[1], kt_buf=backward_buffers[2],
-        grad_buf=backward_buffers[3],
+        row_x=row_sides, row_y=row_sides, row_last=row_sides,
+        pads=buffers[0], bias=buffers[1], kt_buf=buffers[2], grad_buf=buffers[3],
         near=pltpu.VMEM((PAIRS, 2, BLOCK), f32),
         far=pltpu.VMEM((PAIRS, 2, rows), f32),
         small=pltpu.VMEM(small_shape, f32),
         small_core=pltpu.VMEM(small_shape, f32),
         small_seq=pltpu.VMEM((4,) + small_shape, f32),
         small_plane=pltpu.VMEM((planes,) + small_shape, f32),
-        own_sem=DMA((3, 4)),
-        c_send=DMA((5, 4)), c_recv=DMA((5, 4)),
-        a_send=DMA((5, 4)), a_recv=DMA((5, 4)),
-        b_send=DMA((5, 2)), b_recv=DMA((5, 2)),
-        z_send=DMA((5, planes - 1)), z_recv=DMA((5, planes - 1)),
-        g_send=DMA((5, 4)), g_recv=DMA((5, 4)),
-        r_send=DMA((2, 3)), r_recv=DMA((2, 3)),
+        f_sem=DMA((3, 2)),
+        c_send=DMA((GROUPS, 4)), c_recv=DMA((GROUPS, 4)),
+        a_send=DMA((GROUPS + 2, 4)), a_recv=DMA((GROUPS + 2, 4)),
+        b_send=DMA((GROUPS + 2, 2)), b_recv=DMA((GROUPS + 2, 2)),
+        z_send=DMA((GROUPS, planes - 1)), z_recv=DMA((GROUPS, planes - 1)),
+        g_send=DMA((GROUPS, 4)), g_recv=DMA((GROUPS, 4)),
         s_send=DMA((3 + planes,)), s_recv=DMA((3 + planes,)),
-        out_sem=DMA((5, 4)), load_sem=DMA((24,)),
+        out_sem=DMA((GROUPS, 4)), load_sem=DMA((24,)),
     )
     scratch_layout, scratch_shapes = flatten(scratch)
     outs = pl.pallas_call(
@@ -1224,14 +1371,14 @@
         out_shape=out_shapes,
         scratch_shapes=scratch_shapes,
         compiler_params=pltpu.CompilerParams(
-            collective_id=1, has_side_effects=True, vmem_limit_bytes=66_000_000
+            collective_id=1, has_side_effects=True, vmem_limit_bytes=67_000_000
         ),
         name="backward_fused",
     )(*operands)
     got = Space(out_layout, outs)
     grads = [got.out[SELF][m] for m in range(4)] + [got.out[CROSS][m] for m in range(4)]
     grads += [got.out[GATE], got.out[UP], got.out[DOWN].reshape(-1, width)]
-    return [grad.astype(f32) for grad in grads], got.grad_tokens, got.enc_sum, got.small_out
+    return got.layer_out, [grad.astype(f32) for grad in grads], got.grad_tokens, got.enc_sum, got.small_out
 
 
 ONE, TWO, GATE_IN, UP_IN, DOWN_IN = range(5)
@@ -1424,13 +1571,11 @@
         return (values * scale * gain[...]).astype(bf16)
 
     def project(out, left, weight):
-        across = weight.shape[1] // BLOCK
-
-        @pl.loop(0, (left.shape[0] // BLOCK) * across)
-        def _(n):
-            first = pl.ds(pl.multiple_of((n // across) * BLOCK, BLOCK), BLOCK)
-            second = pl.ds(pl.multiple_of((n % across) * BLOCK, BLOCK), BLOCK)
-            out[first, second] = product(left[first, :], weight[:, second]).astype(out.dtype)
+        step = min(left.shape[0], 512)
+
+        @row_steps(left.shape[0], step)
+        def _(part):
+            out[part, :] = product(left[part, :], weight[...]).astype(out.dtype)
 
     here.meet()
     rows_start(0)
@@ -1447,7 +1592,7 @@
     rows_turn(1)
     rows_done(0)
 
-    @row_steps(count)
+    @row_steps(count, 128)
     def _(part):
         r.normed[part, :] = norm_rows(r.source_rows[part, :].astype(f32), r.gain_one)
 
@@ -1492,10 +1637,10 @@
     store(7, r.turned_one, r.mixed_self_turned)
     project(r.hidden, r.mixed, r.weights_one.at[3])
 
-    @row_steps(rows)
+    @row_steps(rows, 64)
     def _(part):
-        start = pl.multiple_of(place * rows + part.start, ROW_STEP)
-        total = r.hidden[part, :] + r.source_rows[pl.ds(start, ROW_STEP), :].astype(f32)
+        start = pl.multiple_of(place * rows + part.start, 64)
+        total = r.hidden[part, :] + r.source_rows[pl.ds(start, 64), :].astype(f32)
         r.hidden[part, :] = total
         r.normed_rows[part, :] = norm_rows(total, r.gain_two)
 
@@ -1529,7 +1674,7 @@
     gather.from_sides(DOWN_IN)
     project(r.hidden_last, r.cmixed, r.weights_two.at[3])
 
-    @row_steps(rows)
+    @row_steps(rows, 64)
     def _(part):
         total = r.hidden_last[part, :] + r.hidden[part, :]
         r.hidden_last[part, :] = total
@@ -1637,34 +1782,54 @@
     place = jnp.stack([seq_place.astype(jnp.int32), length])
 
     source = tokens[0].astype(f32)
-    fit = kernels_fit(shards)
-    if fit:
+    if kernels_fit(shards):
         forward = forward_fused(
             shards, lengths, tokens[0], encoded[0],
             dict(
                 profile=profile, gain_one=gain_one[None], gain_two=gain_two[None], gain_three=gain_three[None]
             ),
         )
+        one_hot_wide = jnp.pad(one_hot.astype(f32), ((0, 0), (0, PAIR - BUCKETS)))
         width = source.shape[1]
-        hidden_two, normed_three = forward.hidden_two, forward.normed_three
         w_gate, w_up, w_down = (full.reshape(-1, full.shape[-1]) for full in forward.ffn_full)
-    else:
-        weights, tokens_all, enc_all = gather_plain(shards, tokens[0], encoded[0])
-        (w_query, w_key, w_value, w_sout, w_cquery, w_ckey, w_cvalue, w_cout, w_gate, w_up, w_down) = weights
-        normed_all = rms_scale(tokens_all.astype(f32), gain_one).astype(bf16)
-        normed_one = rms_scale(source, gain_one).astype(bf16)
-        queries = product(normed_one, w_query).astype(bf16)
-        keys = product(normed_all, w_key).astype(bf16)
-        values = product(normed_all, w_value).astype(bf16)
-        mixed_self, mixed_self_turned, log_self = self_forward(place, profile, queries, keys, values)
-        hidden_one = source + product(mixed_self, w_sout)
-        normed_two = rms_scale(hidden_one, gain_two).astype(bf16)
-        cqueries = product(normed_two, w_cquery).astype(bf16)
-        ckeys = product(enc_all, w_ckey).astype(bf16)
-        cvalues = product(enc_all, w_cvalue).astype(bf16)
-        mixed_cross, mixed_cross_turned, log_cross = cross_forward(cqueries, ckeys, cvalues)
-        hidden_two = hidden_one + product(mixed_cross, w_cout)
-        normed_three = rms_scale(hidden_two, gain_three).astype(bf16)
+        layer_out, grads, grad_tokens, enc_sum, small = backward_fused(
+            shards, lengths,
+            dict(
+                profile=profile, log_cross=forward.log_cross, log_self=forward.log_self,
+                gain_one=gain_one[None], gain_two=gain_two[None], gain_three=gain_three[None],
+                one_hot=one_hot_wide,
+            ),
+            dict(
+                cotangent=cotangent[0], w_gate=w_gate, w_up=w_up, w_down=w_down,
+                normed_three_in=forward.normed_three, hidden_two_in=forward.hidden_two,
+                w_one=forward.w_one, w_two=forward.w_two, mixed_cross_in=forward.mixed_cross_turned,
+                cqueries_in=forward.cqueries, ckeys_in=forward.ckeys, cvalues_in=forward.cvalues,
+                normed_two_in=forward.normed_two, enc_in=forward.enc_all, hidden_one_in=forward.hidden_one,
+                mixed_self_in=forward.mixed_self_turned, queries_in=forward.queries, keys_in=forward.keys,
+                values_in=forward.values, normed_all_in=forward.normed_all,
+                tokens_all_in=forward.tokens_all,
+            ),
+        )
+        table_sum = small[8 : 8 + HEADS, :BUCKETS].T
+        return (
+            layer_out[None], grad_tokens[None], enc_sum[None], small[0], small[1], small[2], table_sum, *grads
+        )
+    weights, tokens_all, enc_all = gather_plain(shards, tokens[0], encoded[0])
+    (w_query, w_key, w_value, w_sout, w_cquery, w_ckey, w_cvalue, w_cout, w_gate, w_up, w_down) = weights
+    normed_all = rms_scale(tokens_all.astype(f32), gain_one).astype(bf16)
+    normed_one = rms_scale(source, gain_one).astype(bf16)
+    queries = product(normed_one, w_query).astype(bf16)
+    keys = product(normed_all, w_key).astype(bf16)
+    values = product(normed_all, w_value).astype(bf16)
+    mixed_self, mixed_self_turned, log_self = self_forward(place, profile, queries, keys, values)
+    hidden_one = source + product(mixed_self, w_sout)
+    normed_two = rms_scale(hidden_one, gain_two).astype(bf16)
+    cqueries = product(normed_two, w_cquery).astype(bf16)
+    ckeys = product(enc_all, w_ckey).astype(bf16)
+    cvalues = product(enc_all, w_cvalue).astype(bf16)
+    mixed_cross, mixed_cross_turned, log_cross = cross_forward(cqueries, ckeys, cvalues)
+    hidden_two = hidden_one + product(mixed_cross, w_cout)
+    normed_three = rms_scale(hidden_two, gain_three).astype(bf16)
     gate = product(normed_three, w_gate)
     up = product(normed_three, w_up)
 
@@ -1689,29 +1854,6 @@
         hidden_two, gain_three, outer_rows(grad_gate, w_gate) + outer_rows(grad_up, w_up)
     )
     grad_two = grad_result + grad_three
-    if fit:
-        one_hot_wide = jnp.pad(one_hot.astype(f32), ((0, 0), (0, PAIR - BUCKETS)))
-        grads, grad_tokens, enc_sum, small = backward_fused(
-            shards, lengths,
-            dict(
-                profile=profile, log_cross=forward.log_cross, log_self=forward.log_self,
-                gain_one=gain_one[None], gain_two=gain_two[None], grad_gain_three=grad_gain_three[None],
-                one_hot=one_hot_wide,
-            ),
-            dict(
-                ffn_parts=[g_gate, g_up, g_down], w_one=forward.w_one, w_two=forward.w_two,
-                grad_two_in=grad_two, mixed_cross_in=forward.mixed_cross_turned,
-                cqueries_in=forward.cqueries, ckeys_in=forward.ckeys, cvalues_in=forward.cvalues,
-                normed_two_in=forward.normed_two, enc_in=forward.enc_all, hidden_one_in=forward.hidden_one,
-                mixed_self_in=forward.mixed_self_turned, queries_in=forward.queries, keys_in=forward.keys,
-                values_in=forward.values, normed_all_in=forward.normed_all,
-                tokens_all_in=forward.tokens_all,
-            ),
-        )
-        table_sum = small[8 : 8 + HEADS, :BUCKETS].T
-        return (
-            result[None], grad_tokens[None], enc_sum[None], small[0], small[1], small[2], table_sum, *grads
-        )
     branch_cross = grad_two.astype(bf16)
     g_cout = inner_rows(mixed_cross, branch_cross).astype(bf16)
     grad_mixed_cross = outer_rows(branch_cross, w_cout).astype(bf16)

time: 305 us -> 258 us (0.85)
  matrix products: 23.9 us -> 0.22 us
  Pallas kernels: 261 us -> 238 us
    pallas_call x1, Pallas kernels: 167 us -> 146 us  [backward_fused(): pl.pallas_call(functools.partial(backward_kernel, kinds, planes, in_layou...]
    dot_general x6 -> x0, matrix products: 15.4 us -> none  [the longest x3 8.16 us: outer_rows(): lax.dot_general(left, right, (((1,), (1,)), ((), ())), preferred_element_...]
    dot_general x4 -> x1, matrix products: 8.52 us -> 0.22 us  [inner_rows(): lax.dot_general(left, right, (((0,), (0,)), ((), ())), preferred_element_...]
where the time goes in v3:
time: 258 us
  Pallas kernels  238 us (92%)
  local copies, waits for them, and re-layouts  9.67 us (4%)
  other arithmetic  8.11 us (3%)
    pallas_call x1, Pallas kernels, backward_fused(): pl.pallas_call(functools.partial(backward_kernel, kinds, planes, in_layou...  146 us
    pallas_call x1, Pallas kernels, forward_fused(): pl.pallas_call(functools.partial(forward_kernel, kinds, planes, in_layout...  92.2 us
    convert_element_type x4, other arithmetic, backward_fused(): grad.astype(f32)  7.33 us

profile of v3, /device:TPU:0, one launch (start us, length us, event | category | flops | bytes accessed | tf_op | source)
XLA Modules:
  0.0 257.6 jit_solution(39646492186885314)
XLA Ops:
  0.7 0.0 copy-start
  1.4 1.3 reshape.137.refs_2_.refs_4_
  2.6 1.3 reshape.138.refs_3_.refs_5_
  3.9 1.3 reshape.139.refs_4_.refs_6_
  5.1 0.0 copy-done
  5.1 0.2 convolution_bitcast_fusion
  5.4 0.6 reshape.133.refs_1_
  6.0 0.1 fusion
  6.1 0.7 pad_convert_fusion.refs_7_
  6.8 92.2 %forward_fused.1 = (bf16[4,768,768]{2,1,0:T(8,128)(2,1)}, bf16[4,768,768]{2,1,0:T(8,128)(2,1)}, bf16[4,2,96,2048]{3,2,1,0:T(8,128)(2,1)}, bf16[4,2,96,2048]{3,2,...) custom-call(s32[1]{0:T(128)S(6)} %copy.40.refs_0_, ...), custom_call_target="tpu_custom_call" | custom-call | tf_op jit(solution)/shard_map/forward_fused/pallas_call | solution.py:1748
  99.0 145.9 %backward_fused.1 = (bf16[4,64,768]{2,1,0:T(8,128)(2,1)}, bf16[96,2048]{1,0:T(8,128)(2,1)}, bf16[96,2048]{1,0:T(8,128)(2,1)}, bf16[4,96,768]{2,1,0:T(8,128)(2,1)...) custom-call(s32[1]{0:T(128)S(6)} %copy.40.refs_0_, ...), custom_call_target="tpu_custom_call" | custom-call | tf_op jit(solution)/shard_map/backward_fused/pallas_call | solution.py:1367
  245.0 0.0 copy-start.2
  245.0 0.0 copy-start.3
  245.0 1.4 slice_bitcast_fusion
  246.4 1.5 slice_reduce_fusion
  247.8 1.9 convert_element_type.236
  249.8 0.0 copy-start.5
  249.8 0.0 copy-start.1
  249.8 2.0 convert_element_type.237
  251.8 1.9 bitcast_convert_fusion
  253.8 0.0 copy-done.2
  253.8 0.0 copy-done.3
  253.8 0.0 copy-start.4
  253.8 1.4 bitcast_convert_fusion.1
  255.2 0.0 copy-done.5
  255.2 0.7 copy.41
  255.9 0.0 copy-done.1
  255.9 0.9 copy.42
  256.8 0.0 copy-done.4
  256.8 0.7 copy.43
  (1 shorter events, 0.0 us)
Async XLA Ops:
  0.7 4.5 %copy-start = (bf16[32,12]{0,1:T(8,128)(2,1)S(1)}, bf16[32,12]{0,1:T(8,128)(2,1)}, u32[]{:S(2)}) copy-start(bf16[32,12]{0,1:T(8,128)(2,1)} %param.26) | copy-start | bytes 2308
  245.0 8.8 %copy-start.2 = (bf16[4,96,768]{2,1,0:T(8,128)(2,1)S(1)}, bf16[4,96,768]{2,1,0:T(8,128)(2,1)}, u32[]{:S(2)}) copy-start(bf16[4,96,768]{2,1,0:T(8,128)(2,1)} %get-tuple-element.76) | copy-start | bytes 1769476
  245.0 8.8 %copy-start.3 = (bf16[4,96,768]{2,1,0:T(8,128)(2,1)S(1)}, bf16[4,96,768]{2,1,0:T(8,128)(2,1)}, u32[]{:S(2)}) copy-start(bf16[4,96,768]{2,1,0:T(8,128)(2,1)} %get-tuple-element.75) | copy-start | bytes 1769476
  249.8 5.4 %copy-start.5 = (bf16[256,768]{1,0:T(8,128)(2,1)S(1)}, bf16[256,768]{1,0:T(8,128)(2,1)}, u32[]{:S(2)}) copy-start(bf16[256,768]{1,0:T(8,128)(2,1)} %get-tuple-element.71) | copy-start | bytes 1179652
  249.8 6.1 %copy-start.1 = (f32[256,768]{1,0:T(8,128)S(1)}, f32[256,768]{1,0:T(8,128)}, u32[]{:S(2)}) copy-start(f32[256,768]{1,0:T(8,128)} %get-tuple-element.72) | copy-start | bytes 2359300
  253.8 3.1 %copy-start.4 = (f32[128,768]{1,0:T(8,128)S(1)}, f32[128,768]{1,0:T(8,128)}, u32[]{:S(2)}) copy-start(f32[128,768]{1,0:T(8,128)} %get-tuple-element.73) | copy-start | bytes 1179652

commit v4 on v3

--- a/solution.py
+++ b/solution.py
@@ -463,12 +463,13 @@
             self.at_plane(self.ahead(k)) for k in range(1, self.planes)
         ]
 
+    def greet(self):
+        barrier = pltpu.get_barrier_semaphore()
+        for other in self.everyone():
+            pl.semaphore_signal(barrier, inc=1, device_id=other, device_id_type=MESH)
+
     def meet(self):
-        barrier = pltpu.get_barrier_semaphore()
-        others = self.everyone()
-        for other in others:
-            pl.semaphore_signal(barrier, inc=1, device_id=other, device_id_type=MESH)
-        pl.semaphore_wait(barrier, len(others))
+        pl.semaphore_wait(pltpu.get_barrier_semaphore(), len(self.everyone()))
 
 
 def remote(source, target, send_sem, recv_sem, device):
@@ -574,10 +575,10 @@
 
 
 def add_low(target, *terms):
-    total = target[...].astype(jnp.float32)
+    total = target[...]
     for term in terms:
-        total = total + term[...].astype(jnp.float32)
-    target[...] = total.astype(jnp.bfloat16)
+        total = total + term[...]
+    target[...] = total
 
 
 def reduce_plain(grads, token_part, enc_part, small):
@@ -683,14 +684,43 @@
         source, target = self.pair_source(n, 1 - self.here.core)
         remote(source, target, r.c_send.at[g, n], r.c_recv.at[g, n], self.here.partner).start()
 
+    def pair_part(self, n):
+        source, target = self.pair_source(n, self.here.core)
+        self.arrived(target, self.r.c_recv.at[self.g, n])
+
+        @pl.loop(0, 4)
+        def _(m):
+            add_low(target.at[m], source.at[m])
+
+        self.send_part(n)
+
     def pair_sum(self):
-        for n in range(4):
-            source, target = self.pair_source(n, self.here.core)
-            self.arrived(target, self.r.c_recv.at[self.g, n])
-
-            @pl.loop(0, 4)
-            def _(m, n=n, source=source, target=target):
-                add_low(target.at[m], source.at[m])
+        @pl.loop(0, 4)
+        def _(n):
+            self.pair_part(n)
+
+        self.sent_parts()
+
+    def parts_sends(self):
+        r, g, here = self.r, self.g, self.here
+        for n, quarter in enumerate((here.along_x, here.corner)):
+            yield quarter, lambda n=n, quarter=quarter: (
+                self.half(quarter, 0), self.side_x.at[n], r.a_send.at[g, n], r.a_recv.at[g, n], here.to_x
+            )
+        for n, quarter in enumerate((here.along_y, here.corner)):
+            yield quarter, lambda n=n, quarter=quarter: (
+                self.half(quarter, 1), self.side_y.at[n], r.a_send.at[g, 2 + n], r.a_recv.at[g, 2 + n], here.to_y
+            )
+
+    def send_part(self, n):
+        for part, make in self.parts_sends():
+
+            @pl.when(n == part)
+            def _(make=make):
+                remote(*make()).start()
+
+    def sent_parts(self):
+        self.started += [make for _, make in self.parts_sends()]
 
     def pair_sent(self):
         for n in range(4):
@@ -704,20 +734,8 @@
         return self.sums.at[quarter, pl.ds(second * size, size)]
 
     def sides(self):
-        r, g, here = self.r, self.g, self.here
-        for n, quarter in enumerate((here.along_x, here.corner)):
-            self.send(
-                lambda n=n, quarter=quarter: (
-                    self.half(quarter, 0), self.side_x.at[n], r.a_send.at[g, n], r.a_recv.at[g, n], here.to_x
-                )
-            )
-        for n, quarter in enumerate((here.along_y, here.corner)):
-            self.send(
-                lambda n=n, quarter=quarter: (
-                    self.half(quarter, 1), self.side_y.at[n],
-                    r.a_send.at[g, 2 + n], r.a_recv.at[g, 2 + n], here.to_y,
-                )
-            )
+        for _, make in Sum.parts_sends(self):
+            self.send(make)
 
     def add_half(self, quarter, second, terms, out=None):
         size = self.planes // 2
@@ -754,15 +772,17 @@
     def plane_share(self, plane):
         return self.sums.at[self.here.seq, plane]
 
-    def start_planes(self):
+    def plane_sends(self):
         r, g, here = self.r, self.g, self.here
         for k in range(1, self.planes):
-            self.send(
-                lambda k=k: (
-                    self.plane_share(here.ahead(k)), self.from_z.at[k - 1],
-                    r.z_send.at[g, k - 1], r.z_recv.at[g, k - 1], here.at_plane(here.ahead(k)),
-                )
+            yield here.ahead(k), lambda k=k: (
+                self.plane_share(here.ahead(k)), self.from_z.at[k - 1],
+                r.z_send.at[g, k - 1], r.z_recv.at[g, k - 1], here.at_plane(here.ahead(k)),
             )
+
+    def start_planes(self):
+        for _, make in self.plane_sends():
+            self.send(make)
 
     def along_planes(self):
         r, g, here = self.r, self.g, self.here
@@ -846,6 +866,9 @@
 
     def plane_share(self, plane):
         return self.sums.at[:, plane]
+
+    def parts_sends(self):
+        return self.plane_sends()
 
     def along_planes(self):
         r, g, here = self.r, self.g, self.here
@@ -967,6 +990,7 @@
         for copy in ffn_copies(n):
             copy.start()
 
+    here.greet()
     cotangent_load = load(0, r.cotangent, r.grad_mixed)
     normed_three_load = load(6, r.normed_three_in, r.normed)
     start_ffn(0)
@@ -976,7 +1000,6 @@
     cqueries_load = load(3, r.cqueries_in, r.queries)
     ckeys_load = load(4, r.ckeys_in, ckeys)
     cvalues_load = load(5, r.cvalues_in, cvalues)
-    here.meet()
 
     def grad_result(part, step):
         slots = place * rows + part.start + iota((step, 1), 0)
@@ -1016,6 +1039,11 @@
         r.rows_both[first, :] = inner_rows(act[...], branch).astype(bf16)
         r.grad_gate[n] = inner_rows(normed, d_gate[...]).astype(bf16)
         r.grad_up[n] = inner_rows(normed, d_up[...]).astype(bf16)
+
+        @pl.when(n == 0)
+        def _():
+            here.meet()
+
         down.start_pair(n)
         gate.start_pair(n)
         up.start_pair(n)
@@ -1036,6 +1064,11 @@
         def _():
             start_ffn(n + 2)
 
+        @pl.when(n > 0)
+        def _():
+            for group in (down, gate, up):
+                group.pair_part(n - 1)
+
     w_cout_load = load(1, r.w_two.at[3], r.grad_self.at[3])
     w_two_loads = [load(8 + m, r.w_two.at[m], r.grad_self.at[m]) for m in range(3)]
     encoded_load = load(7, r.enc_in, enc_all)
@@ -1047,7 +1080,7 @@
         hidden = r.hidden[part, :]
         slots = place * rows + part.start + iota((64, 1), 0)
         r.dq[part, :] = jnp.where(slots < length, hidden + r.grad_two[part, :], 0.0).astype(bf16)
-        grad, gain = norm_back_rows(hidden, r.gain_three[...], r.gy[part, :])
+        grad, gain = norm_back_rows(hidden, r.gains[2:3, :], r.gy[part, :])
         total = grad_result(part, 64) + grad
         r.grad_two[part, :] = total
         r.branch[part, :] = total.astype(bf16)
@@ -1058,17 +1091,14 @@
     hidden_load = load(11, r.hidden_one_in, r.hidden)
     fill_pads(r.pads, count)
     fill_fixed_bias(r.bias)
-    down.pair_sum()
-    down.start_planes()
+    for group in (down, gate, up):
+        group.pair_part(3)
+        group.sent_parts()
     w_cout_load.wait()
     r.grad_mixed[...] = outer_rows(r.branch[...], r.grad_self[3]).astype(bf16)
     w_sout_load = load(12, r.w_one.at[3], r.grad_self.at[3])
     mixed_load.wait()
     weight_grad_turned(r.grad_cross.at[3], r.mixed, r.branch)
-    gate.pair_sum()
-    gate.sides()
-    up.pair_sum()
-    up.sides()
     for copy in (cqueries_load, ckeys_load, cvalues_load):
         copy.wait()
     result_copy.wait()
@@ -1119,7 +1149,7 @@
 
     @row_steps(rows, 64)
     def _(part):
-        grad, gain = norm_back_rows(r.hidden[part, :], r.gain_two[...], r.gy[part, :])
+        grad, gain = norm_back_rows(r.hidden[part, :], r.gains[1:2, :], r.gy[part, :])
         total = r.grad_two[part, :] + grad
         r.grad_two[part, :] = total
         r.branch[part, :] = total.astype(bf16)
@@ -1141,7 +1171,6 @@
 
     def cross_sides():
         cross.pair_sum()
-        cross.sides()
 
     def load_normed():
         enc_sum.sent()
@@ -1196,9 +1225,7 @@
         r.token_part[part, :] = total.astype(bf16)
 
     self_one.pair_sum()
-    self_one.sides()
     self_two.pair_sum()
-    self_two.sides()
     gate.along_planes()
     down.second_side()
     cross.second_side()
@@ -1266,7 +1293,7 @@
 
     def keep_tokens(part, total):
         values = own_rows(keys, rows, part, 64)
-        grad, _ = norm_back_rows(values, r.gain_one[...], r.gy[part, :] + total)
+        grad, _ = norm_back_rows(values, r.gains[0:1, :], r.gy[part, :] + total)
         r.hidden[part, :] = r.grad_two[part, :] + grad
 
     token_sum.total(keep_tokens)
@@ -1568,7 +1595,7 @@
 
     def norm_rows(values, gain):
         scale = lax.rsqrt(jnp.mean(values * values, axis=-1, keepdims=True) + EPSILON)
-        return (values * scale * gain[...]).astype(bf16)
+        return (values * scale * gain).astype(bf16)
 
     def project(out, left, weight):
         step = min(left.shape[0], 512)
@@ -1577,6 +1604,7 @@
         def _(part):
             out[part, :] = product(left[part, :], weight[...]).astype(out.dtype)
 
+    here.greet()
     here.meet()
     rows_start(0)
     gather.start_planes(ONE)
@@ -1594,7 +1622,7 @@
 
     @row_steps(count, 128)
     def _(part):
-        r.normed[part, :] = norm_rows(r.source_rows[part, :].astype(f32), r.gain_one)
+        r.normed[part, :] = norm_rows(r.source_rows[part, :].astype(f32), r.gains[0:1, :])
 
     store(0, r.source_rows, r.tokens_all)
     store(1, r.normed, r.normed_all)
@@ -1642,7 +1670,7 @@
         start = pl.multiple_of(place * rows + part.start, 64)
         total = r.hidden[part, :] + r.source_rows[pl.ds(start, 64), :].astype(f32)
         r.hidden[part, :] = total
-        r.normed_rows[part, :] = norm_rows(total, r.gain_two)
+        r.normed_rows[part, :] = norm_rows(total, r.gains[1:2, :])
 
     store(8, r.hidden, r.hidden_one)
     store(9, r.normed_rows, r.normed_two)
@@ -1678,7 +1706,7 @@
     def _(part):
         total = r.hidden_last[part, :] + r.hidden[part, :]
         r.hidden_last[part, :] = total
-        r.normed_last[part, :] = norm_rows(total, r.gain_three)
+        r.normed_last[part, :] = norm_rows(total, r.gains[2:3, :])
 
     store(15, r.hidden_last, r.hidden_two)
     store(16, r.normed_last, r.normed_three)
@@ -1783,10 +1811,11 @@
 
     source = tokens[0].astype(f32)
     if kernels_fit(shards):
+        gains = jnp.stack([gain_one, gain_two, gain_three])
         forward = forward_fused(
             shards, lengths, tokens[0], encoded[0],
             dict(
-                profile=profile, gain_one=gain_one[None], gain_two=gain_two[None], gain_three=gain_three[None]
+                profile=profile, gains=gains
             ),
         )
         one_hot_wide = jnp.pad(one_hot.astype(f32), ((0, 0), (0, PAIR - BUCKETS)))
@@ -1796,8 +1825,7 @@
             shards, lengths,
             dict(
                 profile=profile, log_cross=forward.log_cross, log_self=forward.log_self,
-                gain_one=gain_one[None], gain_two=gain_two[None], gain_three=gain_three[None],
-                one_hot=one_hot_wide,
+                gains=gains, one_hot=one_hot_wide,
             ),
             dict(
                 cotangent=cotangent[0], w_gate=w_gate, w_up=w_up, w_down=w_down,

time: 258 us -> 254 us (0.984)
  Pallas kernels: 238 us -> 234 us
    pallas_call x1, Pallas kernels: 146 us -> 142 us  [backward_fused(): pl.pallas_call(functools.partial(backward_kernel, kinds, planes, in_layou...]
    broadcast_in_dim x3 -> x0, local copies, waits for them, and re-layouts: 3.79 us -> none  [the longest x1 1.26 us: local(): gain_one[None]]
where the time goes in v4:
time: 254 us; the launch traced here: 252 us
  Pallas kernels  234 us (92%)
  other arithmetic  8.73 us (3%)
  local copies, waits for them, and re-layouts  7.94 us (3%)
    pallas_call x1, Pallas kernels, backward_fused(): pl.pallas_call(functools.partial(backward_kernel, kinds, planes, in_layou...  142 us
    pallas_call x1, Pallas kernels, forward_fused(): pl.pallas_call(functools.partial(forward_kernel, kinds, planes, in_layout...  92.2 us
    convert_element_type x4, other arithmetic, backward_fused(): grad.astype(f32)  7.33 us

profile of v4, /device:TPU:0, one launch (start us, length us, event | category | flops | bytes accessed | tf_op | source)
XLA Modules:
  0.0 252.3 jit_solution(2776987785328102306)
XLA Ops:
  0.7 0.0 copy-start
  1.4 0.7 stack.17
  2.0 0.7 stack.18
  2.7 0.7 stack.19
  3.4 0.6 maximum_convert_fusion.refs_2_.refs_4_
  4.0 0.0 copy-done
  4.0 0.2 convolution_bitcast_fusion
  4.2 0.6 reshape.133.refs_1_
  4.9 0.1 fusion
  5.0 0.7 pad_convert_fusion.refs_5_
  5.6 92.2 %forward_fused.1 = (bf16[4,768,768]{2,1,0:T(8,128)(2,1)}, bf16[4,768,768]{2,1,0:T(8,128)(2,1)}, bf16[4,2,96,2048]{3,2,1,0:T(8,128)(2,1)}, bf16[4,2,96,2048]{3,2,...) custom-call(s32[1]{0:T(128)S(6)} %copy.40.refs_0_, ...), custom_call_target="tpu_custom_call" | custom-call | tf_op jit(solution)/shard_map/forward_fused/pallas_call | solution.py:1776
  97.9 141.8 %backward_fused.1 = (bf16[4,64,768]{2,1,0:T(8,128)(2,1)}, bf16[96,2048]{1,0:T(8,128)(2,1)}, bf16[96,2048]{1,0:T(8,128)(2,1)}, bf16[4,96,768]{2,1,0:T(8,128)(2,1)...) custom-call(s32[1]{0:T(128)S(6)} %copy.40.refs_0_, ...), custom_call_target="tpu_custom_call" | custom-call | tf_op jit(solution)/shard_map/backward_fused/pallas_call | solution.py:1394
  239.7 0.0 copy-start.2
  239.7 0.0 copy-start.3
  239.7 1.4 slice_bitcast_fusion
  241.1 1.5 slice_reduce_fusion
  242.5 1.9 convert_element_type.236
  244.5 0.0 copy-start.5
  244.5 0.0 copy-start.1
  244.5 2.0 convert_element_type.237
  246.5 1.9 bitcast_convert_fusion
  248.5 0.0 copy-done.2
  248.5 0.0 copy-done.3
  248.5 0.0 copy-start.4
  248.5 1.4 bitcast_convert_fusion.1
  249.9 0.0 copy-done.5
  249.9 0.7 copy.41
  250.6 0.0 copy-done.1
  250.6 0.9 copy.42
  251.5 0.0 copy-done.4
  251.5 0.7 copy.43
  (1 shorter events, 0.0 us)
Async XLA Ops:
  0.7 3.4 %copy-start = (bf16[32,12]{0,1:T(8,128)(2,1)S(1)}, bf16[32,12]{0,1:T(8,128)(2,1)}, u32[]{:S(2)}) copy-start(bf16[32,12]{0,1:T(8,128)(2,1)} %param.26) | copy-start | bytes 2308
  239.7 8.8 %copy-start.2 = (bf16[4,96,768]{2,1,0:T(8,128)(2,1)S(1)}, bf16[4,96,768]{2,1,0:T(8,128)(2,1)}, u32[]{:S(2)}) copy-start(bf16[4,96,768]{2,1,0:T(8,128)(2,1)} %get-tuple-element.76) | copy-start | bytes 1769476
  239.7 8.8 %copy-start.3 = (bf16[4,96,768]{2,1,0:T(8,128)(2,1)S(1)}, bf16[4,96,768]{2,1,0:T(8,128)(2,1)}, u32[]{:S(2)}) copy-start(bf16[4,96,768]{2,1,0:T(8,128)(2,1)} %get-tuple-element.75) | copy-start | bytes 1769476
  244.5 5.4 %copy-start.5 = (bf16[256,768]{1,0:T(8,128)(2,1)S(1)}, bf16[256,768]{1,0:T(8,128)(2,1)}, u32[]{:S(2)}) copy-start(bf16[256,768]{1,0:T(8,128)(2,1)} %get-tuple-element.71) | copy-start | bytes 1179652
  244.5 6.1 %copy-start.1 = (f32[256,768]{1,0:T(8,128)S(1)}, f32[256,768]{1,0:T(8,128)}, u32[]{:S(2)}) copy-start(f32[256,768]{1,0:T(8,128)} %get-tuple-element.72) | copy-start | bytes 2359300
  248.5 3.1 %copy-start.4 = (f32[128,768]{1,0:T(8,128)S(1)}, f32[128,768]{1,0:T(8,128)}, u32[]{:S(2)}) copy-start(f32[128,768]{1,0:T(8,128)} %get-tuple-element.73) | copy-start | bytes 1179652

commit v5 on v4

--- a/solution.py
+++ b/solution.py
@@ -1188,9 +1188,9 @@
 
     self_steps = {
         0: [up.first_side, cross_sides],
-        1: [enc_sum.first_side, gate.second_side],
-        2: [down.along_planes, up.second_side],
-        3: [enc_done, load_normed],
+        1: [enc_sum.first_side],
+        2: [gate.second_side],
+        3: [enc_done, load_normed, down.along_planes, up.second_side],
         4: [down.first_side, load_w_one],
         5: [cross.first_side],
     }
@@ -1229,7 +1229,6 @@
     gate.along_planes()
     down.second_side()
     cross.second_side()
-    token_sum.sides()
     r.gy[...] = outer_rows(r.dq[...], r.grad_cross[0])
     up.along_planes()
     tokens_load.wait()
@@ -1270,7 +1269,7 @@
         )
     down.finish()
     self_two.first_side()
-    token_sum.first_side()
+    token_sum.sides()
     cross.along_planes()
     up.spread()
     self_one.second_side()
@@ -1286,6 +1285,7 @@
         )
     gate.finish()
     self_two.second_side()
+    token_sum.first_side()
     cross.spread()
     up.finish()
     self_one.along_planes()

time: 254 us -> 252 us (level)
  no operation moved by 1% of the time
where the time goes in v5:
time: 252 us; the launch traced here: 251 us
  Pallas kernels  232 us (92%)
  other arithmetic  8.73 us (3%)
  local copies, waits for them, and re-layouts  7.94 us (3%)
    pallas_call x1, Pallas kernels, backward_fused(): pl.pallas_call(functools.partial(backward_kernel, kinds, planes, in_layou...  140 us
    pallas_call x1, Pallas kernels, forward_fused(): pl.pallas_call(functools.partial(forward_kernel, kinds, planes, in_layout...  92.2 us
    convert_element_type x4, other arithmetic, backward_fused(): grad.astype(f32)  7.33 us

profile of v5, /device:TPU:0, one launch (start us, length us, event | category | flops | bytes accessed | tf_op | source)
XLA Modules:
  0.0 250.6 jit_solution(6396602625036728660)
XLA Ops:
  0.7 0.0 copy-start
  1.4 0.7 stack.17
  2.0 0.7 stack.18
  2.7 0.7 stack.19
  3.4 0.6 maximum_convert_fusion.refs_2_.refs_4_
  4.0 0.0 copy-done
  4.0 0.2 convolution_bitcast_fusion
  4.2 0.6 reshape.133.refs_1_
  4.9 0.1 fusion
  5.0 0.7 pad_convert_fusion.refs_5_
  5.6 92.2 %forward_fused.1 = (bf16[4,768,768]{2,1,0:T(8,128)(2,1)}, bf16[4,768,768]{2,1,0:T(8,128)(2,1)}, bf16[4,2,96,2048]{3,2,1,0:T(8,128)(2,1)}, bf16[4,2,96,2048]{3,2,...) custom-call(s32[1]{0:T(128)S(6)} %copy.40.refs_0_, ...), custom_call_target="tpu_custom_call" | custom-call | tf_op jit(solution)/shard_map/forward_fused/pallas_call | solution.py:1776
  97.9 140.1 %backward_fused.1 = (bf16[4,64,768]{2,1,0:T(8,128)(2,1)}, bf16[96,2048]{1,0:T(8,128)(2,1)}, bf16[96,2048]{1,0:T(8,128)(2,1)}, bf16[4,96,768]{2,1,0:T(8,128)(2,1)...) custom-call(s32[1]{0:T(128)S(6)} %copy.40.refs_0_, ...), custom_call_target="tpu_custom_call" | custom-call | tf_op jit(solution)/shard_map/backward_fused/pallas_call | solution.py:1394
  238.0 0.0 copy-start.2
  238.0 0.0 copy-start.3
  238.1 1.4 slice_bitcast_fusion
  239.4 1.5 slice_reduce_fusion
  240.9 1.9 convert_element_type.236
  242.9 0.0 copy-start.5
  242.9 0.0 copy-start.1
  242.9 2.0 convert_element_type.237
  244.9 1.9 bitcast_convert_fusion
  246.8 0.0 copy-done.2
  246.8 0.0 copy-done.3
  246.8 0.0 copy-start.4
  246.8 1.4 bitcast_convert_fusion.1
  248.3 0.0 copy-done.5
  248.3 0.7 copy.41
  249.0 0.0 copy-done.1
  249.0 0.9 copy.42
  249.9 0.0 copy-done.4
  249.9 0.7 copy.43
  (1 shorter events, 0.0 us)
Async XLA Ops:
  0.7 3.4 %copy-start = (bf16[32,12]{0,1:T(8,128)(2,1)S(1)}, bf16[32,12]{0,1:T(8,128)(2,1)}, u32[]{:S(2)}) copy-start(bf16[32,12]{0,1:T(8,128)(2,1)} %param.26) | copy-start | bytes 2308
  238.0 8.8 %copy-start.2 = (bf16[4,96,768]{2,1,0:T(8,128)(2,1)S(1)}, bf16[4,96,768]{2,1,0:T(8,128)(2,1)}, u32[]{:S(2)}) copy-start(bf16[4,96,768]{2,1,0:T(8,128)(2,1)} %get-tuple-element.76) | copy-start | bytes 1769476
  238.0 8.8 %copy-start.3 = (bf16[4,96,768]{2,1,0:T(8,128)(2,1)S(1)}, bf16[4,96,768]{2,1,0:T(8,128)(2,1)}, u32[]{:S(2)}) copy-start(bf16[4,96,768]{2,1,0:T(8,128)(2,1)} %get-tuple-element.75) | copy-start | bytes 1769476
  242.9 5.4 %copy-start.5 = (bf16[256,768]{1,0:T(8,128)(2,1)S(1)}, bf16[256,768]{1,0:T(8,128)(2,1)}, u32[]{:S(2)}) copy-start(bf16[256,768]{1,0:T(8,128)(2,1)} %get-tuple-element.71) | copy-start | bytes 1179652
  242.9 6.1 %copy-start.1 = (f32[256,768]{1,0:T(8,128)S(1)}, f32[256,768]{1,0:T(8,128)}, u32[]{:S(2)}) copy-start(f32[256,768]{1,0:T(8,128)} %get-tuple-element.72) | copy-start | bytes 2359300
  246.8 3.1 %copy-start.4 = (f32[128,768]{1,0:T(8,128)S(1)}, f32[128,768]{1,0:T(8,128)}, u32[]{:S(2)}) copy-start(f32[128,768]{1,0:T(8,128)} %get-tuple-element.73) | copy-start | bytes 1179652

commit v6 on v5

--- a/solution.py
+++ b/solution.py
@@ -1080,7 +1080,7 @@
         hidden = r.hidden[part, :]
         slots = place * rows + part.start + iota((64, 1), 0)
         r.dq[part, :] = jnp.where(slots < length, hidden + r.grad_two[part, :], 0.0).astype(bf16)
-        grad, gain = norm_back_rows(hidden, r.gains[2:3, :], r.gy[part, :])
+        grad, gain = norm_back_rows(hidden, r.gains[:, 2 * width : 3 * width], r.gy[part, :])
         total = grad_result(part, 64) + grad
         r.grad_two[part, :] = total
         r.branch[part, :] = total.astype(bf16)
@@ -1149,7 +1149,7 @@
 
     @row_steps(rows, 64)
     def _(part):
-        grad, gain = norm_back_rows(r.hidden[part, :], r.gains[1:2, :], r.gy[part, :])
+        grad, gain = norm_back_rows(r.hidden[part, :], r.gains[:, 1 * width : 2 * width], r.gy[part, :])
         total = r.grad_two[part, :] + grad
         r.grad_two[part, :] = total
         r.branch[part, :] = total.astype(bf16)
@@ -1293,7 +1293,7 @@
 
     def keep_tokens(part, total):
         values = own_rows(keys, rows, part, 64)
-        grad, _ = norm_back_rows(values, r.gains[0:1, :], r.gy[part, :] + total)
+        grad, _ = norm_back_rows(values, r.gains[:, 0 * width : 1 * width], r.gy[part, :] + total)
         r.hidden[part, :] = r.grad_two[part, :] + grad
 
     token_sum.total(keep_tokens)
@@ -1622,7 +1622,7 @@
 
     @row_steps(count, 128)
     def _(part):
-        r.normed[part, :] = norm_rows(r.source_rows[part, :].astype(f32), r.gains[0:1, :])
+        r.normed[part, :] = norm_rows(r.source_rows[part, :].astype(f32), r.gains[:, 0 * width : 1 * width])
 
     store(0, r.source_rows, r.tokens_all)
     store(1, r.normed, r.normed_all)
@@ -1670,7 +1670,7 @@
         start = pl.multiple_of(place * rows + part.start, 64)
         total = r.hidden[part, :] + r.source_rows[pl.ds(start, 64), :].astype(f32)
         r.hidden[part, :] = total
-        r.normed_rows[part, :] = norm_rows(total, r.gains[1:2, :])
+        r.normed_rows[part, :] = norm_rows(total, r.gains[:, 1 * width : 2 * width])
 
     store(8, r.hidden, r.hidden_one)
     store(9, r.normed_rows, r.normed_two)
@@ -1706,7 +1706,7 @@
     def _(part):
         total = r.hidden_last[part, :] + r.hidden[part, :]
         r.hidden_last[part, :] = total
-        r.normed_last[part, :] = norm_rows(total, r.gains[2:3, :])
+        r.normed_last[part, :] = norm_rows(total, r.gains[:, 2 * width : 3 * width])
 
     store(15, r.hidden_last, r.hidden_two)
     store(16, r.normed_last, r.normed_three)
@@ -1811,7 +1811,7 @@
 
     source = tokens[0].astype(f32)
     if kernels_fit(shards):
-        gains = jnp.stack([gain_one, gain_two, gain_three])
+        gains = jnp.concatenate([gain_one, gain_two, gain_three])[None]
         forward = forward_fused(
             shards, lengths, tokens[0], encoded[0],
             dict(

time: 252 us -> 251 us (level)
  no operation moved by 1% of the time
where the time goes in v6:
time: 251 us; the launch traced here: 249 us
  Pallas kernels  232 us (92%)
  other arithmetic  8.83 us (4%)
  local copies, waits for them, and re-layouts  6.49 us (3%)
    pallas_call x1, Pallas kernels, backward_fused(): pl.pallas_call(functools.partial(backward_kernel, kinds, planes, in_layou...  140 us
    pallas_call x1, Pallas kernels, forward_fused(): pl.pallas_call(functools.partial(forward_kernel, kinds, planes, in_layout...  92.2 us
    convert_element_type x4, other arithmetic, backward_fused(): grad.astype(f32)  7.33 us

profile of v6, /device:TPU:0, one launch (start us, length us, event | category | flops | bytes accessed | tf_op | source)
XLA Modules:
  0.0 249.3 jit_solution(10899984484624726839)
XLA Ops:
  0.7 0.0 copy-start
  1.4 0.7 maximum_convert_fusion
  2.1 0.6 reshape.137.refs_2_.refs_4_
  2.7 0.0 copy-done
  2.7 0.2 convolution_bitcast_fusion
  2.9 0.6 reshape.133.refs_1_
  3.5 0.1 fusion
  3.6 0.7 pad_convert_fusion.refs_5_
  4.3 92.2 %forward_fused.1 = (bf16[4,768,768]{2,1,0:T(8,128)(2,1)}, bf16[4,768,768]{2,1,0:T(8,128)(2,1)}, bf16[4,2,96,2048]{3,2,1,0:T(8,128)(2,1)}, bf16[4,2,96,2048]{3,2,...) custom-call(s32[1]{0:T(128)S(6)} %copy.40.refs_0_, ...), custom_call_target="tpu_custom_call" | custom-call | tf_op jit(solution)/shard_map/forward_fused/pallas_call | solution.py:1776
  96.5 140.2 %backward_fused.1 = (bf16[4,64,768]{2,1,0:T(8,128)(2,1)}, bf16[96,2048]{1,0:T(8,128)(2,1)}, bf16[96,2048]{1,0:T(8,128)(2,1)}, bf16[4,96,768]{2,1,0:T(8,128)(2,1)...) custom-call(s32[1]{0:T(128)S(6)} %copy.40.refs_0_, ...), custom_call_target="tpu_custom_call" | custom-call | tf_op jit(solution)/shard_map/backward_fused/pallas_call | solution.py:1394
  236.7 0.0 copy-start.2
  236.7 0.0 copy-start.3
  236.7 1.4 slice_bitcast_fusion
  238.1 1.5 slice_reduce_fusion
  239.6 1.9 convert_element_type.236
  241.5 0.0 copy-start.5
  241.6 0.0 copy-start.1
  241.6 2.0 convert_element_type.237
  243.6 1.9 bitcast_convert_fusion
  245.5 0.0 copy-done.2
  245.5 0.0 copy-done.3
  245.5 0.0 copy-start.4
  245.5 1.4 bitcast_convert_fusion.1
  246.9 0.0 copy-done.5
  246.9 0.7 copy.41
  247.7 0.0 copy-done.1
  247.7 0.9 copy.42
  248.6 0.0 copy-done.4
  248.6 0.7 copy.43
  (1 shorter events, 0.0 us)
Async XLA Ops:
  0.7 2.0 copy-start
  236.7 8.8 %copy-start.2 = (bf16[4,96,768]{2,1,0:T(8,128)(2,1)S(1)}, bf16[4,96,768]{2,1,0:T(8,128)(2,1)}, u32[]{:S(2)}) copy-start(bf16[4,96,768]{2,1,0:T(8,128)(2,1)} %get-tuple-element.76) | copy-start | bytes 1769476
  236.7 8.8 %copy-start.3 = (bf16[4,96,768]{2,1,0:T(8,128)(2,1)S(1)}, bf16[4,96,768]{2,1,0:T(8,128)(2,1)}, u32[]{:S(2)}) copy-start(bf16[4,96,768]{2,1,0:T(8,128)(2,1)} %get-tuple-element.75) | copy-start | bytes 1769476
  241.5 5.4 %copy-start.5 = (bf16[256,768]{1,0:T(8,128)(2,1)S(1)}, bf16[256,768]{1,0:T(8,128)(2,1)}, u32[]{:S(2)}) copy-start(bf16[256,768]{1,0:T(8,128)(2,1)} %get-tuple-element.71) | copy-start | bytes 1179652
  241.6 6.1 %copy-start.1 = (f32[256,768]{1,0:T(8,128)S(1)}, f32[256,768]{1,0:T(8,128)}, u32[]{:S(2)}) copy-start(f32[256,768]{1,0:T(8,128)} %get-tuple-element.72) | copy-start | bytes 2359300
  245.5 3.1 %copy-start.4 = (f32[128,768]{1,0:T(8,128)S(1)}, f32[128,768]{1,0:T(8,128)}, u32[]{:S(2)}) copy-start(f32[128,768]{1,0:T(8,128)} %get-tuple-element.73) | copy-start | bytes 1179652
